TPU v7x, 32 devices: a whole 2x2x4 slice. The times are simulated.
32 devices in a mesh: row: 4 (over y, x), col: 8 (over z, core).
Axes of the slice: x: 2, y: 2, z: 4, core: 2. Of those that a mesh axis runs over, the one named last changes fastest.
Arguments:
- block_tiles: bfloat16 [4, 160, 128, 128], P('row', 'col'), may hold values from -0.31622777 to 0.31622777
- block_rows: int32 [4, 160], P('row', 'col'), may hold values from 0 to 15, as said below
- block_cols: int32 [4, 160], P('row', 'col'), may hold values from 0 to 7, as said below
- counts: int32 [4, 8], P('row', 'col'), may hold values from 1 to 20, as said below
- start_basis: bfloat16 [8192, 256], P('col'), may hold values from -6 to 6
Outputs:
- image_out: bfloat16 [8192, 256], P(('row', 'col'))
- basis_out: bfloat16 [8192, 256], P(('col', 'row'))
Inputs may be any that keep to these rules, and one draw needn't show every extreme that they name: `block_rows`: each entry lies in 0 to 15; within the 20 slots of one slab pair no pair of block row and block column repeats. `block_cols`: each entry lies in 0 to 7; see block_rows. `counts`: some slab pair has all 20 slots live in every draw.
All inputs are finite; a program needn't handle non-finite values.
Results may differ from a plain program's by a relative error of at most 0.025.
Values may be sent and summed in bfloat16 or wider, within the bound.
No kernel may reach another device: no remote copies, remote signals or barrier semaphores. Data moves between devices by JAX's collectives and lax.ppermute only.
A program may use at most 64 MiB of HBM per device.

v0:
```python
import functools
import math

import jax
import jax.numpy as jnp
from jax import lax
from jax.experimental import pallas as pl
from jax.experimental.pallas import tpu as pltpu
from jax.sharding import PartitionSpec as P


BF = jnp.bfloat16
F32 = jnp.float32


def in_vmem(value):
    return pltpu.with_memory_space_constraint(value, pltpu.VMEM)


def first_product(place, found, start, tiles, row_blocks):
    slots, size, _ = tiles.shape
    col_blocks, rank = start.shape[0] // size, start.shape[1]
    width = rank // 8

    def body(place_ref, found_ref, start_ref, tile_ref, keep_ref, send_ref, flipped, acc):
        for c in range(col_blocks):
            flipped[c] = start_ref[c * size:(c + 1) * size, :].T
        acc[...] = jnp.zeros_like(acc)
        for s in range(slots):
            to = found_ref[0, s]
            to = jnp.where(to < 0, row_blocks, to)
            acc[to] += lax.dot_general(
                flipped[found_ref[1, s]], tile_ref[s], (((1,), (1,)), ((), ())), preferred_element_type=F32)
        x, z, core = place_ref[0], place_ref[1], place_ref[2]
        for dx in range(2):
            for dz in range(2):
                at = 4 * jnp.bitwise_xor(x, dx) + 2 * jnp.bitwise_xor(z, dz)
                for ref, mine in ((keep_ref, core), (send_ref, 1 - core)):
                    first = pl.multiple_of((at + mine) * width, width)
                    ref[2 * dx + dz] = acc[0:row_blocks, pl.ds(first, width), :].astype(BF)

    smem = pl.BlockSpec(memory_space=pltpu.SMEM)
    vmem = pl.BlockSpec(memory_space=pltpu.VMEM)
    return pl.pallas_call(
        body,
        out_shape=[pltpu.VMEM((4, row_blocks, width, size), BF)] * 2,
        in_specs=[smem, smem, vmem, vmem],
        out_specs=[vmem, vmem],
        scratch_shapes=[
            pltpu.VMEM((col_blocks, rank, size), BF),
            pltpu.VMEM((row_blocks + 1, rank, size), F32),
        ],
        compiler_params=pltpu.CompilerParams(vmem_limit_bytes=12 * 1024 * 1024),
        name="first",
    )(place, found, in_vmem(start), in_vmem(tiles))


def flip_blocks(tiles):
    count = len(tiles)
    unroll = functools.reduce(math.gcd, [t.shape[0] for t in tiles])

    def body(*refs):
        for ref, out, same in zip(refs[:count], refs[count:2 * count], refs[2 * count:]):
            def some(i, carry, ref=ref, out=out, same=same):
                for s in range(unroll):
                    block = ref[i * unroll + s]
                    out[i * unroll + s] = block.T
                    same[i * unroll + s] = block
                return carry

            lax.fori_loop(0, ref.shape[0] // unroll, some, 0)

    vmem = pl.BlockSpec(memory_space=pltpu.VMEM)
    return pl.pallas_call(
        body,
        out_shape=[pltpu.VMEM(t.shape, t.dtype) for t in (*tiles, *tiles)],
        in_specs=[vmem] * count,
        out_specs=[vmem] * (2 * count),
        compiler_params=pltpu.CompilerParams(vmem_limit_bytes=8 * 1024 * 1024),
        name="flip",
    )(*[in_vmem(t) for t in tiles])


def block_product(ids, which, tiles, parts, out_blocks, scale_parts=(), total=None, want_sum=False, want_value=False):
    size = tiles[0].shape[1]
    in_blocks, width, _ = parts[0].shape
    n_tiles, n_parts, n_scale = len(tiles), len(parts), len(scale_parts)
    contract = (((1,), (0,)), ((), ()))
    runs = [[]]
    for t in range(n_tiles):
        if sum(tiles[u].shape[0] for u in runs[-1]) >= 40:
            runs.append([])
        runs[-1].append(t)

    def body(*refs):
        ids_ref = refs[0]
        tile_refs = refs[1:1 + n_tiles]
        part_refs = refs[1 + n_tiles:1 + n_tiles + n_parts]
        scale_refs = refs[1 + n_tiles + n_parts:1 + n_tiles + n_parts + n_scale]
        rest = list(refs[1 + n_tiles + n_parts + n_scale:])
        out_ref = rest.pop(0)
        sum_ref = rest.pop(0) if want_sum else None
        value_ref = rest.pop(0) if want_value else None
        operand, acc, where, sem = rest
        copy = pltpu.make_async_copy(ids_ref, where, sem)
        copy.start()
        acc[...] = jnp.zeros_like(acc)
        if n_scale:
            squares = scale_refs[0][...]
            for ref in scale_refs[1:]:
                squares = squares + ref[...]
            scale = lax.rsqrt(jnp.sum(squares, axis=1, keepdims=True) / total + 1e-6)

        def gather_operand(i, carry):
            value = part_refs[0][i].astype(F32)
            for ref in part_refs[1:]:
                value = value + ref[i].astype(F32)
            if n_scale:
                value = value * scale
            operand[i] = value.astype(BF)
            if want_value:
                value_ref[i] = value.astype(BF)
            return carry + value * value if want_sum else carry

        squares_out = lax.fori_loop(
            0, in_blocks, gather_operand, jnp.zeros((width, size), F32) if want_sum else 0, unroll=4)
        if want_sum:
            sum_ref[...] = squares_out
        copy.wait()
        slot = 0
        for ref in tile_refs:
            for s in range(ref.shape[0]):
                to = where[which, slot]
                source = where[which + 1, slot]
                acc[to] += lax.dot_general(operand[source], ref[s], contract, preferred_element_type=F32)
                slot += 1
        out_ref[...] = acc[0:out_blocks].astype(BF)

    out_shape = [pltpu.VMEM((out_blocks, width, size), BF)]
    if want_sum:
        out_shape.append(pltpu.VMEM((width, size), F32))
    if want_value:
        out_shape.append(pltpu.VMEM((in_blocks, width, size), BF))
    vmem = pl.BlockSpec(memory_space=pltpu.VMEM)
    return pl.pallas_call(
        body,
        out_shape=out_shape,
        in_specs=[pl.BlockSpec(memory_space=pl.ANY)] + [vmem] * (n_tiles + n_parts + n_scale),
        out_specs=[vmem] * len(out_shape),
        scratch_shapes=[
            pltpu.VMEM((in_blocks, width, size), BF),
            pltpu.VMEM((out_blocks + 1, width, size), F32),
            pltpu.SMEM(ids.shape, jnp.int32),
            pltpu.SemaphoreType.DMA,
        ],
        compiler_params=pltpu.CompilerParams(vmem_limit_bytes=8 * 1024 * 1024),
        name="product",
    )(ids, *[in_vmem(t) for t in (*tiles, *parts, *scale_parts)])


def shards(n_row, n_col, slab_rows, block_tiles, block_rows, block_cols, counts, start_basis):
    tiles = block_tiles[0]
    slots, size, _ = tiles.shape
    slab_cols, rank = start_basis.shape
    row_blocks = slab_rows // size
    col_blocks = slab_cols // size
    width = rank // 8
    out_rows = 2 * row_blocks
    out_cols = 4 * col_blocks
    row = lax.axis_index("row")
    col = lax.axis_index("col")
    x = row % 2
    z = (col // 2) % 2
    core = col % 2
    half_z = col // 4
    half_row = row // 2

    def send(value, dx, dz, dc):
        return lax.ppermute(value, ("row", "col"), [
            (r * n_col + c, (r ^ dx) * n_col + (c ^ (2 * dz + dc)))
            for r in range(n_row) for c in range(n_col)])

    def others_z(value):
        return [
            lax.ppermute(value, "col", [(c, (c + 4 * k) % n_col) for c in range(n_col)])
            for k in range(1, n_col // 4)
        ]

    def others_row(value):
        return [
            lax.ppermute(value, "row", [(r, (r + 2 * k) % n_row) for r in range(n_row)])
            for k in range(1, n_row // 2)
        ]

    tiles_x = send(tiles, 1, 0, 0)
    found = jnp.stack([
        jnp.where(jnp.arange(slots, dtype=jnp.int32) < counts[0, 0], block_rows[0], -1), block_cols[0]])
    keep, other = first_product(jnp.stack([x, z, core]), found, start_basis, tiles, row_blocks)
    image = keep.astype(F32) + send(other, 0, 0, 1).astype(F32)
    image = image.astype(BF).reshape(2, 2, row_blocks, width, size)
    other = image[:, 1]
    image = (image[:, 0].astype(F32) + send(other, 0, 1, 0).astype(F32)).astype(BF)

    tiles_z = send(lax.optimization_barrier((tiles, other))[0], 0, 1, 0)
    image = jnp.concatenate([image[0], send(image[1], 1, 0, 0)])
    image = [image] + others_z(image)
    part = slots // 2
    corner_b = send(tiles_z[part:], 1, 0, 0)
    corner_a = send(lax.optimization_barrier((tiles_x[:part], image[0]))[0], 0, 1, 0)
    all_tiles = []
    for t in (tiles, tiles_x, tiles_z, corner_a, corner_b):
        all_tiles += [t, send(t, 0, 0, 1)]

    found = jnp.stack([found, send(found, 0, 0, 1)])
    found_x = send(found, 1, 0, 0)
    found_z = send(found, 0, 1, 0)
    found_xz = send(found, 1, 1, 0)

    found_x, found_z, found_xz, _ = lax.optimization_barrier((found_x, found_z, found_xz, image[0]))

    def index(at, dx, dz, dc):
        live = at[0] >= 0
        to_row = at[0] + dx * row_blocks
        to_col = at[1] + (2 * dz + dc) * col_blocks
        return jnp.stack([
            jnp.where(live, to_row, out_rows), to_col, jnp.where(live, to_col, out_cols), jnp.where(live, to_row, 0)])

    ids = []
    for at, dx, dz in ((found, 0, 0), (found_x, 1, 0), (found_z, 0, 1), (found_xz[:, :, :part], 1, 1),
                       (found_xz[:, :, part:], 1, 1)):
        ids += [index(at[0], dx, dz, 0), index(at[1], dx, dz, 1)]
    ids = jnp.concatenate(ids, axis=1)

    total = n_col * slab_cols
    (basis,) = block_product(ids, 2, all_tiles, image, out_cols)
    basis = [basis] + others_row(basis)
    flipped = flip_blocks(all_tiles)
    flipped, all_tiles = flipped[:len(all_tiles)], flipped[len(all_tiles):]
    image, squares = block_product(ids, 0, flipped, basis, out_rows, want_sum=True)
    basis, value = block_product(
        ids, 2, all_tiles, [image] + others_z(image), out_cols,
        scale_parts=[squares] + others_z(squares), total=total, want_value=True)
    basis = [basis] + others_row(basis)
    basis = functools.reduce(jnp.add, [b.astype(F32) for b in basis])
    squares = jnp.sum(jnp.sum(basis * basis, axis=0), axis=1, keepdims=True)
    squares = functools.reduce(jnp.add, [squares] + others_z(squares))
    basis = (basis * lax.rsqrt(squares / total + 1e-6)).astype(BF)

    image_rows = slab_rows // n_col
    basis_rows = slab_cols // n_row
    image_span = max(image_rows // size, 1)
    basis_span = max(basis_rows // size, 1)
    value = value.reshape(2, row_blocks, width, size)
    basis = basis.reshape(2, 2, col_blocks, width, size)

    def pieces(dc):
        out = []
        for dx in range(2):
            for dz in range(2):
                first = (4 * half_z + 2 * (z ^ dz) + (core ^ dc)) * image_rows // size
                out.append(lax.dynamic_slice_in_dim(value[dx], first, image_span, 0))
                first = (2 * half_row + (x ^ dx)) * basis_rows // size
                out.append(lax.dynamic_slice_in_dim(basis[dz, dc], first, basis_span, 0))
        return jnp.concatenate(out).reshape(2, 2, image_span + basis_span, width, size)

    keep = pieces(0)
    twin = send(pieces(1), 0, 0, 1)
    got = [[jnp.stack([keep[dx, dz], twin[dx, dz]]) for dz in range(2)] for dx in range(2)]
    got = [[got[0][0], send(got[0][1], 0, 1, 0)], [send(got[1][0], 1, 0, 0), send(got[1][1], 1, 1, 0)]]
    got = [[jnp.where(core == 0, g, g[::-1]) for g in row_of] for row_of in got]
    got = [jnp.where(z == 0, jnp.stack(g), jnp.stack(g[::-1])) for g in got]
    got = jnp.where(x == 0, jnp.stack(got), jnp.stack(got[::-1]))
    got = got.reshape(8, image_span + basis_span, width, size).transpose(1, 3, 0, 2)
    got = got.reshape((image_span + basis_span) * size, rank)
    image_piece = got[:image_span * size]
    basis_piece = got[image_span * size:]
    if image_rows < size:
        image_piece = lax.dynamic_slice_in_dim(image_piece, col * image_rows % size, image_rows, 0)
    if basis_rows < size:
        basis_piece = lax.dynamic_slice_in_dim(basis_piece, row * basis_rows % size, basis_rows, 0)
    return image_piece, basis_piece


def solution(mesh):
    n_row, n_col = mesh.shape["row"], mesh.shape["col"]

    def whole(block_tiles, block_rows, block_cols, counts, start_basis):
        slab_rows = start_basis.shape[0] // n_row
        return jax.shard_map(
            functools.partial(shards, n_row, n_col, slab_rows),
            mesh=mesh,
            in_specs=(
                P("row", "col", None, None),
                P("row", "col"),
                P("row", "col"),
                P("row", "col"),
                P("col", None),
            ),
            out_specs=(P(("row", "col"), None), P(("col", "row"), None)),
            check_vma=False,
        )(block_tiles, block_rows, block_cols, counts, start_basis)

    return whole
```

profile of v0, /device:TPU:0, one launch (start us, length us, event | category | flops | bytes accessed | tf_op | source)
XLA Modules:
  0.0 115.3 jit_solution(3250018287247199170)
XLA Ops:
  1.3 0.6 copy-done.2
  2.0 0.7 copy-done.1
  2.7 1.0 copy-done
  3.8 2.0 %first.1 = (bf16[4,16,32,128]{3,2,1,0:T(8,128)(2,1)S(1)}, bf16[4,16,32,128]{3,2,1,0:T(8,128)(2,1)S(1)}) custom-call(s32[3]{0:T(128)S(1)} %pad_add_fusion.12.place_ref, s32[2,20]{1,0:T(2,128)S(1)} %get-tuple-element.127.found_ref, bf16[1024,256]{1,0:T(8,128)(2,1)S(1)} %copy-done, bf16[20,128,128]{2,1,0:T(8,128)(2,1)} %bitcast.6.tile_ref.refs_0_.refs_1_), custom_call_target="tpu_custom_call" | custom-call | tf_op jit(solution)/shard_map/first/pallas_call | solution.py:44
  5.7 0.6 collective-permute-start.4
  6.4 2.9 %collective-permute-start.8 = (bf16[20,128,128]{2,1,0:T(8,128)(2,1)}, bf16[20,128,128]{2,1,0:T(8,128)(2,1)S(1)}, u32[]{:S(2)}, u32[]{:S(2)}) collective-permute-start(bf16[20,128,128]{2,1,0:T(8,128)(2,1)} %bitcast.6.tile_ref.refs_0_.refs_1_), channel_id=1, source_target_pairs={{0,8},{1,9},{2,10},{3,11},{4,12},{5,13},{6,14},{7,15},{8,0},{9,1},... | collective-permute-start | bytes 1966088 | tf_op jit(solution)/shard_map/ppermute | solution.py:179
  9.5 1.6 %collective-permute-start.5 = (bf16[2,16,32,128]{3,2,1,0:T(8,128)(2,1)S(1)}, bf16[2,16,32,128]{3,2,1,0:T(8,128)(2,1)S(1)}, u32[]{:S(2)}, u32[]{:S(2)}) collective-permute-start(bf16[2,16,32,128]{3,2,1,0:T(8,128)(2,1)S(1)} %slice_bitcast_fusion), channel_id=1, source_target_pairs={{0,2},{1,3},{2,0},{3,1},{4,6},{5,7},{6,4},{7,5},{8,10},{9,11},{10,... | collective-permute-start | bytes 786440 | tf_op jit(solution)/shard_map/ppermute | solution.py:179
  11.1 1.3 %collective-permute-start.3 = (s32[2,2,20]{2,1,0:T(2,128)S(1)}, s32[2,2,20]{2,1,0:T(2,128)S(1)}, u32[]{:S(2)}, u32[]{:S(2)}) collective-permute-start(s32[2,2,20]{2,1,0:T(2,128)S(1)} %pad_add_fusion.2), channel_id=1, source_target_pairs={{0,10},{1,11},{2,8},{3,9},{4,14},{5,15},{6,12},{7,13},{8,2},{9,3},... | collective-permute-start | bytes 968 | tf_op jit(solution)/shard_map/ppermute | solution.py:179
  12.5 1.6 %collective-permute-start.2 = (s32[2,2,20]{2,1,0:T(2,128)S(1)}, s32[2,2,20]{2,1,0:T(2,128)S(1)}, u32[]{:S(2)}, u32[]{:S(2)}) collective-permute-start(s32[2,2,20]{2,1,0:T(2,128)S(1)} %pad_add_fusion.2), channel_id=1, source_target_pairs={{0,2},{1,3},{2,0},{3,1},{4,6},{5,7},{6,4},{7,5},{8,10},{9,11},{10,... | collective-permute-start | bytes 968 | tf_op jit(solution)/shard_map/ppermute | solution.py:179
  14.1 4.2 %collective-permute-done.5 = bf16[2,16,32,128]{3,2,1,0:T(8,128)(2,1)S(1)} collective-permute-done((bf16[2,16,32,128]{3,2,1,0:T(8,128)(2,1)S(1)}, bf16[2,16,32,128]{3,2,1,0:T(8,128)(2,1)S(1)}, u32[]{:S(2)}, u32[]{:S(2)}) %collective-permute-start.5) | collective-permute-done | bytes 262176 | tf_op jit(solution)/shard_map/ppermute | solution.py:179
  18.4 1.1 collective-permute-start.6
  19.5 5.6 %collective-permute-done.8.refs_2_.refs_3_ = bf16[20,128,128]{2,1,0:T(8,128)(2,1)S(1)} collective-permute-done((bf16[20,128,128]{2,1,0:T(8,128)(2,1)}, bf16[20,128,128]{2,1,0:T(8,128)(2,1)S(1)}, u32[]{:S(2)}, u32[]{:S(2)}) %collective-permute-start.8) | collective-permute-done | bytes 655392 | tf_op jit(solution)/shard_map/ppermute | solution.py:179
  25.1 2.0 %collective-permute-start.1 = (s32[2,2,20]{2,1,0:T(2,128)S(1)}, s32[2,2,20]{2,1,0:T(2,128)S(1)}, u32[]{:S(2)}, u32[]{:S(2)}) collective-permute-start(s32[2,2,20]{2,1,0:T(2,128)S(1)} %pad_add_fusion.2), channel_id=1, source_target_pairs={{0,8},{1,9},{2,10},{3,11},{4,12},{5,13},{6,14},{7,15},{8,0},{9,1},... | collective-permute-start | bytes 968 | tf_op jit(solution)/shard_map/ppermute | solution.py:179
  27.3 1.8 %collective-permute-start.10 = (bf16[20,128,128]{2,1,0:T(8,128)(2,1)}, bf16[20,128,128]{2,1,0:T(8,128)(2,1)S(1)}, u32[]{:S(2)}, u32[]{:S(2)}) collective-permute-start(bf16[20,128,128]{2,1,0:T(8,128)(2,1)} %bitcast.6.tile_ref.refs_0_.refs_1_), channel_id=1, source_target_pairs={{0,2},{1,3},{2,0},{3,1},{4,6},{5,7},{6,4},{7,5},{8,10},{9,11},{10,... | collective-permute-start | bytes 1966088 | tf_op jit(solution)/shard_map/ppermute | solution.py:179
  29.3 1.5 %collective-permute-start.12 = (bf16[10,128,128]{2,1,0:T(8,128)(2,1)S(1)}, bf16[10,128,128]{2,1,0:T(8,128)(2,1)}, u32[]{:S(2)}, u32[]{:S(2)}) collective-permute-start(bf16[10,128,128]{2,1,0:T(8,128)(2,1)S(1)} %slice.242), channel_id=1, source_target_pairs={{0,2},{1,3},{2,0},{3,1},{4,6},{5,7},{6,4},{7,5},{8,10},{9,11},{10,... | collective-permute-start | bytes 983048 | tf_op jit(solution)/shard_map/ppermute | solution.py:179
  30.8 0.6 pad_add_fusion.5
  31.5 13.7 %collective-permute-done.10.refs_4_.refs_5_ = bf16[20,128,128]{2,1,0:T(8,128)(2,1)S(1)} collective-permute-done((bf16[20,128,128]{2,1,0:T(8,128)(2,1)}, bf16[20,128,128]{2,1,0:T(8,128)(2,1)S(1)}, u32[]{:S(2)}, u32[]{:S(2)}) %collective-permute-start.10) | collective-permute-done | bytes 655392 | tf_op jit(solution)/shard_map/ppermute | solution.py:179
  45.2 1.8 %collective-permute-start.14 = (bf16[10,128,128]{2,1,0:T(8,128)(2,1)S(1)}, bf16[10,128,128]{2,1,0:T(8,128)(2,1)}, u32[]{:S(2)}, u32[]{:S(2)}) collective-permute-start(bf16[10,128,128]{2,1,0:T(8,128)(2,1)S(1)} %slice.243), channel_id=1, source_target_pairs={{0,8},{1,9},{2,10},{3,11},{4,12},{5,13},{6,14},{7,15},{8,0},{9,1},... | collective-permute-start | bytes 983048 | tf_op jit(solution)/shard_map/ppermute | solution.py:179
  47.0 0.6 pad_add_fusion.3
  47.7 2.6 %collective-permute-start.16 = (bf16[32,32,128]{2,1,0:T(8,128)(2,1)S(1)}, bf16[32,32,128]{2,1,0:T(8,128)(2,1)}, u32[]{:S(2)}, u32[]{:S(2)}) collective-permute-start(bf16[32,32,128]{2,1,0:T(8,128)(2,1)S(1)} %pad_maximum_fusion.refs_11_), channel_id=1, source_target_pairs={{0,4},{1,5},{2,6},{3,7},{4,0},{5,1},{6,2},{7,3},{8,12},{9,13},{10,... | collective-permute-start | bytes 786440 | tf_op jit(solution)/shard_map/ppermute | solution.py:185
  50.3 0.5 collective-permute-done.12.refs_6_.refs_7_
  50.8 1.6 %collective-permute-done.14.refs_8_.refs_9_ = bf16[10,128,128]{2,1,0:T(8,128)(2,1)} collective-permute-done((bf16[10,128,128]{2,1,0:T(8,128)(2,1)S(1)}, bf16[10,128,128]{2,1,0:T(8,128)(2,1)}, u32[]{:S(2)}, u32[]{:S(2)}) %collective-permute-start.14) | collective-permute-done | bytes 327712 | tf_op jit(solution)/shard_map/ppermute | solution.py:179
  52.4 0.6 pad_add_fusion.4
  53.0 0.6 pad_add_fusion.9
  53.6 0.6 pad_add_fusion.7
  54.2 0.8 concatenate.41.refs_0_
  55.0 8.0 %collective-permute-done.16.refs_12_ = bf16[32,32,128]{2,1,0:T(8,128)(2,1)} collective-permute-done((bf16[32,32,128]{2,1,0:T(8,128)(2,1)S(1)}, bf16[32,32,128]{2,1,0:T(8,128)(2,1)}, u32[]{:S(2)}, u32[]{:S(2)}) %collective-permute-start.16) | collective-permute-done | bytes 262176 | tf_op jit(solution)/shard_map/ppermute | solution.py:185
  63.1 3.7 %product.3.refs_11_ = bf16[32,32,128]{2,1,0:T(8,128)(2,1)S(1)} custom-call(s32[4,160]{1,0:T(4,128)S(1)} %concatenate.41.refs_0_, bf16[20,128,128]{2,1,0:T(8,128)(2,1)} %bitcast.6.tile_ref.refs_0_.refs_1_, bf16[20,128,128]{2,1,0:T(8,128)(2,1)S(1)} %collective-permute-done.7.refs_1_.refs_2_, bf16[20,128,128]{2,1,0:T(8,128)(2,1)S(1)} %collective-permute-done.8.refs_2_.refs_3_, ...), custom_call_target="tpu_custom_call" | custom-call | tf_op jit(solution)/shard_map/product/pallas_call | solution.py:145
  66.8 1.6 %collective-permute-start.17 = (bf16[32,32,128]{2,1,0:T(8,128)(2,1)S(1)}, bf16[32,32,128]{2,1,0:T(8,128)(2,1)S(1)}, u32[]{:S(2)}, u32[]{:S(2)}) collective-permute-start(bf16[32,32,128]{2,1,0:T(8,128)(2,1)S(1)} %product.3.refs_11_), channel_id=1, source_target_pairs={{0,16},{8,24},{16,0},{24,8},{1,17},{9,25},{17,1},{25,9},{2,18},{10... | collective-permute-start | bytes 786440 | tf_op jit(solution)/shard_map/ppermute | solution.py:191
  68.4 4.0 %flip.1 = (bf16[20,128,128]{2,1,0:T(8,128)(2,1)S(1)}, bf16[20,128,128]{2,1,0:T(8,128)(2,1)S(1)}, bf16[20,128,128]{2,1,0:T(8,128)(2,1)S(1)}, bf16[20,128,128]{2,1...) custom-call(bf16[20,128,128]{2,1,0:T(8,128)(2,1)} %bitcast.6.tile_re, ...), custom_call_target="tpu_custom_call" | custom-call | tf_op jit(solution)/shard_map/flip/pallas_call | solution.py:74
  72.4 2.3 %collective-permute-done.17.refs_12_ = bf16[32,32,128]{2,1,0:T(8,128)(2,1)S(1)} collective-permute-done((bf16[32,32,128]{2,1,0:T(8,128)(2,1)S(1)}, bf16[32,32,128]{2,1,0:T(8,128)(2,1)S(1)}, u32[]{:S(2)}, u32[]{:S(2)}) %collective-permute-start.17) | collective-permute-done | bytes 262176 | tf_op jit(solution)/shard_map/ppermute | solution.py:191
  74.7 2.2 %product.4 = (bf16[32,32,128]{2,1,0:T(8,128)(2,1)S(1)}, f32[32,128]{1,0:T(8,128)S(1)}) custom-call(s32[4,160]{1,0:T(4,128)S(1)} %concatenate.41.refs_0_, bf16[20,128,128]{2,1,0:T(8,128)(2,1)S(1)} %get-tuple-element.50.refs_1_, bf16[20,128,128]{2,1,0:T(8,128)(2,1)S(1)} %get-tuple-element.51.refs_2_, bf16[20,128,128]{2,1,0:T(8,128)(2,1)S(1)} %get-tuple-element.52.refs_3_, ...), custom_call_target="tpu_custom_call" | custom-call | tf_op jit(solution)/shard_map/product/pallas_call | solution.py:145
  77.0 2.9 %collective-permute-start.19 = (f32[32,128]{1,0:T(8,128)S(1)}, f32[32,128]{1,0:T(8,128)S(1)}, u32[]{:S(2)}, u32[]{:S(2)}) collective-permute-start(f32[32,128]{1,0:T(8,128)S(1)} %get-tuple-element.61.refs_13_), channel_id=1, source_target_pairs={{0,4},{1,5},{2,6},{3,7},{4,0},{5,1},{6,2},{7,3},{8,12},{9,13},{10,... | collective-permute-start | bytes 49160 | tf_op jit(solution)/shard_map/ppermute | solution.py:185
  79.9 11.3 %collective-permute-done.19.refs_14_ = f32[32,128]{1,0:T(8,128)S(1)} collective-permute-done((f32[32,128]{1,0:T(8,128)S(1)}, f32[32,128]{1,0:T(8,128)S(1)}, u32[]{:S(2)}, u32[]{:S(2)}) %collective-permute-start.19) | collective-permute-done | bytes 16416 | tf_op jit(solution)/shard_map/ppermute | solution.py:185
  91.2 2.2 %product.5 = (bf16[32,32,128]{2,1,0:T(8,128)(2,1)S(1)}, bf16[32,32,128]{2,1,0:T(8,128)(2,1)S(1)}) custom-call(s32[4,160]{1,0:T(4,128)S(1)} %concatenate.41.refs_0_, bf16[20,128,128]{2,1,0:T(8,128)(2,1)S(1)} %get-tuple-element.40.refs_1_, bf16[20,128,128]{2,1,0:T(8,128)(2,1)S(1)} %get-tuple-element.41.refs_2_, ...), custom_call_target="tpu_custom_call" | custom-call | tf_op jit(solution)/shard_map/product/pallas_call | solution.py:145
  93.4 1.6 %collective-permute-start.20 = (bf16[32,32,128]{2,1,0:T(8,128)(2,1)S(1)}, bf16[32,32,128]{2,1,0:T(8,128)(2,1)S(1)}, u32[]{:S(2)}, u32[]{:S(2)}) collective-permute-start(bf16[32,32,128]{2,1,0:T(8,128)(2,1)S(1)} %get-tuple-element.63), channel_id=1, source_target_pairs={{0,16},{8,24},{16,0},{24,8},{1,17},{9,25},{17,1},{25,9},{2,18},{10... | collective-permute-start | bytes 786440 | tf_op jit(solution)/shard_map/ppermute | solution.py:191
  95.0 5.0 %collective-permute-done.20 = bf16[32,32,128]{2,1,0:T(8,128)(2,1)S(1)} collective-permute-done((bf16[32,32,128]{2,1,0:T(8,128)(2,1)S(1)}, bf16[32,32,128]{2,1,0:T(8,128)(2,1)S(1)}, u32[]{:S(2)}, u32[]{:S(2)}) %collective-permute-start.20) | collective-permute-done | bytes 262176 | tf_op jit(solution)/shard_map/ppermute | solution.py:191
  99.9 0.2 multiply_reduce_fusion
  100.2 4.4 %collective-permute-done.21 = f32[32,1]{0,1:T(1,128)S(1)} collective-permute-done((f32[32,1]{0,1:T(1,128)S(1)}, f32[32,1]{0,1:T(1,128)S(1)}, u32[]{:S(2)}, u32[]{:S(2)}) %collective-permute-start.21) | collective-permute-done | bytes 160 | tf_op jit(solution)/shard_map/ppermute | solution.py:185
  105.1 1.3 %collective-permute-done.22 = bf16[2,2,4,32,128]{4,3,2,1,0:T(8,128)(2,1)S(1)} collective-permute-done((bf16[2,2,4,32,128]{4,3,2,1,0:T(8,128)(2,1)S(1)}, bf16[2,2,4,32,128]{4,3,2,1,0:T(8,128)(2,1)S(1)}, u32[]{:S(2)}, u32[]{:S(2)}) %collective-permute-start.22) | collective-permute-done | bytes 131104 | tf_op jit(solution)/shard_map/ppermute | solution.py:179
  106.5 0.6 collective-permute-start.23
  107.1 0.9 collective-permute-start.24
  108.1 2.1 %collective-permute-start.25 = (bf16[2,4,32,128]{3,2,1,0:T(8,128)(2,1)S(1)}, bf16[2,4,32,128]{3,2,1,0:T(8,128)(2,1)S(1)}, u32[]{:S(2)}, u32[]{:S(2)}) collective-permute-start(bf16[2,4,32,128]{3,2,1,0:T(8,128)(2,1)S(1)} %pad_maximum_fusion.4), channel_id=1, source_target_pairs={{0,10},{1,11},{2,8},{3,9},{4,14},{5,15},{6,12},{7,13},{8,2},{9,3},... | collective-permute-start | bytes 196616 | tf_op jit(solution)/shard_map/ppermute | solution.py:179
  110.2 0.6 collective-permute-done.23
  110.8 0.7 collective-permute-done.24
  111.6 1.7 %collective-permute-done.25 = bf16[2,4,32,128]{3,2,1,0:T(8,128)(2,1)S(1)} collective-permute-done((bf16[2,4,32,128]{3,2,1,0:T(8,128)(2,1)S(1)}, bf16[2,4,32,128]{3,2,1,0:T(8,128)(2,1)S(1)}, u32[]{:S(2)}, u32[]{:S(2)}) %collective-permute-start.25) | collective-permute-done | bytes 65568 | tf_op jit(solution)/shard_map/ppermute | solution.py:179
  113.7 0.8 copy.12
  114.5 0.8 copy.11
  (77 shorter events, 2.1 us)
Async XLA Ops:
  1.3 0.7 copy-start.2
  2.0 0.7 copy-start.1
  2.7 1.0 copy-start
  5.7 3.6 %collective-permute-start.4 = (bf16[4,16,32,128]{3,2,1,0:T(8,128)(2,1)S(1)}, bf16[4,16,32,128]{3,2,1,0:T(8,128)(2,1)S(1)}, u32[]{:S(2)}, u32[]{:S(2)}) collective-permute-start(bf16[4,16,32,128]{3,2,1,0:T(8,128)(2,1)S(1)} %get-tuple-element.34), channel_id=1, source_target_pairs={{0,1},{1,0},{2,3},{3,2},{4,5},{5,4},{6,7},{7,6},{8,9},{9,8},{10,11... | collective-permute-start | bytes 1572872 | tf_op jit(solution)/shard_map/ppermute | solution.py:179
  6.3 4.8 %collective-permute-start = (s32[2,20]{1,0:T(2,128)S(1)}, s32[2,20]{1,0:T(2,128)S(1)}, u32[]{:S(2)}, u32[]{:S(2)}) collective-permute-start(s32[2,20]{1,0:T(2,128)S(1)} %get-tuple-element.127.found_ref), channel_id=1, source_target_pairs={{0,1},{1,0},{2,3},{3,2},{4,5},{5,4},{6,7},{7,6},{8,9},{9,8},{10,11... | collective-permute-start | bytes 488 | tf_op jit(solution)/shard_map/ppermute | solution.py:179
  6.4 18.7 %collective-permute-start.8 = (bf16[20,128,128]{2,1,0:T(8,128)(2,1)}, bf16[20,128,128]{2,1,0:T(8,128)(2,1)S(1)}, u32[]{:S(2)}, u32[]{:S(2)}) collective-permute-start(bf16[20,128,128]{2,1,0:T(8,128)(2,1)} %bitcast.6.tile_ref.refs_0_.refs_1_), channel_id=1, source_target_pairs={{0,8},{1,9},{2,10},{3,11},{4,12},{5,13},{6,14},{7,15},{8,0},{9,1},... | collective-permute-start | bytes 1966088 | tf_op jit(solution)/shard_map/ppermute | solution.py:179
  9.3 38.4 %collective-permute-start.7 = (bf16[20,128,128]{2,1,0:T(8,128)(2,1)}, bf16[20,128,128]{2,1,0:T(8,128)(2,1)S(1)}, u32[]{:S(2)}, u32[]{:S(2)}) collective-permute-start(bf16[20,128,128]{2,1,0:T(8,128)(2,1)} %bitcast.6.tile_ref.refs_0_.refs_1_), channel_id=1, source_target_pairs={{0,1},{1,0},{2,3},{3,2},{4,5},{5,4},{6,7},{7,6},{8,9},{9,8},{10,11... | collective-permute-start | bytes 1966088 | tf_op jit(solution)/shard_map/ppermute | solution.py:179
  9.5 8.8 %collective-permute-start.5 = (bf16[2,16,32,128]{3,2,1,0:T(8,128)(2,1)S(1)}, bf16[2,16,32,128]{3,2,1,0:T(8,128)(2,1)S(1)}, u32[]{:S(2)}, u32[]{:S(2)}) collective-permute-start(bf16[2,16,32,128]{3,2,1,0:T(8,128)(2,1)S(1)} %slice_bitcast_fusion), channel_id=1, source_target_pairs={{0,2},{1,3},{2,0},{3,1},{4,6},{5,7},{6,4},{7,5},{8,10},{9,11},{10,... | collective-permute-start | bytes 786440 | tf_op jit(solution)/shard_map/ppermute | solution.py:179
  11.1 18.1 %collective-permute-start.3 = (s32[2,2,20]{2,1,0:T(2,128)S(1)}, s32[2,2,20]{2,1,0:T(2,128)S(1)}, u32[]{:S(2)}, u32[]{:S(2)}) collective-permute-start(s32[2,2,20]{2,1,0:T(2,128)S(1)} %pad_add_fusion.2), channel_id=1, source_target_pairs={{0,10},{1,11},{2,8},{3,9},{4,14},{5,15},{6,12},{7,13},{8,2},{9,3},... | collective-permute-start | bytes 968 | tf_op jit(solution)/shard_map/ppermute | solution.py:179
  12.5 16.8 %collective-permute-start.2 = (s32[2,2,20]{2,1,0:T(2,128)S(1)}, s32[2,2,20]{2,1,0:T(2,128)S(1)}, u32[]{:S(2)}, u32[]{:S(2)}) collective-permute-start(s32[2,2,20]{2,1,0:T(2,128)S(1)} %pad_add_fusion.2), channel_id=1, source_target_pairs={{0,2},{1,3},{2,0},{3,1},{4,6},{5,7},{6,4},{7,5},{8,10},{9,11},{10,... | collective-permute-start | bytes 968 | tf_op jit(solution)/shard_map/ppermute | solution.py:179
  18.4 8.9 %collective-permute-start.6 = (bf16[16,32,128]{2,1,0:T(8,128)(2,1)S(1)}, bf16[16,32,128]{2,1,0:T(8,128)(2,1)S(1)}, u32[]{:S(2)}, u32[]{:S(2)}) collective-permute-start(bf16[16,32,128]{2,1,0:T(8,128)(2,1)S(1)} %get-tuple-element.77), channel_id=1, source_target_pairs={{0,8},{1,9},{2,10},{3,11},{4,12},{5,13},{6,14},{7,15},{8,0},{9,1},... | collective-permute-start | bytes 393224 | tf_op jit(solution)/shard_map/ppermute | solution.py:179
  25.1 4.2 %collective-permute-start.1 = (s32[2,2,20]{2,1,0:T(2,128)S(1)}, s32[2,2,20]{2,1,0:T(2,128)S(1)}, u32[]{:S(2)}, u32[]{:S(2)}) collective-permute-start(s32[2,2,20]{2,1,0:T(2,128)S(1)} %pad_add_fusion.2), channel_id=1, source_target_pairs={{0,8},{1,9},{2,10},{3,11},{4,12},{5,13},{6,14},{7,15},{8,0},{9,1},... | collective-permute-start | bytes 968 | tf_op jit(solution)/shard_map/ppermute | solution.py:179
  27.3 17.8 %collective-permute-start.10 = (bf16[20,128,128]{2,1,0:T(8,128)(2,1)}, bf16[20,128,128]{2,1,0:T(8,128)(2,1)S(1)}, u32[]{:S(2)}, u32[]{:S(2)}) collective-permute-start(bf16[20,128,128]{2,1,0:T(8,128)(2,1)} %bitcast.6.tile_ref.refs_0_.refs_1_), channel_id=1, source_target_pairs={{0,2},{1,3},{2,0},{3,1},{4,6},{5,7},{6,4},{7,5},{8,10},{9,11},{10,... | collective-permute-start | bytes 1966088 | tf_op jit(solution)/shard_map/ppermute | solution.py:179
  29.2 33.8 %collective-permute-start.9 = (bf16[20,128,128]{2,1,0:T(8,128)(2,1)S(1)}, bf16[20,128,128]{2,1,0:T(8,128)(2,1)S(1)}, u32[]{:S(2)}, u32[]{:S(2)}) collective-permute-start(bf16[20,128,128]{2,1,0:T(8,128)(2,1)S(1)} %collective-permute-done.8.refs_2_.refs_3_), channel_id=1, source_target_pairs={{0,1},{1,0},{2,3},{3,2},{4,5},{5,4},{6,7},{7,6},{8,9},{9,8},{10,11... | collective-permute-start | bytes 1966088 | tf_op jit(solution)/shard_map/ppermute | solution.py:179
  29.3 21.5 %collective-permute-start.12 = (bf16[10,128,128]{2,1,0:T(8,128)(2,1)S(1)}, bf16[10,128,128]{2,1,0:T(8,128)(2,1)}, u32[]{:S(2)}, u32[]{:S(2)}) collective-permute-start(bf16[10,128,128]{2,1,0:T(8,128)(2,1)S(1)} %slice.242), channel_id=1, source_target_pairs={{0,2},{1,3},{2,0},{3,1},{4,6},{5,7},{6,4},{7,5},{8,10},{9,11},{10,... | collective-permute-start | bytes 983048 | tf_op jit(solution)/shard_map/ppermute | solution.py:179
  45.2 7.2 %collective-permute-start.14 = (bf16[10,128,128]{2,1,0:T(8,128)(2,1)S(1)}, bf16[10,128,128]{2,1,0:T(8,128)(2,1)}, u32[]{:S(2)}, u32[]{:S(2)}) collective-permute-start(bf16[10,128,128]{2,1,0:T(8,128)(2,1)S(1)} %slice.243), channel_id=1, source_target_pairs={{0,8},{1,9},{2,10},{3,11},{4,12},{5,13},{6,14},{7,15},{8,0},{9,1},... | collective-permute-start | bytes 983048 | tf_op jit(solution)/shard_map/ppermute | solution.py:179
  47.0 16.1 %collective-permute-start.11 = (bf16[20,128,128]{2,1,0:T(8,128)(2,1)S(1)}, bf16[20,128,128]{2,1,0:T(8,128)(2,1)S(1)}, u32[]{:S(2)}, u32[]{:S(2)}) collective-permute-start(bf16[20,128,128]{2,1,0:T(8,128)(2,1)S(1)} %collective-permute-done.10.refs_4_.refs_5_), channel_id=1, source_target_pairs={{0,1},{1,0},{2,3},{3,2},{4,5},{5,4},{6,7},{7,6},{8,9},{9,8},{10,11... | collective-permute-start | bytes 1966088 | tf_op jit(solution)/shard_map/ppermute | solution.py:179
  47.7 15.4 %collective-permute-start.16 = (bf16[32,32,128]{2,1,0:T(8,128)(2,1)S(1)}, bf16[32,32,128]{2,1,0:T(8,128)(2,1)}, u32[]{:S(2)}, u32[]{:S(2)}) collective-permute-start(bf16[32,32,128]{2,1,0:T(8,128)(2,1)S(1)} %pad_maximum_fusion.refs_11_), channel_id=1, source_target_pairs={{0,4},{1,5},{2,6},{3,7},{4,0},{5,1},{6,2},{7,3},{8,12},{9,13},{10,... | collective-permute-start | bytes 786440 | tf_op jit(solution)/shard_map/ppermute | solution.py:185
  50.8 12.2 %collective-permute-start.13 = (bf16[10,128,128]{2,1,0:T(8,128)(2,1)}, bf16[10,128,128]{2,1,0:T(8,128)(2,1)}, u32[]{:S(2)}, u32[]{:S(2)}) collective-permute-start(bf16[10,128,128]{2,1,0:T(8,128)(2,1)} %collective-permute-done.12.refs_6_.refs_7_), channel_id=1, source_target_pairs={{0,1},{1,0},{2,3},{3,2},{4,5},{5,4},{6,7},{7,6},{8,9},{9,8},{10,11... | collective-permute-start | bytes 983048 | tf_op jit(solution)/shard_map/ppermute | solution.py:179
  52.4 10.6 %collective-permute-start.15 = (bf16[10,128,128]{2,1,0:T(8,128)(2,1)}, bf16[10,128,128]{2,1,0:T(8,128)(2,1)}, u32[]{:S(2)}, u32[]{:S(2)}) collective-permute-start(bf16[10,128,128]{2,1,0:T(8,128)(2,1)} %collective-permute-done.14.refs_8_.refs_9_), channel_id=1, source_target_pairs={{0,1},{1,0},{2,3},{3,2},{4,5},{5,4},{6,7},{7,6},{8,9},{9,8},{10,11... | collective-permute-start | bytes 983048 | tf_op jit(solution)/shard_map/ppermute | solution.py:179
  66.8 7.9 %collective-permute-start.17 = (bf16[32,32,128]{2,1,0:T(8,128)(2,1)S(1)}, bf16[32,32,128]{2,1,0:T(8,128)(2,1)S(1)}, u32[]{:S(2)}, u32[]{:S(2)}) collective-permute-start(bf16[32,32,128]{2,1,0:T(8,128)(2,1)S(1)} %product.3.refs_11_), channel_id=1, source_target_pairs={{0,16},{8,24},{16,0},{24,8},{1,17},{9,25},{17,1},{25,9},{2,18},{10... | collective-permute-start | bytes 786440 | tf_op jit(solution)/shard_map/ppermute | solution.py:191
  76.9 14.3 %collective-permute-start.18 = (bf16[32,32,128]{2,1,0:T(8,128)(2,1)S(1)}, bf16[32,32,128]{2,1,0:T(8,128)(2,1)S(1)}, u32[]{:S(2)}, u32[]{:S(2)}) collective-permute-start(bf16[32,32,128]{2,1,0:T(8,128)(2,1)S(1)} %get-tuple-element.60.refs_11_), channel_id=1, source_target_pairs={{0,4},{1,5},{2,6},{3,7},{4,0},{5,1},{6,2},{7,3},{8,12},{9,13},{10,... | collective-permute-start | bytes 786440 | tf_op jit(solution)/shard_map/ppermute | solution.py:185
  77.0 14.2 %collective-permute-start.19 = (f32[32,128]{1,0:T(8,128)S(1)}, f32[32,128]{1,0:T(8,128)S(1)}, u32[]{:S(2)}, u32[]{:S(2)}) collective-permute-start(f32[32,128]{1,0:T(8,128)S(1)} %get-tuple-element.61.refs_13_), channel_id=1, source_target_pairs={{0,4},{1,5},{2,6},{3,7},{4,0},{5,1},{6,2},{7,3},{8,12},{9,13},{10,... | collective-permute-start | bytes 49160 | tf_op jit(solution)/shard_map/ppermute | solution.py:185
  93.4 6.6 %collective-permute-start.20 = (bf16[32,32,128]{2,1,0:T(8,128)(2,1)S(1)}, bf16[32,32,128]{2,1,0:T(8,128)(2,1)S(1)}, u32[]{:S(2)}, u32[]{:S(2)}) collective-permute-start(bf16[32,32,128]{2,1,0:T(8,128)(2,1)S(1)} %get-tuple-element.63), channel_id=1, source_target_pairs={{0,16},{8,24},{16,0},{24,8},{1,17},{9,25},{17,1},{25,9},{2,18},{10... | collective-permute-start | bytes 786440 | tf_op jit(solution)/shard_map/ppermute | solution.py:191
  100.1 4.5 %collective-permute-start.21 = (f32[32,1]{0,1:T(1,128)S(1)}, f32[32,1]{0,1:T(1,128)S(1)}, u32[]{:S(2)}, u32[]{:S(2)}) collective-permute-start(f32[32,1]{0,1:T(1,128)S(1)} %bitcast.182), channel_id=1, source_target_pairs={{0,4},{1,5},{2,6},{3,7},{4,0},{5,1},{6,2},{7,3},{8,12},{9,13},{10,... | collective-permute-start | bytes 392 | tf_op jit(solution)/shard_map/ppermute | solution.py:185
  105.0 1.4 %collective-permute-start.22 = (bf16[2,2,4,32,128]{4,3,2,1,0:T(8,128)(2,1)S(1)}, bf16[2,2,4,32,128]{4,3,2,1,0:T(8,128)(2,1)S(1)}, u32[]{:S(2)}, u32[]{:S(2)}) collective-permute-start(bf16[2,2,4,32,128]{4,3,2,1,0:T(8,128)(2,1)S(1)} %bitcast.181), channel_id=1, source_target_pairs={{0,1},{1,0},{2,3},{3,2},{4,5},{5,4},{6,7},{7,6},{8,9},{9,8},{10,11... | collective-permute-start | bytes 393224 | tf_op jit(solution)/shard_map/ppermute | solution.py:179
  106.5 4.3 %collective-permute-start.23 = (bf16[2,4,32,128]{3,2,1,0:T(8,128)(2,1)S(1)}, bf16[2,4,32,128]{3,2,1,0:T(8,128)(2,1)S(1)}, u32[]{:S(2)}, u32[]{:S(2)}) collective-permute-start(bf16[2,4,32,128]{3,2,1,0:T(8,128)(2,1)S(1)} %pad_maximum_fusion.2), channel_id=1, source_target_pairs={{0,2},{1,3},{2,0},{3,1},{4,6},{5,7},{6,4},{7,5},{8,10},{9,11},{10,... | collective-permute-start | bytes 196616 | tf_op jit(solution)/shard_map/ppermute | solution.py:179
  107.1 4.4 %collective-permute-start.24 = (bf16[2,4,32,128]{3,2,1,0:T(8,128)(2,1)S(1)}, bf16[2,4,32,128]{3,2,1,0:T(8,128)(2,1)S(1)}, u32[]{:S(2)}, u32[]{:S(2)}) collective-permute-start(bf16[2,4,32,128]{3,2,1,0:T(8,128)(2,1)S(1)} %pad_maximum_fusion.3), channel_id=1, source_target_pairs={{0,8},{1,9},{2,10},{3,11},{4,12},{5,13},{6,14},{7,15},{8,0},{9,1},... | collective-permute-start | bytes 196616 | tf_op jit(solution)/shard_map/ppermute | solution.py:179
  108.1 5.2 %collective-permute-start.25 = (bf16[2,4,32,128]{3,2,1,0:T(8,128)(2,1)S(1)}, bf16[2,4,32,128]{3,2,1,0:T(8,128)(2,1)S(1)}, u32[]{:S(2)}, u32[]{:S(2)}) collective-permute-start(bf16[2,4,32,128]{3,2,1,0:T(8,128)(2,1)S(1)} %pad_maximum_fusion.4), channel_id=1, source_target_pairs={{0,10},{1,11},{2,8},{3,9},{4,14},{5,15},{6,12},{7,13},{8,2},{9,3},... | collective-permute-start | bytes 196616 | tf_op jit(solution)/shard_map/ppermute | solution.py:179
where the time goes:
time: 116 us; the launch traced here: 115 us
  waiting for transfers between devices  61.2 us (53%)
  starting transfers between devices  29 us (25%)
  Pallas kernels  14 us (12%)
  local copies, waits for them, and re-layouts  5.39 us (5%)
  other arithmetic  3.97 us (3%)
  between operations  1.69 us (1%)
    ppermute x20, waiting for transfers between devices, send(): lax.ppermute(value, ('row', 'col'), [(r * n_col + c, (r ^ dx) * n_col + (...  30.2 us
    ppermute x4, waiting for transfers between devices, others_z(): lax.ppermute(value, 'col', [(c, (c + 4 * k) % n_col) for c in range(n_col)])  23.7 us
    ppermute x20, starting transfers between devices, send(): lax.ppermute(value, ('row', 'col'), [(r * n_col + c, (r ^ dx) * n_col + (...  20.2 us
    pallas_call x3, Pallas kernels, block_product(): pl.pallas_call(body, out_shape=out_shape, in_specs=[pl.BlockSpec(memory_s...  8.06 us
    ppermute x2, waiting for transfers between devices, others_row(): lax.ppermute(value, 'row', [(r, (r + 2 * k) % n_row) for r in range(n_row)])  7.3 us
    ppermute x4, starting transfers between devices, others_z(): lax.ppermute(value, 'col', [(c, (c + 4 * k) % n_col) for c in range(n_col)])  5.67 us
    unnamed x20, local copies, waits for them, and re-layouts  4.07 us
    pallas_call x1, Pallas kernels, flip_blocks(): pl.pallas_call(body, out_shape=[pltpu.VMEM(t.shape, t.dtype) for t in (*t...  3.99 us
  transfers between devices with their start and end apart: 26, of which 15 were waited for; matrix products, arithmetic and copies ran while one was open for 4% of the time, Pallas kernels for 3%

commit v1 on v0

v1 whole, which is shorter than its diff:
```python
import functools

import jax
import jax.numpy as jnp
from jax import lax
from jax.experimental import pallas as pl
from jax.experimental.pallas import tpu as pltpu
from jax.sharding import PartitionSpec as P


BF = jnp.bfloat16
F32 = jnp.float32


def in_vmem(value):
    return pltpu.with_memory_space_constraint(value, pltpu.VMEM)


def first_product(block_rows, block_cols, counts, start, tiles, row_blocks, cut):
    slots, size, _ = tiles.shape
    col_blocks, rank = start.shape[0] // size, start.shape[1]
    width = rank // 8

    def body(rows_ref, cols_ref, count_ref, start_hbm, tile_hbm, keep_ref, send_ref, head_ref, tail_ref, start_ref, flipped, acc, sems):
        copies = [
            pltpu.make_async_copy(start_hbm, start_ref, sems.at[0]),
            pltpu.make_async_copy(tile_hbm.at[pl.ds(0, cut)], head_ref, sems.at[1]),
            pltpu.make_async_copy(tile_hbm.at[pl.ds(cut, slots - cut)], tail_ref, sems.at[2]),
        ]
        for copy in copies:
            copy.start()
        acc[...] = jnp.zeros_like(acc)
        copies[0].wait()
        for c in range(col_blocks):
            flipped[c] = start_ref[c * size:(c + 1) * size, :].T
        copies[1].wait()
        copies[2].wait()
        count = count_ref[0, 0]
        for s in range(slots):
            to = jnp.where(s < count, rows_ref[0, s], row_blocks)
            block = head_ref[s] if s < cut else tail_ref[s - cut]
            acc[to] += lax.dot_general(
                flipped[cols_ref[0, s]], block, (((1,), (1,)), ((), ())), preferred_element_type=F32)
        x = lax.axis_index("row") % 2
        z = (lax.axis_index("col") // 2) % 2
        core = lax.axis_index("col") % 2
        for dx in range(2):
            for dz in range(2):
                at = 4 * jnp.bitwise_xor(x, dx) + 2 * jnp.bitwise_xor(z, dz)
                for ref, mine in ((keep_ref, core), (send_ref, 1 - core)):
                    first = pl.multiple_of((at + mine) * width, width)
                    ref[2 * dx + dz] = acc[0:row_blocks, pl.ds(first, width), :].astype(BF)

    smem = pl.BlockSpec(memory_space=pltpu.SMEM)
    hbm = pl.BlockSpec(memory_space=pltpu.HBM)
    vmem = pl.BlockSpec(memory_space=pltpu.VMEM)
    return pl.pallas_call(
        body,
        out_shape=[pltpu.VMEM((4, row_blocks, width, size), BF)] * 2
        + [pltpu.VMEM((n, size, size), BF) for n in (cut, slots - cut)],
        in_specs=[smem, smem, smem, hbm, hbm],
        out_specs=[vmem] * 4,
        scratch_shapes=[
            pltpu.VMEM(start.shape, BF),
            pltpu.VMEM((col_blocks, rank, size), BF),
            pltpu.VMEM((row_blocks + 1, rank, size), F32),
            pltpu.SemaphoreType.DMA((3,)),
        ],
        compiler_params=pltpu.CompilerParams(vmem_limit_bytes=12 * 1024 * 1024),
        name="first",
    )(block_rows, block_cols, counts, *[pltpu.with_memory_space_constraint(v, pltpu.HBM) for v in (start, tiles)])


def flip_blocks(tiles):
    count = len(tiles)

    def body(*refs):
        for ref, out, same in zip(refs[:count], refs[count:2 * count], refs[2 * count:]):
            def some(i, carry, ref=ref, out=out, same=same):
                block = ref[i]
                out[i] = block.T
                same[i] = block
                return carry

            n = ref.shape[0]
            lax.fori_loop(0, n, some, 0, unroll=max(u for u in range(1, 11) if n % u == 0))

    vmem = pl.BlockSpec(memory_space=pltpu.VMEM)
    out = pl.pallas_call(
        body,
        out_shape=[pltpu.VMEM(t.shape, t.dtype) for t in (*tiles, *tiles)],
        in_specs=[vmem] * count,
        out_specs=[vmem] * (2 * count),
        compiler_params=pltpu.CompilerParams(vmem_limit_bytes=8 * 1024 * 1024),
        name="flip",
    )(*[in_vmem(t) for t in tiles])
    return out[:count], out[count:]


def block_product(backward, found, groups, parts, row_blocks, col_blocks, scale_parts=(), total=None, want_sum=False,
                  want_value=False, so_far=None, want_acc=False):
    size = groups[0][0].shape[1]
    in_blocks, width, _ = parts[0].shape
    out_blocks = 4 * col_blocks if backward else 2 * row_blocks
    tiles = [g[0] for g in groups]
    n_found, n_tiles, n_parts, n_scale = len(found), len(tiles), len(parts), len(scale_parts)
    n_so_far = 0 if so_far is None else 1
    contract = (((1,), (0,)), ((), ()))

    def body(*refs):
        rest = list(refs)

        def take(count):
            out = rest[:count]
            del rest[:count]
            return out

        found_refs, tile_refs, part_refs = take(n_found), take(n_tiles), take(n_parts)
        scale_refs, so_far_refs = take(n_scale), take(n_so_far)
        (out_ref,) = take(1)
        sum_refs, value_refs = take(int(want_sum)), take(int(want_value))
        operand, acc = take(2)
        where, (sems,) = take(n_found), take(1)
        if want_acc:
            acc = out_ref
        copies = [
            pltpu.make_async_copy(found_refs[i], where[i], sems.at[i]) for i in range(n_found)]
        for copy in copies:
            copy.start()
        acc[...] = so_far_refs[0][...] if n_so_far else jnp.zeros_like(acc)
        if n_scale:
            squares = scale_refs[0][...]
            for ref in scale_refs[1:]:
                squares = squares + ref[...]
            scale = lax.rsqrt(jnp.sum(squares, axis=1, keepdims=True) / total + 1e-6)

        def gather_operand(i, carry):
            value = part_refs[0][i].astype(F32)
            for ref in part_refs[1:]:
                value = value + ref[i].astype(F32)
            if n_scale:
                value = value * scale
            operand[i] = value.astype(BF)
            if want_value:
                value_refs[0][i] = value.astype(BF)
            return carry + value * value if want_sum else carry

        squares_out = lax.fori_loop(
            0, in_blocks, gather_operand, jnp.zeros((width, size), F32) if want_sum else 0, unroll=4)
        if want_sum:
            sum_refs[0][...] = squares_out
        for copy in copies:
            copy.wait()
        for ref, (_, which, dx, dz, dc, first) in zip(tile_refs, groups):
            for s in range(ref.shape[0]):
                at_row = where[which][dc, 0, first + s]
                at_col = where[which][dc, 1, first + s] + (2 * dz + dc) * col_blocks
                live = at_row >= 0
                if backward:
                    to = jnp.where(live, at_col, out_blocks)
                    source = jnp.maximum(at_row, 0) + dx * row_blocks
                else:
                    to = jnp.where(live, at_row + dx * row_blocks, out_blocks)
                    source = at_col
                acc[to] += lax.dot_general(operand[source], ref[s], contract, preferred_element_type=F32)
        if not want_acc:
            out_ref[...] = acc[0:out_blocks].astype(BF)

    acc_shape = (out_blocks + 1, width, size)
    out_shape = [pltpu.VMEM(acc_shape, F32) if want_acc else pltpu.VMEM((out_blocks, width, size), BF)]
    if want_sum:
        out_shape.append(pltpu.VMEM((width, size), F32))
    if want_value:
        out_shape.append(pltpu.VMEM((in_blocks, width, size), BF))
    vmem = pl.BlockSpec(memory_space=pltpu.VMEM)
    others = [*tiles, *parts, *scale_parts] + ([so_far] if n_so_far else [])
    return pl.pallas_call(
        body,
        out_shape=out_shape,
        in_specs=[pl.BlockSpec(memory_space=pl.ANY)] * n_found + [vmem] * len(others),
        out_specs=[vmem] * len(out_shape),
        scratch_shapes=[
            pltpu.VMEM((in_blocks, width, size), BF),
            pltpu.VMEM((8, 128) if want_acc else acc_shape, F32),
        ]
        + [pltpu.SMEM(f.shape, jnp.int32) for f in found]
        + [pltpu.SemaphoreType.DMA((n_found,))],
        compiler_params=pltpu.CompilerParams(vmem_limit_bytes=8 * 1024 * 1024),
        name="product",
    )(*found, *[in_vmem(t) for t in others])


def assemble(messages, spans):
    _, blocks, width, size = messages[0][0].shape
    flat = [messages[dx][dz] for dx in range(2) for dz in range(2)]

    def body(*refs):
        image_ref, basis_ref, scratch = refs[4:]
        x = lax.axis_index("row") % 2
        z = (lax.axis_index("col") // 2) % 2
        core = lax.axis_index("col") % 2
        for dx in range(2):
            for dz in range(2):
                for dc in range(2):
                    at = 4 * jnp.bitwise_xor(x, dx) + 2 * jnp.bitwise_xor(z, dz) + jnp.bitwise_xor(core, dc)
                    at = pl.multiple_of(at * width, width)
                    for b in range(blocks):
                        scratch[b, pl.ds(at, width), :] = refs[2 * dx + dz][dc, b].astype(F32)
        for b in range(blocks):
            ref, row = (image_ref, b) if b < spans[0] else (basis_ref, b - spans[0])
            ref[row * size:(row + 1) * size, :] = scratch[b].T.astype(BF)

    vmem = pl.BlockSpec(memory_space=pltpu.VMEM)
    return pl.pallas_call(
        body,
        out_shape=[jax.ShapeDtypeStruct((span * size, 8 * width), BF) for span in spans],
        in_specs=[vmem] * 4,
        out_specs=[vmem] * 2,
        scratch_shapes=[pltpu.VMEM((blocks, 8 * width, size), F32)],
        compiler_params=pltpu.CompilerParams(vmem_limit_bytes=8 * 1024 * 1024),
        name="assemble",
    )(*[in_vmem(m) for m in flat])


def shards(n_row, n_col, slab_rows, block_tiles, block_rows, block_cols, counts, start_basis):
    tiles = block_tiles[0]
    slots, size, _ = tiles.shape
    slab_cols, rank = start_basis.shape
    row_blocks = slab_rows // size
    col_blocks = slab_cols // size
    width = rank // 8
    row = lax.axis_index("row")
    col = lax.axis_index("col")
    x = row % 2
    z = (col // 2) % 2
    core = col % 2
    half_z = col // 4
    half_row = row // 2

    def send(value, dx, dz, dc):
        return lax.ppermute(value, ("row", "col"), [
            (r * n_col + c, (r ^ dx) * n_col + (c ^ (2 * dz + dc)))
            for r in range(n_row) for c in range(n_col)])

    def others_z(value):
        return [
            lax.ppermute(value, "col", [(c, (c + 4 * k) % n_col) for c in range(n_col)])
            for k in range(1, n_col // 4)
        ]

    def others_row(value):
        return [
            lax.ppermute(value, "row", [(r, (r + 2 * k) % n_row) for r in range(n_row)])
            for k in range(1, n_row // 2)
        ]

    cut = slots // 2
    late = slots - slots // 5
    keep, other, tiles_0, tiles_1 = first_product(
        block_rows, block_cols, counts, start_basis, tiles, row_blocks, cut)
    image = keep.astype(F32) + send(other, 0, 0, 1).astype(F32)
    image = image.astype(BF).reshape(2, 2, row_blocks, width, size)
    image = (image[:, 0].astype(F32) + send(image[:, 1], 0, 1, 0).astype(F32)).astype(BF)
    image = jnp.concatenate([image[0], send(image[1], 1, 0, 0)])
    image = [image] + others_z(image)

    tiles_x0 = send(tiles_0, 1, 0, 0)
    tiles_x1 = send(tiles_1, 1, 0, 0)
    tiles_z0 = send(tiles_0, 0, 1, 0)
    tiles_z1 = send(tiles_1, 0, 1, 0)
    corner_0 = send(tiles_z0, 1, 0, 0)
    corner_1 = send(tiles_z1[:late - cut], 1, 0, 0)
    corner_2 = send(tiles_x1[late - cut:], 0, 1, 0)

    block_rows, block_cols, counts, _ = lax.optimization_barrier((block_rows, block_cols, counts, other))
    own = jnp.stack([
        jnp.where(jnp.arange(slots, dtype=jnp.int32) < counts[0, 0], block_rows[0], -1), block_cols[0]])
    own = jnp.stack([own, send(own, 0, 0, 1)])
    found = [own, send(own, 1, 0, 0), send(own, 0, 1, 0), send(own, 1, 1, 0)]

    groups = []
    for blocks, which, dx, dz, at in (
        (tiles_0, 0, 0, 0, 0), (tiles_1, 0, 0, 0, cut), (tiles_x0, 1, 1, 0, 0),
        (tiles_x1, 1, 1, 0, cut),
        (tiles_z0, 2, 0, 1, 0), (tiles_z1, 2, 0, 1, cut), (corner_0, 3, 1, 1, 0),
        (corner_1, 3, 1, 1, cut), (corner_2, 3, 1, 1, late)):
        groups += [(blocks, which, dx, dz, 0, at), (send(blocks, 0, 0, 1), which, dx, dz, 1, at)]

    total = n_col * slab_cols
    product = functools.partial(block_product, row_blocks=row_blocks, col_blocks=col_blocks)
    (some,) = product(True, found[:3], groups[:12], image, want_acc=True)
    (basis,) = product(True, found[3:], [(g[0], 0, *g[2:]) for g in groups[12:]], image, so_far=some)
    basis = [basis] + others_row(basis)
    flipped, same = flip_blocks([g[0] for g in groups])
    flipped = [(t, *g[1:]) for t, g in zip(flipped, groups)]
    groups = [(t, *g[1:]) for t, g in zip(same, groups)]
    image, squares = product(False, found, flipped, basis, want_sum=True)
    basis, value = product(
        True, found, groups, [image] + others_z(image),
        scale_parts=[squares] + others_z(squares), total=total, want_value=True)
    basis = [basis] + others_row(basis)
    basis = functools.reduce(jnp.add, [b.astype(F32) for b in basis])
    squares = jnp.sum(jnp.sum(basis * basis, axis=0), axis=1, keepdims=True)
    squares = functools.reduce(jnp.add, [squares] + others_z(squares))
    basis = (basis * lax.rsqrt(squares / total + 1e-6)).astype(BF)

    image_rows = slab_rows // n_col
    basis_rows = slab_cols // n_row
    image_span = max(image_rows // size, 1)
    basis_span = max(basis_rows // size, 1)
    value = value.reshape(2, row_blocks, width, size)
    basis = basis.reshape(2, 2, col_blocks, width, size)

    def pieces(dc):
        out = []
        for dx in range(2):
            for dz in range(2):
                first = (4 * half_z + 2 * (z ^ dz) + (core ^ dc)) * image_rows // size
                out.append(lax.dynamic_slice_in_dim(value[dx], first, image_span, 0))
                first = (2 * half_row + (x ^ dx)) * basis_rows // size
                out.append(lax.dynamic_slice_in_dim(basis[dz, dc], first, basis_span, 0))
        return jnp.concatenate(out).reshape(2, 2, image_span + basis_span, width, size)

    keep = pieces(0)
    twin = send(pieces(1), 0, 0, 1)
    messages = [[jnp.stack([keep[dx, dz], twin[dx, dz]]) for dz in range(2)] for dx in range(2)]
    messages = [
        [messages[0][0], send(messages[0][1], 0, 1, 0)],
        [send(messages[1][0], 1, 0, 0), send(messages[1][1], 1, 1, 0)],
    ]
    image_piece, basis_piece = assemble(messages, (image_span, basis_span))
    if image_rows < size:
        image_piece = lax.dynamic_slice_in_dim(image_piece, col * image_rows % size, image_rows, 0)
    if basis_rows < size:
        basis_piece = lax.dynamic_slice_in_dim(basis_piece, row * basis_rows % size, basis_rows, 0)
    return image_piece, basis_piece


def solution(mesh):
    n_row, n_col = mesh.shape["row"], mesh.shape["col"]

    def whole(block_tiles, block_rows, block_cols, counts, start_basis):
        slab_rows = start_basis.shape[0] // n_row
        return jax.shard_map(
            functools.partial(shards, n_row, n_col, slab_rows),
            mesh=mesh,
            in_specs=(
                P("row", "col", None, None),
                P("row", "col"),
                P("row", "col"),
                P("row", "col"),
                P("col", None),
            ),
            out_specs=(P(("row", "col"), None), P(("col", "row"), None)),
            check_vma=False,
        )(block_tiles, block_rows, block_cols, counts, start_basis)

    return whole
```

time: 116 us -> 113 us (0.974)
  waiting for transfers between devices: 61.2 us -> 68.2 us
  local copies, waits for them, and re-layouts: 5.39 us -> 0.96 us
  other arithmetic: 3.97 us -> 0.62 us
  Pallas kernels: 14 us -> 12.6 us
    ppermute x2, waiting for transfers between devices: 7.3 us -> 11.4 us  [others_row(): lax.ppermute(value, 'row', [(r, (r + 2 * k) % n_row) for r in range(n_row)])]
    unnamed x20 -> x13, local copies, waits for them, and re-layouts: 4.07 us -> 0.81 us
    another operation x15 -> x2, other arithmetic: 3.14 us -> 0.01 us  [shards(): own = jnp.stack([own, send(own, 0, 0, 1)])]
    ppermute x4, waiting for transfers between devices: 23.7 us -> 26.1 us  [others_z(): lax.ppermute(value, 'col', [(c, (c + 4 * k) % n_col) for c in range(n_col)])]
    pallas_call x1, Pallas kernels: 3.99 us -> 1.83 us  [flip_blocks(): pl.pallas_call(body, out_shape=[pltpu.VMEM(t.shape, t.dtype) for t in (*t...]
    ppermute x20 -> x27, starting transfers between devices: 20.2 us -> 20.8 us  [send(): lax.ppermute(value, ('row', 'col'), [(r * n_col + c, (r ^ dx) * n_col + (...]
    ppermute x20 -> x27, waiting for transfers between devices: 30.2 us -> 30.8 us  [send(): lax.ppermute(value, ('row', 'col'), [(r * n_col + c, (r ^ dx) * n_col + (...]
    pallas_call x3 -> x4, Pallas kernels: 8.06 us -> 7.46 us  [block_product(): pl.pallas_call(body, out_shape=out_shape, in_specs=[pl.BlockSpec(memory_s...]
  transfers between devices with their start and end apart: 26 -> 33, of which waited for: 15 -> 16; matrix products, arithmetic and copies ran while one was open for 4% -> 0% of each run, Pallas kernels for 3% -> 3%
where the time goes in v1:
time: 113 us
  waiting for transfers between devices  68.2 us (60%)
  starting transfers between devices  28.9 us (26%)
  Pallas kernels  12.6 us (11%)
  between operations  1.61 us (1%)
    ppermute x27, waiting for transfers between devices, send(): lax.ppermute(value, ('row', 'col'), [(r * n_col + c, (r ^ dx) * n_col + (...  30.8 us
    ppermute x4, waiting for transfers between devices, others_z(): lax.ppermute(value, 'col', [(c, (c + 4 * k) % n_col) for c in range(n_col)])  26.1 us
    ppermute x27, starting transfers between devices, send(): lax.ppermute(value, ('row', 'col'), [(r * n_col + c, (r ^ dx) * n_col + (...  20.8 us
    ppermute x2, waiting for transfers between devices, others_row(): lax.ppermute(value, 'row', [(r, (r + 2 * k) % n_row) for r in range(n_row)])  11.4 us
    pallas_call x4, Pallas kernels, block_product(): pl.pallas_call(body, out_shape=out_shape, in_specs=[pl.BlockSpec(memory_s...  7.46 us
    ppermute x4, starting transfers between devices, others_z(): lax.ppermute(value, 'col', [(c, (c + 4 * k) % n_col) for c in range(n_col)])  5.44 us
    ppermute x2, starting transfers between devices, others_row(): lax.ppermute(value, 'row', [(r, (r + 2 * k) % n_row) for r in range(n_row)])  2.61 us
    pallas_call x1, Pallas kernels, first_product(): pl.pallas_call(body, out_shape=[pltpu.VMEM((4, row_blocks, width, size),...  2.43 us
  transfers between devices with their start and end apart: 33, of which 16 were waited for; matrix products, arithmetic and copies ran while one was open for 0% of the time, Pallas kernels for 3%

profile of v1, /device:TPU:0, one launch (start us, length us, event | category | flops | bytes accessed | tf_op | source)
XLA Modules:
  0.0 112.8 jit_solution(9274643188244805075)
XLA Ops:
  1.3 0.6 copy-done
  1.9 2.4 %first.1 = (bf16[4,16,32,128]{3,2,1,0:T(8,128)(2,1)S(1)}, bf16[4,16,32,128]{3,2,1,0:T(8,128)(2,1)S(1)}, bf16[10,128,128]{2,1,0:T(8,128)(2,1)S(1)}, bf16[10,128,128]{2,1,0:T(8,128)(2,1)S(1)}) custom-call(s32[1,20]{1,0:T(1,128)S(1)} %copy-done.1, s32[1,20]{1,0:T(1,128)S(1)} %copy-done, s32[1,1]{1,0:T(1,128)} %copy.25.count_ref, bf16[1024,256]{1,0:T(8,128)(2,1)} %start_hbm.1, ...), custom_call_target="tpu_custom_call" | custom-call | tf_op jit(solution)/shard_map/first/pallas_call | solution.py:57
  4.4 0.6 collective-permute-start.20
  4.9 2.6 %collective-permute-start.12 = (bf16[10,128,128]{2,1,0:T(8,128)(2,1)S(1)}, bf16[10,128,128]{2,1,0:T(8,128)(2,1)S(1)}, u32[]{:S(2)}, u32[]{:S(2)}) collective-permute-start(bf16[10,128,128]{2,1,0:T(8,128)(2,1)S(1)} %get-tuple-element.54.refs_2_.refs_5_), channel_id=1, source_target_pairs={{0,2},{1,3},{2,0},{3,1},{4,6},{5,7},{6,4},{7,5},{8,10},{9,11},{10,... | collective-permute-start | bytes 983048 | tf_op jit(solution)/shard_map/ppermute | solution.py:241
  7.6 1.5 %collective-permute-start.8 = (bf16[10,128,128]{2,1,0:T(8,128)(2,1)S(1)}, bf16[10,128,128]{2,1,0:T(8,128)(2,1)S(1)}, u32[]{:S(2)}, u32[]{:S(2)}) collective-permute-start(bf16[10,128,128]{2,1,0:T(8,128)(2,1)S(1)} %get-tuple-element.54.refs_2_.refs_5_), channel_id=1, source_target_pairs={{0,8},{1,9},{2,10},{3,11},{4,12},{5,13},{6,14},{7,15},{8,0},{9,1},... | collective-permute-start | bytes 983048 | tf_op jit(solution)/shard_map/ppermute | solution.py:241
  9.1 0.1 add_convert_fusion
  9.3 0.5 collective-permute-start.21
  9.8 1.2 %collective-permute-done = s32[2,20]{1,0:T(2,128)S(1)} collective-permute-done((s32[2,20]{1,0:T(2,128)S(1)}, s32[2,20]{1,0:T(2,128)S(1)}, u32[]{:S(2)}, u32[]{:S(2)}) %collective-permute-start) | collective-permute-done | bytes 192 | tf_op jit(solution)/shard_map/ppermute | solution.py:241
  11.0 1.6 %collective-permute-start.2 = (s32[2,2,20]{2,1,0:T(2,128)S(1)}, s32[2,2,20]{2,1,0:T(2,128)S(1)}, u32[]{:S(2)}, u32[]{:S(2)}) collective-permute-start(s32[2,2,20]{2,1,0:T(2,128)S(1)} %pad_add_fusion.refs_0_), channel_id=1, source_target_pairs={{0,2},{1,3},{2,0},{3,1},{4,6},{5,7},{6,4},{7,5},{8,10},{9,11},{10,... | collective-permute-start | bytes 968 | tf_op jit(solution)/shard_map/ppermute | solution.py:241
  12.5 0.4 collective-permute-start.10
  13.0 8.8 %collective-permute-done.2.refs_2_ = s32[2,2,20]{2,1,0:T(2,128)S(1)} collective-permute-done((s32[2,2,20]{2,1,0:T(2,128)S(1)}, s32[2,2,20]{2,1,0:T(2,128)S(1)}, u32[]{:S(2)}, u32[]{:S(2)}) %collective-permute-start.2) | collective-permute-done | bytes 352 | tf_op jit(solution)/shard_map/ppermute | solution.py:241
  21.8 1.9 %collective-permute-start.6 = (bf16[10,128,128]{2,1,0:T(8,128)(2,1)S(1)}, bf16[10,128,128]{2,1,0:T(8,128)(2,1)S(1)}, u32[]{:S(2)}, u32[]{:S(2)}) collective-permute-start(bf16[10,128,128]{2,1,0:T(8,128)(2,1)S(1)} %get-tuple-element.53.refs_0_.refs_3_), channel_id=1, source_target_pairs={{0,8},{1,9},{2,10},{3,11},{4,12},{5,13},{6,14},{7,15},{8,0},{9,1},... | collective-permute-start | bytes 983048 | tf_op jit(solution)/shard_map/ppermute | solution.py:241
  23.8 0.5 collective-permute-start.5
  24.3 0.2 collective-permute-start.1
  24.5 6.5 %collective-permute-done.1.refs_1_ = s32[2,2,20]{2,1,0:T(2,128)S(1)} collective-permute-done((s32[2,2,20]{2,1,0:T(2,128)S(1)}, s32[2,2,20]{2,1,0:T(2,128)S(1)}, u32[]{:S(2)}, u32[]{:S(2)}) %collective-permute-start.1) | collective-permute-done | bytes 352 | tf_op jit(solution)/shard_map/ppermute | solution.py:241
  31.1 1.4 %collective-permute-start.16 = (bf16[6,128,128]{2,1,0:T(8,128)(2,1)S(1)}, bf16[6,128,128]{2,1,0:T(8,128)(2,1)S(1)}, u32[]{:S(2)}, u32[]{:S(2)}) collective-permute-start(bf16[6,128,128]{2,1,0:T(8,128)(2,1)S(1)} %slice.92), channel_id=1, source_target_pairs={{0,8},{1,9},{2,10},{3,11},{4,12},{5,13},{6,14},{7,15},{8,0},{9,1},... | collective-permute-start | bytes 589832 | tf_op jit(solution)/shard_map/ppermute | solution.py:241
  32.4 1.6 %collective-permute-start.18 = (bf16[4,128,128]{2,1,0:T(8,128)(2,1)S(1)}, bf16[4,128,128]{2,1,0:T(8,128)(2,1)S(1)}, u32[]{:S(2)}, u32[]{:S(2)}) collective-permute-start(bf16[4,128,128]{2,1,0:T(8,128)(2,1)S(1)} %slice.93), channel_id=1, source_target_pairs={{0,2},{1,3},{2,0},{3,1},{4,6},{5,7},{6,4},{7,5},{8,10},{9,11},{10,... | collective-permute-start | bytes 393224 | tf_op jit(solution)/shard_map/ppermute | solution.py:241
  34.0 0.5 collective-permute-start.14
  34.6 0.5 collective-permute-start.7
  35.1 2.3 %collective-permute-done.18.refs_16_.refs_5_ = bf16[4,128,128]{2,1,0:T(8,128)(2,1)S(1)} collective-permute-done((bf16[4,128,128]{2,1,0:T(8,128)(2,1)S(1)}, bf16[4,128,128]{2,1,0:T(8,128)(2,1)S(1)}, u32[]{:S(2)}, u32[]{:S(2)}) %collective-permute-start.18) | collective-permute-done | bytes 131104 | tf_op jit(solution)/shard_map/ppermute | solution.py:241
  37.4 0.6 collective-permute-start.22
  38.1 0.8 collective-permute-done.16.refs_14_.refs_3_
  38.8 6.2 %collective-permute-done.14.refs_12_.refs_1_ = bf16[10,128,128]{2,1,0:T(8,128)(2,1)S(1)} collective-permute-done((bf16[10,128,128]{2,1,0:T(8,128)(2,1)S(1)}, bf16[10,128,128]{2,1,0:T(8,128)(2,1)S(1)}, u32[]{:S(2)}, u32[]{:S(2)}) %collective-permute-start.14) | collective-permute-done | bytes 327712 | tf_op jit(solution)/shard_map/ppermute | solution.py:241
  45.0 1.4 %collective-permute-done.22 = bf16[16,32,128]{2,1,0:T(8,128)(2,1)S(1)} collective-permute-done((bf16[16,32,128]{2,1,0:T(8,128)(2,1)S(1)}, bf16[16,32,128]{2,1,0:T(8,128)(2,1)S(1)}, u32[]{:S(2)}, u32[]{:S(2)}) %collective-permute-start.22) | collective-permute-done | bytes 131104 | tf_op jit(solution)/shard_map/ppermute | solution.py:241
  46.5 2.4 %collective-permute-start.23 = (bf16[32,32,128]{2,1,0:T(8,128)(2,1)S(1)}, bf16[32,32,128]{2,1,0:T(8,128)(2,1)S(1)}, u32[]{:S(2)}, u32[]{:S(2)}) collective-permute-start(bf16[32,32,128]{2,1,0:T(8,128)(2,1)S(1)} %pad_maximum_fusion.refs_15_.refs_7_), channel_id=1, source_target_pairs={{0,4},{1,5},{2,6},{3,7},{4,0},{5,1},{6,2},{7,3},{8,12},{9,13},{10,... | collective-permute-start | bytes 786440 | tf_op jit(solution)/shard_map/ppermute | solution.py:247
  48.9 0.2 collective-permute-start.17
  49.1 0.3 collective-permute-start.19
  49.4 2.1 %collective-permute-start.3 = (s32[2,2,20]{2,1,0:T(2,128)S(1)}, s32[2,2,20]{2,1,0:T(2,128)S(1)}, u32[]{:S(2)}, u32[]{:S(2)}) collective-permute-start(s32[2,2,20]{2,1,0:T(2,128)S(1)} %pad_add_fusion.refs_0_), channel_id=1, source_target_pairs={{0,10},{1,11},{2,8},{3,9},{4,14},{5,15},{6,12},{7,13},{8,2},{9,3},... | collective-permute-start | bytes 968 | tf_op jit(solution)/shard_map/ppermute | solution.py:241
  51.5 10.3 %collective-permute-done.23.refs_16_.refs_8_ = bf16[32,32,128]{2,1,0:T(8,128)(2,1)S(1)} collective-permute-done((bf16[32,32,128]{2,1,0:T(8,128)(2,1)S(1)}, bf16[32,32,128]{2,1,0:T(8,128)(2,1)S(1)}, u32[]{:S(2)}, u32[]{:S(2)}) %collective-permute-start.23) | collective-permute-done | bytes 262176 | tf_op jit(solution)/shard_map/ppermute | solution.py:247
  61.8 1.8 %product.4.refs_9_ = f32[33,32,128]{2,1,0:T(8,128)S(1)} custom-call(s32[2,2,20]{2,1,0:T(2,128)S(1)} %pad_add_fusion.refs_0_, s32[2,2,20]{2,1,0:T(2,128)S(1)} %collective-permute-done.1.refs_1_, s32[2,2,20]{2,1,0:T(2,128)S(1)} %collective-permute-done.2.refs_2_, bf16[10,128,128]{2,1,0:T(8,128)(2,1)S(1)} %get-tuple-element.53.refs_0_.refs_3_, ...), custom_call_target="tpu_custom_call" | custom-call | tf_op jit(solution)/shard_map/product/pallas_call | solution.py:177
  63.7 1.1 product.5.refs_22_
  64.8 1.3 %collective-permute-start.24 = (bf16[32,32,128]{2,1,0:T(8,128)(2,1)S(1)}, bf16[32,32,128]{2,1,0:T(8,128)(2,1)S(1)}, u32[]{:S(2)}, u32[]{:S(2)}) collective-permute-start(bf16[32,32,128]{2,1,0:T(8,128)(2,1)S(1)} %product.5.refs_22_), channel_id=1, source_target_pairs={{0,16},{8,24},{16,0},{24,8},{1,17},{9,25},{17,1},{25,9},{2,18},{10... | collective-permute-start | bytes 786440 | tf_op jit(solution)/shard_map/ppermute | solution.py:253
  66.1 1.8 %flip.1 = (bf16[10,128,128]{2,1,0:T(8,128)(2,1)S(1)}, bf16[10,128,128]{2,1,0:T(8,128)(2,1)S(1)}, bf16[10,128,128]{2,1,0:T(8,128)(2,1)S(1)}, bf16[10,128,128]{2,1...) custom-call(bf16[10,128,128]{2,1,0:T(8,128)(2,1)S(1)} %get-tuple-ele, ...), custom_call_target="tpu_custom_call" | custom-call | tf_op jit(solution)/shard_map/flip/pallas_call | solution.py:89
  67.9 4.8 %collective-permute-done.24.refs_23_ = bf16[32,32,128]{2,1,0:T(8,128)(2,1)S(1)} collective-permute-done((bf16[32,32,128]{2,1,0:T(8,128)(2,1)S(1)}, bf16[32,32,128]{2,1,0:T(8,128)(2,1)S(1)}, u32[]{:S(2)}, u32[]{:S(2)}) %collective-permute-start.24) | collective-permute-done | bytes 262176 | tf_op jit(solution)/shard_map/ppermute | solution.py:253
  72.7 2.3 %product.6 = (bf16[32,32,128]{2,1,0:T(8,128)(2,1)S(1)}, f32[32,128]{1,0:T(8,128)S(1)}) custom-call(s32[2,2,20]{2,1,0:T(2,128)S(1)} %pad_add_fusion.refs_0_, s32[2,2,20]{2,1,0:T(2,128)S(1)} %collective-permute-done.1.refs_1_, s32[2,2,20]{2,1,0:T(2,128)S(1)} %collective-permute-done.2.refs_2_, s32[2,2,20]{2,1,0:T(2,128)S(1)} %collective-permute-done.3.refs_0_.refs_3_, ...), custom_call_target="tpu_custom_call" | custom-call | tf_op jit(solution)/shard_map/product/pallas_call | solution.py:177
  75.1 2.9 %collective-permute-start.26 = (f32[32,128]{1,0:T(8,128)S(1)}, f32[32,128]{1,0:T(8,128)S(1)}, u32[]{:S(2)}, u32[]{:S(2)}) collective-permute-start(f32[32,128]{1,0:T(8,128)S(1)} %get-tuple-element.93.refs_24_), channel_id=1, source_target_pairs={{0,4},{1,5},{2,6},{3,7},{4,0},{5,1},{6,2},{7,3},{8,12},{9,13},{10,... | collective-permute-start | bytes 49160 | tf_op jit(solution)/shard_map/ppermute | solution.py:247
  78.0 11.3 %collective-permute-done.26.refs_25_ = f32[32,128]{1,0:T(8,128)S(1)} collective-permute-done((f32[32,128]{1,0:T(8,128)S(1)}, f32[32,128]{1,0:T(8,128)S(1)}, u32[]{:S(2)}, u32[]{:S(2)}) %collective-permute-start.26) | collective-permute-done | bytes 16416 | tf_op jit(solution)/shard_map/ppermute | solution.py:247
  89.3 2.3 %product.7 = (bf16[32,32,128]{2,1,0:T(8,128)(2,1)S(1)}, bf16[32,32,128]{2,1,0:T(8,128)(2,1)S(1)}) custom-call(s32[2,2,20]{2,1,0:T(2,128)S(1)} %pad_add_fusion.refs_0_, s32[2,2,20]{2,1,0:T(2,128)S(1)} %collective-permute-done.1.refs_1_, s32[2,2,20]{2,1,0:T(2,128)S(1)} %collective-permute-done.2.refs_2_, ...), custom_call_target="tpu_custom_call" | custom-call | tf_op jit(solution)/shard_map/product/pallas_call | solution.py:177
  91.6 1.3 %collective-permute-start.27 = (bf16[32,32,128]{2,1,0:T(8,128)(2,1)S(1)}, bf16[32,32,128]{2,1,0:T(8,128)(2,1)S(1)}, u32[]{:S(2)}, u32[]{:S(2)}) collective-permute-start(bf16[32,32,128]{2,1,0:T(8,128)(2,1)S(1)} %get-tuple-element.95), channel_id=1, source_target_pairs={{0,16},{8,24},{16,0},{24,8},{1,17},{9,25},{17,1},{25,9},{2,18},{10... | collective-permute-start | bytes 786440 | tf_op jit(solution)/shard_map/ppermute | solution.py:253
  92.9 6.6 %collective-permute-done.27 = bf16[32,32,128]{2,1,0:T(8,128)(2,1)S(1)} collective-permute-done((bf16[32,32,128]{2,1,0:T(8,128)(2,1)S(1)}, bf16[32,32,128]{2,1,0:T(8,128)(2,1)S(1)}, u32[]{:S(2)}, u32[]{:S(2)}) %collective-permute-start.27) | collective-permute-done | bytes 262176 | tf_op jit(solution)/shard_map/ppermute | solution.py:253
  99.5 0.2 multiply_reduce_fusion
  99.8 4.4 %collective-permute-done.28 = f32[32,1]{0,1:T(1,128)S(1)} collective-permute-done((f32[32,1]{0,1:T(1,128)S(1)}, f32[32,1]{0,1:T(1,128)S(1)}, u32[]{:S(2)}, u32[]{:S(2)}) %collective-permute-start.28) | collective-permute-done | bytes 160 | tf_op jit(solution)/shard_map/ppermute | solution.py:247
  104.7 1.3 %collective-permute-done.29 = bf16[2,2,4,32,128]{4,3,2,1,0:T(8,128)(2,1)S(1)} collective-permute-done((bf16[2,2,4,32,128]{4,3,2,1,0:T(8,128)(2,1)S(1)}, bf16[2,2,4,32,128]{4,3,2,1,0:T(8,128)(2,1)S(1)}, u32[]{:S(2)}, u32[]{:S(2)}) %collective-permute-start.29) | collective-permute-done | bytes 131104 | tf_op jit(solution)/shard_map/ppermute | solution.py:241
  106.2 3.5 %collective-permute-start.32 = (bf16[2,4,32,128]{3,2,1,0:T(8,128)(2,1)S(1)}, bf16[2,4,32,128]{3,2,1,0:T(8,128)(2,1)S(1)}, u32[]{:S(2)}, u32[]{:S(2)}) collective-permute-start(bf16[2,4,32,128]{3,2,1,0:T(8,128)(2,1)S(1)} %pad_maximum_fusion.4), channel_id=1, source_target_pairs={{0,10},{1,11},{2,8},{3,9},{4,14},{5,15},{6,12},{7,13},{8,2},{9,3},... | collective-permute-start | bytes 196616 | tf_op jit(solution)/shard_map/ppermute | solution.py:241
  109.7 0.8 collective-permute-done.30.refs_1_
  110.5 0.6 collective-permute-done.31.refs_2_
  111.2 0.8 collective-permute-done.32.refs_3_
  112.0 0.8 assemble.1
  (61 shorter events, 1.0 us)
Async XLA Ops:
  1.3 0.7 copy-start
  1.3 0.7 copy-start.1
  4.4 4.7 %collective-permute-start.20 = (bf16[4,16,32,128]{3,2,1,0:T(8,128)(2,1)S(1)}, bf16[4,16,32,128]{3,2,1,0:T(8,128)(2,1)S(1)}, u32[]{:S(2)}, u32[]{:S(2)}) collective-permute-start(bf16[4,16,32,128]{3,2,1,0:T(8,128)(2,1)S(1)} %get-tuple-element.49), channel_id=1, source_target_pairs={{0,1},{1,0},{2,3},{3,2},{4,5},{5,4},{6,7},{7,6},{8,9},{9,8},{10,11... | collective-permute-start | bytes 1572872 | tf_op jit(solution)/shard_map/ppermute | solution.py:241
  4.9 18.8 %collective-permute-start.12 = (bf16[10,128,128]{2,1,0:T(8,128)(2,1)S(1)}, bf16[10,128,128]{2,1,0:T(8,128)(2,1)S(1)}, u32[]{:S(2)}, u32[]{:S(2)}) collective-permute-start(bf16[10,128,128]{2,1,0:T(8,128)(2,1)S(1)} %get-tuple-element.54.refs_2_.refs_5_), channel_id=1, source_target_pairs={{0,2},{1,3},{2,0},{3,1},{4,6},{5,7},{6,4},{7,5},{8,10},{9,11},{10,... | collective-permute-start | bytes 983048 | tf_op jit(solution)/shard_map/ppermute | solution.py:241
  7.6 16.2 %collective-permute-start.8 = (bf16[10,128,128]{2,1,0:T(8,128)(2,1)S(1)}, bf16[10,128,128]{2,1,0:T(8,128)(2,1)S(1)}, u32[]{:S(2)}, u32[]{:S(2)}) collective-permute-start(bf16[10,128,128]{2,1,0:T(8,128)(2,1)S(1)} %get-tuple-element.54.refs_2_.refs_5_), channel_id=1, source_target_pairs={{0,8},{1,9},{2,10},{3,11},{4,12},{5,13},{6,14},{7,15},{8,0},{9,1},... | collective-permute-start | bytes 983048 | tf_op jit(solution)/shard_map/ppermute | solution.py:241
  9.3 15.0 %collective-permute-start.21 = (bf16[2,16,32,128]{3,2,1,0:T(8,128)(2,1)S(1)}, bf16[2,16,32,128]{3,2,1,0:T(8,128)(2,1)S(1)}, u32[]{:S(2)}, u32[]{:S(2)}) collective-permute-start(bf16[2,16,32,128]{3,2,1,0:T(8,128)(2,1)S(1)} %slice_bitcast_fusion), channel_id=1, source_target_pairs={{0,2},{1,3},{2,0},{3,1},{4,6},{5,7},{6,4},{7,5},{8,10},{9,11},{10,... | collective-permute-start | bytes 786440 | tf_op jit(solution)/shard_map/ppermute | solution.py:241
  9.8 1.2 %collective-permute-start = (s32[2,20]{1,0:T(2,128)S(1)}, s32[2,20]{1,0:T(2,128)S(1)}, u32[]{:S(2)}, u32[]{:S(2)}) collective-permute-start(s32[2,20]{1,0:T(2,128)S(1)} %get-tuple-element.121), channel_id=1, source_target_pairs={{0,1},{1,0},{2,3},{3,2},{4,5},{5,4},{6,7},{7,6},{8,9},{9,8},{10,11... | collective-permute-start | bytes 488 | tf_op jit(solution)/shard_map/ppermute | solution.py:241
  11.0 10.9 %collective-permute-start.2 = (s32[2,2,20]{2,1,0:T(2,128)S(1)}, s32[2,2,20]{2,1,0:T(2,128)S(1)}, u32[]{:S(2)}, u32[]{:S(2)}) collective-permute-start(s32[2,2,20]{2,1,0:T(2,128)S(1)} %pad_add_fusion.refs_0_), channel_id=1, source_target_pairs={{0,2},{1,3},{2,0},{3,1},{4,6},{5,7},{6,4},{7,5},{8,10},{9,11},{10,... | collective-permute-start | bytes 968 | tf_op jit(solution)/shard_map/ppermute | solution.py:241
  12.5 19.9 %collective-permute-start.10 = (bf16[10,128,128]{2,1,0:T(8,128)(2,1)S(1)}, bf16[10,128,128]{2,1,0:T(8,128)(2,1)S(1)}, u32[]{:S(2)}, u32[]{:S(2)}) collective-permute-start(bf16[10,128,128]{2,1,0:T(8,128)(2,1)S(1)} %get-tuple-element.53.refs_0_.refs_3_), channel_id=1, source_target_pairs={{0,2},{1,3},{2,0},{3,1},{4,6},{5,7},{6,4},{7,5},{8,10},{9,11},{10,... | collective-permute-start | bytes 983048 | tf_op jit(solution)/shard_map/ppermute | solution.py:241
  21.8 12.2 %collective-permute-start.6 = (bf16[10,128,128]{2,1,0:T(8,128)(2,1)S(1)}, bf16[10,128,128]{2,1,0:T(8,128)(2,1)S(1)}, u32[]{:S(2)}, u32[]{:S(2)}) collective-permute-start(bf16[10,128,128]{2,1,0:T(8,128)(2,1)S(1)} %get-tuple-element.53.refs_0_.refs_3_), channel_id=1, source_target_pairs={{0,8},{1,9},{2,10},{3,11},{4,12},{5,13},{6,14},{7,15},{8,0},{9,1},... | collective-permute-start | bytes 983048 | tf_op jit(solution)/shard_map/ppermute | solution.py:241
  23.7 10.8 %collective-permute-start.4 = (bf16[10,128,128]{2,1,0:T(8,128)(2,1)S(1)}, bf16[10,128,128]{2,1,0:T(8,128)(2,1)S(1)}, u32[]{:S(2)}, u32[]{:S(2)}) collective-permute-start(bf16[10,128,128]{2,1,0:T(8,128)(2,1)S(1)} %get-tuple-element.53.refs_0_.refs_3_), channel_id=1, source_target_pairs={{0,1},{1,0},{2,3},{3,2},{4,5},{5,4},{6,7},{7,6},{8,9},{9,8},{10,11... | collective-permute-start | bytes 983048 | tf_op jit(solution)/shard_map/ppermute | solution.py:241
  23.8 10.8 %collective-permute-start.5 = (bf16[10,128,128]{2,1,0:T(8,128)(2,1)S(1)}, bf16[10,128,128]{2,1,0:T(8,128)(2,1)S(1)}, u32[]{:S(2)}, u32[]{:S(2)}) collective-permute-start(bf16[10,128,128]{2,1,0:T(8,128)(2,1)S(1)} %get-tuple-element.54.refs_2_.refs_5_), channel_id=1, source_target_pairs={{0,1},{1,0},{2,3},{3,2},{4,5},{5,4},{6,7},{7,6},{8,9},{9,8},{10,11... | collective-permute-start | bytes 983048 | tf_op jit(solution)/shard_map/ppermute | solution.py:241
  24.3 6.8 %collective-permute-start.1 = (s32[2,2,20]{2,1,0:T(2,128)S(1)}, s32[2,2,20]{2,1,0:T(2,128)S(1)}, u32[]{:S(2)}, u32[]{:S(2)}) collective-permute-start(s32[2,2,20]{2,1,0:T(2,128)S(1)} %pad_add_fusion.refs_0_), channel_id=1, source_target_pairs={{0,8},{1,9},{2,10},{3,11},{4,12},{5,13},{6,14},{7,15},{8,0},{9,1},... | collective-permute-start | bytes 968 | tf_op jit(solution)/shard_map/ppermute | solution.py:241
  31.1 7.8 %collective-permute-start.16 = (bf16[6,128,128]{2,1,0:T(8,128)(2,1)S(1)}, bf16[6,128,128]{2,1,0:T(8,128)(2,1)S(1)}, u32[]{:S(2)}, u32[]{:S(2)}) collective-permute-start(bf16[6,128,128]{2,1,0:T(8,128)(2,1)S(1)} %slice.92), channel_id=1, source_target_pairs={{0,8},{1,9},{2,10},{3,11},{4,12},{5,13},{6,14},{7,15},{8,0},{9,1},... | collective-permute-start | bytes 589832 | tf_op jit(solution)/shard_map/ppermute | solution.py:241
  32.4 5.0 %collective-permute-start.18 = (bf16[4,128,128]{2,1,0:T(8,128)(2,1)S(1)}, bf16[4,128,128]{2,1,0:T(8,128)(2,1)S(1)}, u32[]{:S(2)}, u32[]{:S(2)}) collective-permute-start(bf16[4,128,128]{2,1,0:T(8,128)(2,1)S(1)} %slice.93), channel_id=1, source_target_pairs={{0,2},{1,3},{2,0},{3,1},{4,6},{5,7},{6,4},{7,5},{8,10},{9,11},{10,... | collective-permute-start | bytes 393224 | tf_op jit(solution)/shard_map/ppermute | solution.py:241
  34.0 11.0 %collective-permute-start.14 = (bf16[10,128,128]{2,1,0:T(8,128)(2,1)S(1)}, bf16[10,128,128]{2,1,0:T(8,128)(2,1)S(1)}, u32[]{:S(2)}, u32[]{:S(2)}) collective-permute-start(bf16[10,128,128]{2,1,0:T(8,128)(2,1)S(1)} %collective-permute-done.10.refs_8_.refs_11_), channel_id=1, source_target_pairs={{0,8},{1,9},{2,10},{3,11},{4,12},{5,13},{6,14},{7,15},{8,0},{9,1},... | collective-permute-start | bytes 983048 | tf_op jit(solution)/shard_map/ppermute | solution.py:241
  34.6 11.9 %collective-permute-start.11 = (bf16[10,128,128]{2,1,0:T(8,128)(2,1)S(1)}, bf16[10,128,128]{2,1,0:T(8,128)(2,1)S(1)}, u32[]{:S(2)}, u32[]{:S(2)}) collective-permute-start(bf16[10,128,128]{2,1,0:T(8,128)(2,1)S(1)} %collective-permute-done.10.refs_8_.refs_11_), channel_id=1, source_target_pairs={{0,1},{1,0},{2,3},{3,2},{4,5},{5,4},{6,7},{7,6},{8,9},{9,8},{10,11... | collective-permute-start | bytes 983048 | tf_op jit(solution)/shard_map/ppermute | solution.py:241
  34.6 14.3 %collective-permute-start.7 = (bf16[10,128,128]{2,1,0:T(8,128)(2,1)S(1)}, bf16[10,128,128]{2,1,0:T(8,128)(2,1)S(1)}, u32[]{:S(2)}, u32[]{:S(2)}) collective-permute-start(bf16[10,128,128]{2,1,0:T(8,128)(2,1)S(1)} %collective-permute-done.6.refs_4_.refs_7_), channel_id=1, source_target_pairs={{0,1},{1,0},{2,3},{3,2},{4,5},{5,4},{6,7},{7,6},{8,9},{9,8},{10,11... | collective-permute-start | bytes 983048 | tf_op jit(solution)/shard_map/ppermute | solution.py:241
  37.4 9.0 %collective-permute-start.22 = (bf16[16,32,128]{2,1,0:T(8,128)(2,1)S(1)}, bf16[16,32,128]{2,1,0:T(8,128)(2,1)S(1)}, u32[]{:S(2)}, u32[]{:S(2)}) collective-permute-start(bf16[16,32,128]{2,1,0:T(8,128)(2,1)S(1)} %get-tuple-element.103), channel_id=1, source_target_pairs={{0,8},{1,9},{2,10},{3,11},{4,12},{5,13},{6,14},{7,15},{8,0},{9,1},... | collective-permute-start | bytes 393224 | tf_op jit(solution)/shard_map/ppermute | solution.py:241
  38.8 10.3 %collective-permute-start.13 = (bf16[10,128,128]{2,1,0:T(8,128)(2,1)S(1)}, bf16[10,128,128]{2,1,0:T(8,128)(2,1)S(1)}, u32[]{:S(2)}, u32[]{:S(2)}) collective-permute-start(bf16[10,128,128]{2,1,0:T(8,128)(2,1)S(1)} %collective-permute-done.12.refs_10_.refs_13_), channel_id=1, source_target_pairs={{0,1},{1,0},{2,3},{3,2},{4,5},{5,4},{6,7},{7,6},{8,9},{9,8},{10,11... | collective-permute-start | bytes 983048 | tf_op jit(solution)/shard_map/ppermute | solution.py:241
  45.0 4.4 %collective-permute-start.9 = (bf16[10,128,128]{2,1,0:T(8,128)(2,1)S(1)}, bf16[10,128,128]{2,1,0:T(8,128)(2,1)S(1)}, u32[]{:S(2)}, u32[]{:S(2)}) collective-permute-start(bf16[10,128,128]{2,1,0:T(8,128)(2,1)S(1)} %collective-permute-done.8.refs_6_.refs_9_), channel_id=1, source_target_pairs={{0,1},{1,0},{2,3},{3,2},{4,5},{5,4},{6,7},{7,6},{8,9},{9,8},{10,11... | collective-permute-start | bytes 983048 | tf_op jit(solution)/shard_map/ppermute | solution.py:241
  46.4 17.2 %collective-permute-start.15 = (bf16[10,128,128]{2,1,0:T(8,128)(2,1)S(1)}, bf16[10,128,128]{2,1,0:T(8,128)(2,1)S(1)}, u32[]{:S(2)}, u32[]{:S(2)}) collective-permute-start(bf16[10,128,128]{2,1,0:T(8,128)(2,1)S(1)} %collective-permute-done.14.refs_12_.refs_1_), channel_id=1, source_target_pairs={{0,1},{1,0},{2,3},{3,2},{4,5},{5,4},{6,7},{7,6},{8,9},{9,8},{10,11... | collective-permute-start | bytes 983048 | tf_op jit(solution)/shard_map/ppermute | solution.py:241
  46.5 15.3 %collective-permute-start.23 = (bf16[32,32,128]{2,1,0:T(8,128)(2,1)S(1)}, bf16[32,32,128]{2,1,0:T(8,128)(2,1)S(1)}, u32[]{:S(2)}, u32[]{:S(2)}) collective-permute-start(bf16[32,32,128]{2,1,0:T(8,128)(2,1)S(1)} %pad_maximum_fusion.refs_15_.refs_7_), channel_id=1, source_target_pairs={{0,4},{1,5},{2,6},{3,7},{4,0},{5,1},{6,2},{7,3},{8,12},{9,13},{10,... | collective-permute-start | bytes 786440 | tf_op jit(solution)/shard_map/ppermute | solution.py:247
  48.9 14.8 %collective-permute-start.17 = (bf16[6,128,128]{2,1,0:T(8,128)(2,1)S(1)}, bf16[6,128,128]{2,1,0:T(8,128)(2,1)S(1)}, u32[]{:S(2)}, u32[]{:S(2)}) collective-permute-start(bf16[6,128,128]{2,1,0:T(8,128)(2,1)S(1)} %collective-permute-done.16.refs_14_.refs_3_), channel_id=1, source_target_pairs={{0,1},{1,0},{2,3},{3,2},{4,5},{5,4},{6,7},{7,6},{8,9},{9,8},{10,11... | collective-permute-start | bytes 589832 | tf_op jit(solution)/shard_map/ppermute | solution.py:241
  49.1 14.5 %collective-permute-start.19 = (bf16[4,128,128]{2,1,0:T(8,128)(2,1)S(1)}, bf16[4,128,128]{2,1,0:T(8,128)(2,1)S(1)}, u32[]{:S(2)}, u32[]{:S(2)}) collective-permute-start(bf16[4,128,128]{2,1,0:T(8,128)(2,1)S(1)} %collective-permute-done.18.refs_16_.refs_5_), channel_id=1, source_target_pairs={{0,1},{1,0},{2,3},{3,2},{4,5},{5,4},{6,7},{7,6},{8,9},{9,8},{10,11... | collective-permute-start | bytes 393224 | tf_op jit(solution)/shard_map/ppermute | solution.py:241
  49.4 14.2 %collective-permute-start.3 = (s32[2,2,20]{2,1,0:T(2,128)S(1)}, s32[2,2,20]{2,1,0:T(2,128)S(1)}, u32[]{:S(2)}, u32[]{:S(2)}) collective-permute-start(s32[2,2,20]{2,1,0:T(2,128)S(1)} %pad_add_fusion.refs_0_), channel_id=1, source_target_pairs={{0,10},{1,11},{2,8},{3,9},{4,14},{5,15},{6,12},{7,13},{8,2},{9,3},... | collective-permute-start | bytes 968 | tf_op jit(solution)/shard_map/ppermute | solution.py:241
  64.8 8.0 %collective-permute-start.24 = (bf16[32,32,128]{2,1,0:T(8,128)(2,1)S(1)}, bf16[32,32,128]{2,1,0:T(8,128)(2,1)S(1)}, u32[]{:S(2)}, u32[]{:S(2)}) collective-permute-start(bf16[32,32,128]{2,1,0:T(8,128)(2,1)S(1)} %product.5.refs_22_), channel_id=1, source_target_pairs={{0,16},{8,24},{16,0},{24,8},{1,17},{9,25},{17,1},{25,9},{2,18},{10... | collective-permute-start | bytes 786440 | tf_op jit(solution)/shard_map/ppermute | solution.py:253
  75.0 14.3 %collective-permute-start.25 = (bf16[32,32,128]{2,1,0:T(8,128)(2,1)S(1)}, bf16[32,32,128]{2,1,0:T(8,128)(2,1)S(1)}, u32[]{:S(2)}, u32[]{:S(2)}) collective-permute-start(bf16[32,32,128]{2,1,0:T(8,128)(2,1)S(1)} %get-tuple-element.92.refs_22_), channel_id=1, source_target_pairs={{0,4},{1,5},{2,6},{3,7},{4,0},{5,1},{6,2},{7,3},{8,12},{9,13},{10,... | collective-permute-start | bytes 786440 | tf_op jit(solution)/shard_map/ppermute | solution.py:247
  75.1 14.2 %collective-permute-start.26 = (f32[32,128]{1,0:T(8,128)S(1)}, f32[32,128]{1,0:T(8,128)S(1)}, u32[]{:S(2)}, u32[]{:S(2)}) collective-permute-start(f32[32,128]{1,0:T(8,128)S(1)} %get-tuple-element.93.refs_24_), channel_id=1, source_target_pairs={{0,4},{1,5},{2,6},{3,7},{4,0},{5,1},{6,2},{7,3},{8,12},{9,13},{10,... | collective-permute-start | bytes 49160 | tf_op jit(solution)/shard_map/ppermute | solution.py:247
  91.6 7.9 %collective-permute-start.27 = (bf16[32,32,128]{2,1,0:T(8,128)(2,1)S(1)}, bf16[32,32,128]{2,1,0:T(8,128)(2,1)S(1)}, u32[]{:S(2)}, u32[]{:S(2)}) collective-permute-start(bf16[32,32,128]{2,1,0:T(8,128)(2,1)S(1)} %get-tuple-element.95), channel_id=1, source_target_pairs={{0,16},{8,24},{16,0},{24,8},{1,17},{9,25},{17,1},{25,9},{2,18},{10... | collective-permute-start | bytes 786440 | tf_op jit(solution)/shard_map/ppermute | solution.py:253
  99.7 4.5 %collective-permute-start.28 = (f32[32,1]{0,1:T(1,128)S(1)}, f32[32,1]{0,1:T(1,128)S(1)}, u32[]{:S(2)}, u32[]{:S(2)}) collective-permute-start(f32[32,1]{0,1:T(1,128)S(1)} %bitcast.68), channel_id=1, source_target_pairs={{0,4},{1,5},{2,6},{3,7},{4,0},{5,1},{6,2},{7,3},{8,12},{9,13},{10,... | collective-permute-start | bytes 392 | tf_op jit(solution)/shard_map/ppermute | solution.py:247
  104.6 1.4 %collective-permute-start.29 = (bf16[2,2,4,32,128]{4,3,2,1,0:T(8,128)(2,1)S(1)}, bf16[2,2,4,32,128]{4,3,2,1,0:T(8,128)(2,1)S(1)}, u32[]{:S(2)}, u32[]{:S(2)}) collective-permute-start(bf16[2,2,4,32,128]{4,3,2,1,0:T(8,128)(2,1)S(1)} %bitcast.66), channel_id=1, source_target_pairs={{0,1},{1,0},{2,3},{3,2},{4,5},{5,4},{6,7},{7,6},{8,9},{9,8},{10,11... | collective-permute-start | bytes 393224 | tf_op jit(solution)/shard_map/ppermute | solution.py:241
  106.0 4.5 %collective-permute-start.30 = (bf16[2,4,32,128]{3,2,1,0:T(8,128)(2,1)S(1)}, bf16[2,4,32,128]{3,2,1,0:T(8,128)(2,1)S(1)}, u32[]{:S(2)}, u32[]{:S(2)}) collective-permute-start(bf16[2,4,32,128]{3,2,1,0:T(8,128)(2,1)S(1)} %pad_maximum_fusion.2), channel_id=1, source_target_pairs={{0,2},{1,3},{2,0},{3,1},{4,6},{5,7},{6,4},{7,5},{8,10},{9,11},{10,... | collective-permute-start | bytes 196616 | tf_op jit(solution)/shard_map/ppermute | solution.py:241
  106.1 5.0 %collective-permute-start.31 = (bf16[2,4,32,128]{3,2,1,0:T(8,128)(2,1)S(1)}, bf16[2,4,32,128]{3,2,1,0:T(8,128)(2,1)S(1)}, u32[]{:S(2)}, u32[]{:S(2)}) collective-permute-start(bf16[2,4,32,128]{3,2,1,0:T(8,128)(2,1)S(1)} %pad_maximum_fusion.3), channel_id=1, source_target_pairs={{0,8},{1,9},{2,10},{3,11},{4,12},{5,13},{6,14},{7,15},{8,0},{9,1},... | collective-permute-start | bytes 196616 | tf_op jit(solution)/shard_map/ppermute | solution.py:241
  106.2 5.7 %collective-permute-start.32 = (bf16[2,4,32,128]{3,2,1,0:T(8,128)(2,1)S(1)}, bf16[2,4,32,128]{3,2,1,0:T(8,128)(2,1)S(1)}, u32[]{:S(2)}, u32[]{:S(2)}) collective-permute-start(bf16[2,4,32,128]{3,2,1,0:T(8,128)(2,1)S(1)} %pad_maximum_fusion.4), channel_id=1, source_target_pairs={{0,10},{1,11},{2,8},{3,9},{4,14},{5,15},{6,12},{7,13},{8,2},{9,3},... | collective-permute-start | bytes 196616 | tf_op jit(solution)/shard_map/ppermute | solution.py:241

commit v2 on v1

--- a/solution.py
+++ b/solution.py
@@ -73,37 +73,40 @@
 
 def flip_blocks(tiles):
     count = len(tiles)
+    size = tiles[0].shape[1]
+    slots = sum(t.shape[0] for t in tiles)
 
     def body(*refs):
-        for ref, out, same in zip(refs[:count], refs[count:2 * count], refs[2 * count:]):
-            def some(i, carry, ref=ref, out=out, same=same):
+        out = refs[count]
+        at = 0
+        for ref in refs[:count]:
+            def some(i, carry, ref=ref, at=at):
                 block = ref[i]
-                out[i] = block.T
-                same[i] = block
+                out[at + i] = block.T
+                out[slots + at + i] = block
                 return carry
 
             n = ref.shape[0]
             lax.fori_loop(0, n, some, 0, unroll=max(u for u in range(1, 11) if n % u == 0))
+            at += n
 
     vmem = pl.BlockSpec(memory_space=pltpu.VMEM)
-    out = pl.pallas_call(
+    return pl.pallas_call(
         body,
-        out_shape=[pltpu.VMEM(t.shape, t.dtype) for t in (*tiles, *tiles)],
+        out_shape=pltpu.VMEM((2 * slots, size, size), tiles[0].dtype),
         in_specs=[vmem] * count,
-        out_specs=[vmem] * (2 * count),
+        out_specs=vmem,
         compiler_params=pltpu.CompilerParams(vmem_limit_bytes=8 * 1024 * 1024),
         name="flip",
     )(*[in_vmem(t) for t in tiles])
-    return out[:count], out[count:]
-
-
-def block_product(backward, found, groups, parts, row_blocks, col_blocks, scale_parts=(), total=None, want_sum=False,
-                  want_value=False, so_far=None, want_acc=False):
-    size = groups[0][0].shape[1]
-    in_blocks, width, _ = parts[0].shape
+
+
+def block_product(backward, found, tiles, groups, parts, row_blocks, col_blocks, total=None, want_sum=False,
+                  want_value=False, so_far=None, want_acc=False, split=1, skip=0):
+    _, width, size = parts[0].shape
+    in_blocks = 2 * row_blocks if backward else 4 * col_blocks
     out_blocks = 4 * col_blocks if backward else 2 * row_blocks
-    tiles = [g[0] for g in groups]
-    n_found, n_tiles, n_parts, n_scale = len(found), len(tiles), len(parts), len(scale_parts)
+    n_found, n_tiles, n_parts = len(found), len(tiles), len(parts)
     n_so_far = 0 if so_far is None else 1
     contract = (((1,), (0,)), ((), ()))
 
@@ -115,44 +118,51 @@
             del rest[:count]
             return out
 
-        found_refs, tile_refs, part_refs = take(n_found), take(n_tiles), take(n_parts)
-        scale_refs, so_far_refs = take(n_scale), take(n_so_far)
-        (out_ref,) = take(1)
-        sum_refs, value_refs = take(int(want_sum)), take(int(want_value))
+        found_refs, tile_refs, part_refs, so_far_refs = take(n_found), take(n_tiles), take(n_parts), take(n_so_far)
+        out_refs, value_refs = take(split), take(int(want_value))
         operand, acc = take(2)
         where, (sems,) = take(n_found), take(1)
         if want_acc:
-            acc = out_ref
+            acc = out_refs[0]
         copies = [
             pltpu.make_async_copy(found_refs[i], where[i], sems.at[i]) for i in range(n_found)]
         for copy in copies:
             copy.start()
         acc[...] = so_far_refs[0][...] if n_so_far else jnp.zeros_like(acc)
-        if n_scale:
-            squares = scale_refs[0][...]
-            for ref in scale_refs[1:]:
-                squares = squares + ref[...]
+        if total is not None:
+            squares = part_refs[0][in_blocks].astype(F32)
+            for ref in part_refs[1:]:
+                squares = squares + ref[in_blocks].astype(F32)
             scale = lax.rsqrt(jnp.sum(squares, axis=1, keepdims=True) / total + 1e-6)
 
         def gather_operand(i, carry):
             value = part_refs[0][i].astype(F32)
             for ref in part_refs[1:]:
                 value = value + ref[i].astype(F32)
-            if n_scale:
+            if total is not None:
                 value = value * scale
             operand[i] = value.astype(BF)
             if want_value:
                 value_refs[0][i] = value.astype(BF)
             return carry + value * value if want_sum else carry
 
-        squares_out = lax.fori_loop(
+        squares = lax.fori_loop(
             0, in_blocks, gather_operand, jnp.zeros((width, size), F32) if want_sum else 0, unroll=4)
         if want_sum:
-            sum_refs[0][...] = squares_out
+            left = jnp.broadcast_to(jnp.sum(squares, axis=1, keepdims=True), (width, size))
+            lane = lax.broadcasted_iota(jnp.int32, (width, size), 1)
+            term = jnp.zeros((width, size), F32)
+            for k in range(3):
+                rounded = left.astype(BF).astype(F32)
+                term = jnp.where(lane == k, rounded, term)
+                left = left - rounded
+            out_refs[0][out_blocks] = term.astype(BF)
         for copy in copies:
             copy.wait()
-        for ref, (_, which, dx, dz, dc, first) in zip(tile_refs, groups):
-            for s in range(ref.shape[0]):
+        blocks = [(ref, i) for ref in tile_refs for i in range(ref.shape[0])][skip:]
+        for count, which, dx, dz, dc, first in groups:
+            for s in range(count):
+                ref, i = blocks.pop(0)
                 at_row = where[which][dc, 0, first + s]
                 at_col = where[which][dc, 1, first + s] + (2 * dz + dc) * col_blocks
                 live = at_row >= 0
@@ -162,18 +172,21 @@
                 else:
                     to = jnp.where(live, at_row + dx * row_blocks, out_blocks)
                     source = at_col
-                acc[to] += lax.dot_general(operand[source], ref[s], contract, preferred_element_type=F32)
+                acc[to] += lax.dot_general(operand[source], ref[i], contract, preferred_element_type=F32)
         if not want_acc:
-            out_ref[...] = acc[0:out_blocks].astype(BF)
+            part = width // split
+            for k, ref in enumerate(out_refs):
+                ref[0:out_blocks] = acc[0:out_blocks, k * part:(k + 1) * part, :].astype(BF)
 
     acc_shape = (out_blocks + 1, width, size)
-    out_shape = [pltpu.VMEM(acc_shape, F32) if want_acc else pltpu.VMEM((out_blocks, width, size), BF)]
-    if want_sum:
-        out_shape.append(pltpu.VMEM((width, size), F32))
+    if want_acc:
+        out_shape = [pltpu.VMEM(acc_shape, F32)]
+    else:
+        out_shape = [pltpu.VMEM((out_blocks + int(want_sum), width // split, size), BF)] * split
     if want_value:
         out_shape.append(pltpu.VMEM((in_blocks, width, size), BF))
     vmem = pl.BlockSpec(memory_space=pltpu.VMEM)
-    others = [*tiles, *parts, *scale_parts] + ([so_far] if n_so_far else [])
+    others = [*tiles, *parts] + ([so_far] if n_so_far else [])
     return pl.pallas_call(
         body,
         out_shape=out_shape,
@@ -188,6 +201,54 @@
         compiler_params=pltpu.CompilerParams(vmem_limit_bytes=8 * 1024 * 1024),
         name="product",
     )(*found, *[in_vmem(t) for t in others])
+
+
+def pack(values, basis, spans, rows, row_blocks, col_blocks):
+    count = len(values)
+    terms = len(basis[0])
+    _, part, size = values[0].shape
+    width = part * count
+
+    def body(*refs):
+        value_refs = refs[:count]
+        basis_refs = [refs[count + terms * k:count + terms * (k + 1)] for k in range(count)]
+        keep_ref, other_ref, squares_ref, summed = refs[count * (terms + 1):]
+        row, col = lax.axis_index("row"), lax.axis_index("col")
+        x, z, core = row % 2, (col // 2) % 2, col % 2
+        for k in range(count):
+            def add(i, carry, k=k):
+                value = basis_refs[k][0][i].astype(F32)
+                for ref in basis_refs[k][1:]:
+                    value = value + ref[i].astype(F32)
+                summed[i, k * part:(k + 1) * part, :] = value
+                return carry + value * value
+
+            squares = lax.fori_loop(0, 4 * col_blocks, add, jnp.zeros((part, size), F32), unroll=4)
+            squares_ref[k * part:(k + 1) * part, :] = squares
+        for dx in range(2):
+            for dz in range(2):
+                for dc, ref in ((0, keep_ref), (1, other_ref)):
+                    at = 4 * (col // 4) + 2 * jnp.bitwise_xor(z, dz) + jnp.bitwise_xor(core, dc)
+                    first = dx * row_blocks + at * rows[0] // size
+                    for b in range(spans[0]):
+                        for k in range(count):
+                            ref[dx, dz, b, k * part:(k + 1) * part, :] = value_refs[k][first + b]
+                    at = 2 * (row // 2) + jnp.bitwise_xor(x, dx)
+                    first = (2 * dz + dc) * col_blocks + at * rows[1] // size
+                    for b in range(spans[1]):
+                        ref[dx, dz, spans[0] + b] = summed[first + b].astype(BF)
+
+    vmem = pl.BlockSpec(memory_space=pltpu.VMEM)
+    operands = [*values, *[t for b in basis for t in b]]
+    return pl.pallas_call(
+        body,
+        out_shape=[pltpu.VMEM((2, 2, sum(spans), width, size), BF)] * 2 + [pltpu.VMEM((width, size), F32)],
+        in_specs=[vmem] * len(operands),
+        out_specs=[vmem] * 3,
+        scratch_shapes=[pltpu.VMEM((4 * col_blocks, width, size), F32)],
+        compiler_params=pltpu.CompilerParams(vmem_limit_bytes=8 * 1024 * 1024),
+        name="pack",
+    )(*[in_vmem(t) for t in operands])
 
 
 def assemble(messages, spans):
@@ -229,13 +290,6 @@
     row_blocks = slab_rows // size
     col_blocks = slab_cols // size
     width = rank // 8
-    row = lax.axis_index("row")
-    col = lax.axis_index("col")
-    x = row % 2
-    z = (col // 2) % 2
-    core = col % 2
-    half_z = col // 4
-    half_row = row // 2
 
     def send(value, dx, dz, dc):
         return lax.ppermute(value, ("row", "col"), [
@@ -278,61 +332,64 @@
     own = jnp.stack([own, send(own, 0, 0, 1)])
     found = [own, send(own, 1, 0, 0), send(own, 0, 1, 0), send(own, 1, 1, 0)]
 
-    groups = []
-    for blocks, which, dx, dz, at in (
+    blocks, groups = [], []
+    for some, which, dx, dz, at in (
         (tiles_0, 0, 0, 0, 0), (tiles_1, 0, 0, 0, cut), (tiles_x0, 1, 1, 0, 0),
-        (tiles_x1, 1, 1, 0, cut),
-        (tiles_z0, 2, 0, 1, 0), (tiles_z1, 2, 0, 1, cut), (corner_0, 3, 1, 1, 0),
-        (corner_1, 3, 1, 1, cut), (corner_2, 3, 1, 1, late)):
-        groups += [(blocks, which, dx, dz, 0, at), (send(blocks, 0, 0, 1), which, dx, dz, 1, at)]
+        (tiles_x1, 1, 1, 0, cut), (tiles_z0, 2, 0, 1, 0), (tiles_z1, 2, 0, 1, cut),
+        (corner_0, 3, 1, 1, 0), (corner_1, 3, 1, 1, cut), (corner_2, 3, 1, 1, late)):
+        blocks += [some, send(some, 0, 0, 1)]
+        groups += [(some.shape[0], which, dx, dz, dc, at) for dc in range(2)]
 
     total = n_col * slab_cols
     product = functools.partial(block_product, row_blocks=row_blocks, col_blocks=col_blocks)
-    (some,) = product(True, found[:3], groups[:12], image, want_acc=True)
-    (basis,) = product(True, found[3:], [(g[0], 0, *g[2:]) for g in groups[12:]], image, so_far=some)
-    basis = [basis] + others_row(basis)
-    flipped, same = flip_blocks([g[0] for g in groups])
-    flipped = [(t, *g[1:]) for t, g in zip(flipped, groups)]
-    groups = [(t, *g[1:]) for t, g in zip(same, groups)]
-    image, squares = product(False, found, flipped, basis, want_sum=True)
-    basis, value = product(
-        True, found, groups, [image] + others_z(image),
-        scale_parts=[squares] + others_z(squares), total=total, want_value=True)
-    basis = [basis] + others_row(basis)
-    basis = functools.reduce(jnp.add, [b.astype(F32) for b in basis])
-    squares = jnp.sum(jnp.sum(basis * basis, axis=0), axis=1, keepdims=True)
-    squares = functools.reduce(jnp.add, [squares] + others_z(squares))
-    basis = (basis * lax.rsqrt(squares / total + 1e-6)).astype(BF)
-
+    (near,) = product(True, found[:3], blocks[:12], groups[:12], image, want_acc=True)
+    corner = [(g[0], 0, *g[2:]) for g in groups[12:]]
+    basis = product(True, found[3:], blocks[12:], corner, image, so_far=near, split=2)
+    both = flip_blocks(blocks)
+    as_they_are = both.shape[0] // 2
+
+    basis = [[b] + others_row(b) for b in basis]
+    image = []
+    for b in basis:
+        (out,) = product(False, found, [both], groups, b, want_sum=True)
+        image.append([out] + others_z(out))
+    basis, values = [], []
+    for i in image:
+        out, value = product(True, found, [both], groups, i, total=total, want_value=True, skip=as_they_are)
+        values.append(value)
+        basis.append([out] + others_row(out))
     image_rows = slab_rows // n_col
     basis_rows = slab_cols // n_row
     image_span = max(image_rows // size, 1)
     basis_span = max(basis_rows // size, 1)
-    value = value.reshape(2, row_blocks, width, size)
-    basis = basis.reshape(2, 2, col_blocks, width, size)
-
-    def pieces(dc):
-        out = []
-        for dx in range(2):
-            for dz in range(2):
-                first = (4 * half_z + 2 * (z ^ dz) + (core ^ dc)) * image_rows // size
-                out.append(lax.dynamic_slice_in_dim(value[dx], first, image_span, 0))
-                first = (2 * half_row + (x ^ dx)) * basis_rows // size
-                out.append(lax.dynamic_slice_in_dim(basis[dz, dc], first, basis_span, 0))
-        return jnp.concatenate(out).reshape(2, 2, image_span + basis_span, width, size)
-
-    keep = pieces(0)
-    twin = send(pieces(1), 0, 0, 1)
-    messages = [[jnp.stack([keep[dx, dz], twin[dx, dz]]) for dz in range(2)] for dx in range(2)]
+    keep, other, squares = pack(
+        values, basis, (image_span, basis_span), (image_rows, basis_rows), row_blocks, col_blocks)
+
+    twin_squares = [
+        lax.ppermute(squares, "col", [(c, (c + 4 * k) % n_col ^ 1) for c in range(n_col)])
+        for k in range(1, n_col // 4)
+    ]
+    twin_squares = functools.reduce(jnp.add, twin_squares + [send(squares, 0, 0, 1)])
+    squares = functools.reduce(jnp.add, [squares] + others_z(squares))
+
+    twin = send(other, 0, 0, 1)
+
+    def scaled(piece, sums):
+        factor = lax.rsqrt(jnp.sum(sums, axis=1, keepdims=True) / total + 1e-6)
+        factor = jnp.broadcast_to(factor, (basis_span, width, 1))
+        factor = jnp.concatenate([jnp.ones((image_span, width, 1), F32), factor])
+        return (piece.astype(F32) * factor).astype(BF)
+
+    messages = [[jnp.stack([scaled(keep[dx, dz], squares), scaled(twin[dx, dz], twin_squares)]) for dz in range(2)] for dx in range(2)]
     messages = [
         [messages[0][0], send(messages[0][1], 0, 1, 0)],
         [send(messages[1][0], 1, 0, 0), send(messages[1][1], 1, 1, 0)],
     ]
     image_piece, basis_piece = assemble(messages, (image_span, basis_span))
     if image_rows < size:
-        image_piece = lax.dynamic_slice_in_dim(image_piece, col * image_rows % size, image_rows, 0)
+        image_piece = lax.dynamic_slice_in_dim(image_piece, lax.axis_index("col") * image_rows % size, image_rows, 0)
     if basis_rows < size:
-        basis_piece = lax.dynamic_slice_in_dim(basis_piece, row * basis_rows % size, basis_rows, 0)
+        basis_piece = lax.dynamic_slice_in_dim(basis_piece, lax.axis_index("row") * basis_rows % size, basis_rows, 0)
     return image_piece, basis_piece
 
 

time: 113 us -> 109 us (0.965)
  waiting for transfers between devices: 68.2 us -> 50.2 us
  starting transfers between devices: 28.9 us -> 36.3 us
  Pallas kernels: 12.6 us -> 17.2 us
  other arithmetic: 0.62 us -> 2.02 us
    ppermute x4, waiting for transfers between devices: 26.1 us -> 16 us  [others_z(): lax.ppermute(value, 'col', [(c, (c + 4 * k) % n_col) for c in range(n_col)])]
    ppermute x27 -> x28, starting transfers between devices: 20.8 us -> 26.1 us  [send(): lax.ppermute(value, ('row', 'col'), [(r * n_col + c, (r ^ dx) * n_col + (...]
    ppermute x2 -> x4, waiting for transfers between devices: 11.4 us -> 6.93 us  [others_row(): lax.ppermute(value, 'row', [(r, (r + 2 * k) % n_row) for r in range(n_row)])]
    pallas_call x4 -> x6, Pallas kernels: 7.46 us -> 11.9 us  [block_product(): pl.pallas_call(body, out_shape=out_shape, in_specs=[pl.BlockSpec(memory_s...]
    ppermute x27 -> x28, waiting for transfers between devices: 30.8 us -> 27.3 us  [send(): lax.ppermute(value, ('row', 'col'), [(r * n_col + c, (r ^ dx) * n_col + (...]
    ppermute x2 -> x4, starting transfers between devices: 2.61 us -> 4.37 us  [others_row(): lax.ppermute(value, 'row', [(r, (r + 2 * k) % n_row) for r in range(n_row)])]
  transfers between devices with their start and end apart: 33 -> 37, of which waited for: 16 -> 16; matrix products, arithmetic and copies ran while one was open for 0% -> 2% of each run, Pallas kernels for 3% -> 12%
where the time goes in v2:
time: 109 us
  waiting for transfers between devices  50.2 us (46%)
  starting transfers between devices  36.3 us (33%)
  Pallas kernels  17.2 us (16%)
  other arithmetic  2.02 us (2%)
  between operations  1.58 us (1%)
  local copies, waits for them, and re-layouts  1.39 us (1%)
    ppermute x28, waiting for transfers between devices, send(): lax.ppermute(value, ('row', 'col'), [(r * n_col + c, (r ^ dx) * n_col + (...  27.3 us
    ppermute x28, starting transfers between devices, send(): lax.ppermute(value, ('row', 'col'), [(r * n_col + c, (r ^ dx) * n_col + (...  26.1 us
    ppermute x4, waiting for transfers between devices, others_z(): lax.ppermute(value, 'col', [(c, (c + 4 * k) % n_col) for c in range(n_col)])  16 us
    pallas_call x6, Pallas kernels, block_product(): pl.pallas_call(body, out_shape=out_shape, in_specs=[pl.BlockSpec(memory_s...  11.9 us
    ppermute x4, waiting for transfers between devices, others_row(): lax.ppermute(value, 'row', [(r, (r + 2 * k) % n_row) for r in range(n_row)])  6.93 us
    ppermute x4, starting transfers between devices, others_z(): lax.ppermute(value, 'col', [(c, (c + 4 * k) % n_col) for c in range(n_col)])  5.69 us
    ppermute x4, starting transfers between devices, others_row(): lax.ppermute(value, 'row', [(r, (r + 2 * k) % n_row) for r in range(n_row)])  4.37 us
    pallas_call x1, Pallas kernels, first_product(): pl.pallas_call(body, out_shape=[pltpu.VMEM((4, row_blocks, width, size),...  2.43 us
  transfers between devices with their start and end apart: 37, of which 16 were waited for; matrix products, arithmetic and copies ran while one was open for 2% of the time, Pallas kernels for 12%

profile of v2, /device:TPU:0, one launch (start us, length us, event | category | flops | bytes accessed | tf_op | source)
XLA Modules:
  0.0 108.6 jit_solution(16855747949975558278)
XLA Ops:
  1.3 0.6 copy-done
  1.9 0.7 copy-done.1
  2.6 2.4 %first.1 = (bf16[4,16,32,128]{3,2,1,0:T(8,128)(2,1)S(1)}, bf16[4,16,32,128]{3,2,1,0:T(8,128)(2,1)S(1)}, bf16[10,128,128]{2,1,0:T(8,128)(2,1)S(1)}, bf16[10,128,128]{2,1,0:T(8,128)(2,1)S(1)}) custom-call(s32[1,20]{1,0:T(1,128)S(1)} %copy-done.1, s32[1,20]{1,0:T(1,128)S(1)} %copy-done, s32[1,1]{1,0:T(1,128)} %copy.11.count_ref, bf16[1024,256]{1,0:T(8,128)(2,1)} %start_hbm.1, ...), custom_call_target="tpu_custom_call" | custom-call | tf_op jit(solution)/shard_map/first/pallas_call | solution.py:57
  5.0 0.6 collective-permute-start.20
  5.6 2.6 %collective-permute-start.12 = (bf16[10,128,128]{2,1,0:T(8,128)(2,1)S(1)}, bf16[10,128,128]{2,1,0:T(8,128)(2,1)S(1)}, u32[]{:S(2)}, u32[]{:S(2)}) collective-permute-start(bf16[10,128,128]{2,1,0:T(8,128)(2,1)S(1)} %get-tuple-element.23.refs_2_.refs_5_), channel_id=1, source_target_pairs={{0,2},{1,3},{2,0},{3,1},{4,6},{5,7},{6,4},{7,5},{8,10},{9,11},{10,... | collective-permute-start | bytes 983048 | tf_op jit(solution)/shard_map/ppermute | solution.py:295
  8.2 1.5 %collective-permute-start.8 = (bf16[10,128,128]{2,1,0:T(8,128)(2,1)S(1)}, bf16[10,128,128]{2,1,0:T(8,128)(2,1)S(1)}, u32[]{:S(2)}, u32[]{:S(2)}) collective-permute-start(bf16[10,128,128]{2,1,0:T(8,128)(2,1)S(1)} %get-tuple-element.23.refs_2_.refs_5_), channel_id=1, source_target_pairs={{0,8},{1,9},{2,10},{3,11},{4,12},{5,13},{6,14},{7,15},{8,0},{9,1},... | collective-permute-start | bytes 983048 | tf_op jit(solution)/shard_map/ppermute | solution.py:295
  9.7 0.7 compare_select_fusion
  11.1 0.7 fusion.9
  11.7 1.2 %collective-permute-done = s32[2,20]{1,0:T(2,128)S(1)} collective-permute-done((s32[2,20]{1,0:T(2,128)S(1)}, s32[2,20]{1,0:T(2,128)S(1)}, u32[]{:S(2)}, u32[]{:S(2)}) %collective-permute-start) | collective-permute-done | bytes 192 | tf_op jit(solution)/shard_map/ppermute | solution.py:295
  12.9 0.7 collective-permute-start.1
  13.6 1.4 %collective-permute-start.10 = (bf16[10,128,128]{2,1,0:T(8,128)(2,1)S(1)}, bf16[10,128,128]{2,1,0:T(8,128)(2,1)S(1)}, u32[]{:S(2)}, u32[]{:S(2)}) collective-permute-start(bf16[10,128,128]{2,1,0:T(8,128)(2,1)S(1)} %get-tuple-element.22.refs_0_.refs_3_), channel_id=1, source_target_pairs={{0,2},{1,3},{2,0},{3,1},{4,6},{5,7},{6,4},{7,5},{8,10},{9,11},{10,... | collective-permute-start | bytes 983048 | tf_op jit(solution)/shard_map/ppermute | solution.py:295
  15.0 3.0 %collective-permute-done.1.refs_1_ = s32[2,2,20]{2,1,0:T(2,128)S(1)} collective-permute-done((s32[2,2,20]{2,1,0:T(2,128)S(1)}, s32[2,2,20]{2,1,0:T(2,128)S(1)}, u32[]{:S(2)}, u32[]{:S(2)}) %collective-permute-start.1) | collective-permute-done | bytes 352 | tf_op jit(solution)/shard_map/ppermute | solution.py:295
  18.0 1.5 %collective-permute-start.6 = (bf16[10,128,128]{2,1,0:T(8,128)(2,1)S(1)}, bf16[10,128,128]{2,1,0:T(8,128)(2,1)S(1)}, u32[]{:S(2)}, u32[]{:S(2)}) collective-permute-start(bf16[10,128,128]{2,1,0:T(8,128)(2,1)S(1)} %get-tuple-element.22.refs_0_.refs_3_), channel_id=1, source_target_pairs={{0,8},{1,9},{2,10},{3,11},{4,12},{5,13},{6,14},{7,15},{8,0},{9,1},... | collective-permute-start | bytes 983048 | tf_op jit(solution)/shard_map/ppermute | solution.py:295
  20.1 2.3 %collective-permute-done.21 = bf16[2,16,32,128]{3,2,1,0:T(8,128)(2,1)S(1)} collective-permute-done((bf16[2,16,32,128]{3,2,1,0:T(8,128)(2,1)S(1)}, bf16[2,16,32,128]{3,2,1,0:T(8,128)(2,1)S(1)}, u32[]{:S(2)}, u32[]{:S(2)}) %collective-permute-start.21) | collective-permute-done | bytes 262176 | tf_op jit(solution)/shard_map/ppermute | solution.py:295
  22.4 2.0 %collective-permute-start.2 = (s32[2,2,20]{2,1,0:T(2,128)S(1)}, s32[2,2,20]{2,1,0:T(2,128)S(1)}, u32[]{:S(2)}, u32[]{:S(2)}) collective-permute-start(s32[2,2,20]{2,1,0:T(2,128)S(1)} %pad_add_fusion.refs_0_), channel_id=1, source_target_pairs={{0,2},{1,3},{2,0},{3,1},{4,6},{5,7},{6,4},{7,5},{8,10},{9,11},{10,... | collective-permute-start | bytes 968 | tf_op jit(solution)/shard_map/ppermute | solution.py:295
  24.5 4.7 %collective-permute-done.2.refs_2_ = s32[2,2,20]{2,1,0:T(2,128)S(1)} collective-permute-done((s32[2,2,20]{2,1,0:T(2,128)S(1)}, s32[2,2,20]{2,1,0:T(2,128)S(1)}, u32[]{:S(2)}, u32[]{:S(2)}) %collective-permute-start.2) | collective-permute-done | bytes 352 | tf_op jit(solution)/shard_map/ppermute | solution.py:295
  29.2 1.7 %collective-permute-start.16 = (bf16[6,128,128]{2,1,0:T(8,128)(2,1)S(1)}, bf16[6,128,128]{2,1,0:T(8,128)(2,1)S(1)}, u32[]{:S(2)}, u32[]{:S(2)}) collective-permute-start(bf16[6,128,128]{2,1,0:T(8,128)(2,1)S(1)} %slice.56), channel_id=1, source_target_pairs={{0,8},{1,9},{2,10},{3,11},{4,12},{5,13},{6,14},{7,15},{8,0},{9,1},... | collective-permute-start | bytes 589832 | tf_op jit(solution)/shard_map/ppermute | solution.py:295
  30.9 1.6 %collective-permute-start.18 = (bf16[4,128,128]{2,1,0:T(8,128)(2,1)S(1)}, bf16[4,128,128]{2,1,0:T(8,128)(2,1)S(1)}, u32[]{:S(2)}, u32[]{:S(2)}) collective-permute-start(bf16[4,128,128]{2,1,0:T(8,128)(2,1)S(1)} %slice.57), channel_id=1, source_target_pairs={{0,2},{1,3},{2,0},{3,1},{4,6},{5,7},{6,4},{7,5},{8,10},{9,11},{10,... | collective-permute-start | bytes 393224 | tf_op jit(solution)/shard_map/ppermute | solution.py:295
  33.5 2.3 %collective-permute-done.18.refs_16_.refs_5_ = bf16[4,128,128]{2,1,0:T(8,128)(2,1)S(1)} collective-permute-done((bf16[4,128,128]{2,1,0:T(8,128)(2,1)S(1)}, bf16[4,128,128]{2,1,0:T(8,128)(2,1)S(1)}, u32[]{:S(2)}, u32[]{:S(2)}) %collective-permute-start.18) | collective-permute-done | bytes 131104 | tf_op jit(solution)/shard_map/ppermute | solution.py:295
  36.2 7.3 %collective-permute-done.14.refs_12_.refs_1_ = bf16[10,128,128]{2,1,0:T(8,128)(2,1)S(1)} collective-permute-done((bf16[10,128,128]{2,1,0:T(8,128)(2,1)S(1)}, bf16[10,128,128]{2,1,0:T(8,128)(2,1)S(1)}, u32[]{:S(2)}, u32[]{:S(2)}) %collective-permute-start.14) | collective-permute-done | bytes 327712 | tf_op jit(solution)/shard_map/ppermute | solution.py:295
  43.6 2.1 %collective-permute-done.22 = bf16[16,32,128]{2,1,0:T(8,128)(2,1)S(1)} collective-permute-done((bf16[16,32,128]{2,1,0:T(8,128)(2,1)S(1)}, bf16[16,32,128]{2,1,0:T(8,128)(2,1)S(1)}, u32[]{:S(2)}, u32[]{:S(2)}) %collective-permute-start.22) | collective-permute-done | bytes 131104 | tf_op jit(solution)/shard_map/ppermute | solution.py:295
  45.7 2.5 %collective-permute-start.23 = (bf16[32,32,128]{2,1,0:T(8,128)(2,1)S(1)}, bf16[32,32,128]{2,1,0:T(8,128)(2,1)S(1)}, u32[]{:S(2)}, u32[]{:S(2)}) collective-permute-start(bf16[32,32,128]{2,1,0:T(8,128)(2,1)S(1)} %pad_maximum_fusion.refs_15_.refs_7_), channel_id=1, source_target_pairs={{0,4},{1,5},{2,6},{3,7},{4,0},{5,1},{6,2},{7,3},{8,12},{9,13},{10,... | collective-permute-start | bytes 786440 | tf_op jit(solution)/shard_map/ppermute | solution.py:301
  48.8 2.5 %collective-permute-start.3 = (s32[2,2,20]{2,1,0:T(2,128)S(1)}, s32[2,2,20]{2,1,0:T(2,128)S(1)}, u32[]{:S(2)}, u32[]{:S(2)}) collective-permute-start(s32[2,2,20]{2,1,0:T(2,128)S(1)} %pad_add_fusion.refs_0_), channel_id=1, source_target_pairs={{0,10},{1,11},{2,8},{3,9},{4,14},{5,15},{6,12},{7,13},{8,2},{9,3},... | collective-permute-start | bytes 968 | tf_op jit(solution)/shard_map/ppermute | solution.py:295
  51.3 9.7 %collective-permute-done.23.refs_16_.refs_8_ = bf16[32,32,128]{2,1,0:T(8,128)(2,1)S(1)} collective-permute-done((bf16[32,32,128]{2,1,0:T(8,128)(2,1)S(1)}, bf16[32,32,128]{2,1,0:T(8,128)(2,1)S(1)}, u32[]{:S(2)}, u32[]{:S(2)}) %collective-permute-start.23) | collective-permute-done | bytes 262176 | tf_op jit(solution)/shard_map/ppermute | solution.py:301
  61.0 1.8 %product.6.refs_9_ = f32[33,32,128]{2,1,0:T(8,128)S(1)} custom-call(s32[2,2,20]{2,1,0:T(2,128)S(1)} %pad_add_fusion.refs_0_, s32[2,2,20]{2,1,0:T(2,128)S(1)} %collective-permute-done.1.refs_1_, s32[2,2,20]{2,1,0:T(2,128)S(1)} %collective-permute-done.2.refs_2_, bf16[10,128,128]{2,1,0:T(8,128)(2,1)S(1)} %get-tuple-element.22.refs_0_.refs_3_, ...), custom_call_target="tpu_custom_call" | custom-call | tf_op jit(solution)/shard_map/product/pallas_call | solution.py:190
  62.9 1.1 product.7
  64.0 1.5 %collective-permute-start.26 = (bf16[32,16,128]{2,1,0:T(8,128)(2,1)S(1)}, bf16[32,16,128]{2,1,0:T(8,128)(2,1)S(1)}, u32[]{:S(2)}, u32[]{:S(2)}) collective-permute-start(bf16[32,16,128]{2,1,0:T(8,128)(2,1)S(1)} %get-tuple-element.27.refs_5_), channel_id=1, source_target_pairs={{0,16},{8,24},{16,0},{24,8},{1,17},{9,25},{17,1},{25,9},{2,18},{10... | collective-permute-start | bytes 393224 | tf_op jit(solution)/shard_map/ppermute | solution.py:307
  65.5 0.6 collective-permute-start.24
  66.1 1.8 %flip.1.refs_4_ = bf16[320,128,128]{2,1,0:T(8,128)(2,1)S(1)} custom-call(bf16[10,128,128]{2,1,0:T(8,128)(2,1)S(1)} %get-tuple-element.22.refs_0_.refs_3_, bf16[10,128,128]{2,1,0:T(8,128)(2,1)S(1)} %collective-permute-done.4.refs_1_.refs_4_, bf16[10,128,128]{2,1,0:T(8,128)(2,1)S(1)} %get-tuple-element.23.refs_2_.refs_5_, ...), custom_call_target="tpu_custom_call" | custom-call | tf_op jit(solution)/shard_map/flip/pallas_call | solution.py:94
  67.9 2.5 %collective-permute-done.26.refs_6_ = bf16[32,16,128]{2,1,0:T(8,128)(2,1)S(1)} collective-permute-done((bf16[32,16,128]{2,1,0:T(8,128)(2,1)S(1)}, bf16[32,16,128]{2,1,0:T(8,128)(2,1)S(1)}, u32[]{:S(2)}, u32[]{:S(2)}) %collective-permute-start.26) | collective-permute-done | bytes 131104 | tf_op jit(solution)/shard_map/ppermute | solution.py:307
  70.5 2.2 %product.10.refs_5_ = bf16[33,16,128]{2,1,0:T(8,128)(2,1)S(1)} custom-call(s32[2,2,20]{2,1,0:T(2,128)S(1)} %pad_add_fusion.refs_0_, s32[2,2,20]{2,1,0:T(2,128)S(1)} %collective-permute-done.1.refs_1_, s32[2,2,20]{2,1,0:T(2,128)S(1)} %collective-permute-done.2.refs_2_, s32[2,2,20]{2,1,0:T(2,128)S(1)} %collective-permute-done.3.refs_0_.refs_3_, ...), custom_call_target="tpu_custom_call" | custom-call | tf_op jit(solution)/shard_map/product/pallas_call | solution.py:190
  72.8 2.2 %product.8.refs_5_ = bf16[33,16,128]{2,1,0:T(8,128)(2,1)S(1)} custom-call(s32[2,2,20]{2,1,0:T(2,128)S(1)} %pad_add_fusion.refs_0_, s32[2,2,20]{2,1,0:T(2,128)S(1)} %collective-permute-done.1.refs_1_, s32[2,2,20]{2,1,0:T(2,128)S(1)} %collective-permute-done.2.refs_2_, s32[2,2,20]{2,1,0:T(2,128)S(1)} %collective-permute-done.3.refs_0_.refs_3_, ...), custom_call_target="tpu_custom_call" | custom-call | tf_op jit(solution)/shard_map/product/pallas_call | solution.py:190
  75.0 3.0 %collective-permute-start.25 = (bf16[33,16,128]{2,1,0:T(8,128)(2,1)S(1)}, bf16[33,16,128]{2,1,0:T(8,128)(2,1)S(1)}, u32[]{:S(2)}, u32[]{:S(2)}) collective-permute-start(bf16[33,16,128]{2,1,0:T(8,128)(2,1)S(1)} %product.8.refs_5_), channel_id=1, source_target_pairs={{0,4},{1,5},{2,6},{3,7},{4,0},{5,1},{6,2},{7,3},{8,12},{9,13},{10,... | collective-permute-start | bytes 405512 | tf_op jit(solution)/shard_map/ppermute | solution.py:301
  78.0 4.5 %collective-permute-done.27.refs_6_ = bf16[33,16,128]{2,1,0:T(8,128)(2,1)S(1)} collective-permute-done((bf16[33,16,128]{2,1,0:T(8,128)(2,1)S(1)}, bf16[33,16,128]{2,1,0:T(8,128)(2,1)S(1)}, u32[]{:S(2)}, u32[]{:S(2)}) %collective-permute-start.27) | collective-permute-done | bytes 135200 | tf_op jit(solution)/shard_map/ppermute | solution.py:301
  82.6 2.2 %product.11 = (bf16[32,16,128]{2,1,0:T(8,128)(2,1)S(1)}, bf16[32,16,128]{2,1,0:T(8,128)(2,1)S(1)}) custom-call(s32[2,2,20]{2,1,0:T(2,128)S(1)} %pad_add_fusion.refs_0_, s32[2,2,20]{2,1,0:T(2,128)S(1)} %collective-permute-done.1.refs_1_, s32[2,2,20]{2,1,0:T(2,128)S(1)} %collective-permute-done.2.refs_2_, ...), custom_call_target="tpu_custom_call" | custom-call | tf_op jit(solution)/shard_map/product/pallas_call | solution.py:190
  84.8 1.6 %collective-permute-start.29 = (bf16[32,16,128]{2,1,0:T(8,128)(2,1)S(1)}, bf16[32,16,128]{2,1,0:T(8,128)(2,1)S(1)}, u32[]{:S(2)}, u32[]{:S(2)}) collective-permute-start(bf16[32,16,128]{2,1,0:T(8,128)(2,1)S(1)} %get-tuple-element.30.refs_4_), channel_id=1, source_target_pairs={{0,16},{8,24},{16,0},{24,8},{1,17},{9,25},{17,1},{25,9},{2,18},{10... | collective-permute-start | bytes 393224 | tf_op jit(solution)/shard_map/ppermute | solution.py:307
  86.5 2.2 %product.9 = (bf16[32,16,128]{2,1,0:T(8,128)(2,1)S(1)}, bf16[32,16,128]{2,1,0:T(8,128)(2,1)S(1)}) custom-call(s32[2,2,20]{2,1,0:T(2,128)S(1)} %pad_add_fusion.refs_0_, s32[2,2,20]{2,1,0:T(2,128)S(1)} %collective-permute-done.1.refs_1_, s32[2,2,20]{2,1,0:T(2,128)S(1)} %collective-permute-done.2.refs_2_, ...), custom_call_target="tpu_custom_call" | custom-call | tf_op jit(solution)/shard_map/product/pallas_call | solution.py:190
  88.7 0.6 collective-permute-start.28
  89.4 0.6 collective-permute-done.29.refs_5_
  90.0 3.8 %collective-permute-done.28.refs_3_ = bf16[32,16,128]{2,1,0:T(8,128)(2,1)S(1)} collective-permute-done((bf16[32,16,128]{2,1,0:T(8,128)(2,1)S(1)}, bf16[32,16,128]{2,1,0:T(8,128)(2,1)S(1)}, u32[]{:S(2)}, u32[]{:S(2)}) %collective-permute-start.28) | collective-permute-done | bytes 131104 | tf_op jit(solution)/shard_map/ppermute | solution.py:307
  94.1 2.9 %collective-permute-start.33 = (f32[32,128]{1,0:T(8,128)S(1)}, f32[32,128]{1,0:T(8,128)S(1)}, u32[]{:S(2)}, u32[]{:S(2)}) collective-permute-start(f32[32,128]{1,0:T(8,128)S(1)} %get-tuple-element.32), channel_id=1, source_target_pairs={{0,1},{1,0},{2,3},{3,2},{4,5},{5,4},{6,7},{7,6},{8,9},{9,8},{10,11... | collective-permute-start | bytes 49160 | tf_op jit(solution)/shard_map/ppermute | solution.py:295
  97.1 1.7 %collective-permute-done.30 = f32[32,128]{1,0:T(8,128)S(1)} collective-permute-done((f32[32,128]{1,0:T(8,128)S(1)}, f32[32,128]{1,0:T(8,128)S(1)}, u32[]{:S(2)}, u32[]{:S(2)}) %collective-permute-start.30) | collective-permute-done | bytes 16416 | tf_op jit(solution)/shard_map/ppermute | solution.py:301
  99.3 3.5 %collective-permute-start.36 = (bf16[2,4,32,128]{3,2,1,0:T(8,128)(2,1)S(1)}, bf16[2,4,32,128]{3,2,1,0:T(8,128)(2,1)S(1)}, u32[]{:S(2)}, u32[]{:S(2)}) collective-permute-start(bf16[2,4,32,128]{3,2,1,0:T(8,128)(2,1)S(1)} %pad_maximum_fusion.4), channel_id=1, source_target_pairs={{0,10},{1,11},{2,8},{3,9},{4,14},{5,15},{6,12},{7,13},{8,2},{9,3},... | collective-permute-start | bytes 196616 | tf_op jit(solution)/shard_map/ppermute | solution.py:295
  102.8 0.6 collective-permute-start.35
  103.5 1.7 %collective-permute-done.36.refs_3_ = bf16[2,4,32,128]{3,2,1,0:T(8,128)(2,1)S(1)} collective-permute-done((bf16[2,4,32,128]{3,2,1,0:T(8,128)(2,1)S(1)}, bf16[2,4,32,128]{3,2,1,0:T(8,128)(2,1)S(1)}, u32[]{:S(2)}, u32[]{:S(2)}) %collective-permute-start.36) | collective-permute-done | bytes 65568 | tf_op jit(solution)/shard_map/ppermute | solution.py:295
  105.2 1.9 %collective-permute-done.35.refs_2_ = bf16[2,4,32,128]{3,2,1,0:T(8,128)(2,1)S(1)} collective-permute-done((bf16[2,4,32,128]{3,2,1,0:T(8,128)(2,1)S(1)}, bf16[2,4,32,128]{3,2,1,0:T(8,128)(2,1)S(1)}, u32[]{:S(2)}, u32[]{:S(2)}) %collective-permute-start.35) | collective-permute-done | bytes 65568 | tf_op jit(solution)/shard_map/ppermute | solution.py:295
  107.1 0.6 collective-permute-done.34.refs_1_
  107.7 0.8 assemble.1
  (64 shorter events, 4.3 us)
Async XLA Ops:
  1.3 0.7 copy-start
  1.9 0.7 copy-start.1
  5.0 5.3 %collective-permute-start.20 = (bf16[4,16,32,128]{3,2,1,0:T(8,128)(2,1)S(1)}, bf16[4,16,32,128]{3,2,1,0:T(8,128)(2,1)S(1)}, u32[]{:S(2)}, u32[]{:S(2)}) collective-permute-start(bf16[4,16,32,128]{3,2,1,0:T(8,128)(2,1)S(1)} %get-tuple-element.18), channel_id=1, source_target_pairs={{0,1},{1,0},{2,3},{3,2},{4,5},{5,4},{6,7},{7,6},{8,9},{9,8},{10,11... | collective-permute-start | bytes 1572872 | tf_op jit(solution)/shard_map/ppermute | solution.py:295
  5.6 13.9 %collective-permute-start.12 = (bf16[10,128,128]{2,1,0:T(8,128)(2,1)S(1)}, bf16[10,128,128]{2,1,0:T(8,128)(2,1)S(1)}, u32[]{:S(2)}, u32[]{:S(2)}) collective-permute-start(bf16[10,128,128]{2,1,0:T(8,128)(2,1)S(1)} %get-tuple-element.23.refs_2_.refs_5_), channel_id=1, source_target_pairs={{0,2},{1,3},{2,0},{3,1},{4,6},{5,7},{6,4},{7,5},{8,10},{9,11},{10,... | collective-permute-start | bytes 983048 | tf_op jit(solution)/shard_map/ppermute | solution.py:295
  8.2 11.3 %collective-permute-start.8 = (bf16[10,128,128]{2,1,0:T(8,128)(2,1)S(1)}, bf16[10,128,128]{2,1,0:T(8,128)(2,1)S(1)}, u32[]{:S(2)}, u32[]{:S(2)}) collective-permute-start(bf16[10,128,128]{2,1,0:T(8,128)(2,1)S(1)} %get-tuple-element.23.refs_2_.refs_5_), channel_id=1, source_target_pairs={{0,8},{1,9},{2,10},{3,11},{4,12},{5,13},{6,14},{7,15},{8,0},{9,1},... | collective-permute-start | bytes 983048 | tf_op jit(solution)/shard_map/ppermute | solution.py:295
  10.6 11.8 %collective-permute-start.21 = (bf16[2,16,32,128]{3,2,1,0:T(8,128)(2,1)S(1)}, bf16[2,16,32,128]{3,2,1,0:T(8,128)(2,1)S(1)}, u32[]{:S(2)}, u32[]{:S(2)}) collective-permute-start(bf16[2,16,32,128]{3,2,1,0:T(8,128)(2,1)S(1)} %slice_bitcast_fusion), channel_id=1, source_target_pairs={{0,2},{1,3},{2,0},{3,1},{4,6},{5,7},{6,4},{7,5},{8,10},{9,11},{10,... | collective-permute-start | bytes 786440 | tf_op jit(solution)/shard_map/ppermute | solution.py:295
  11.7 1.2 %collective-permute-start = (s32[2,20]{1,0:T(2,128)S(1)}, s32[2,20]{1,0:T(2,128)S(1)}, u32[]{:S(2)}, u32[]{:S(2)}) collective-permute-start(s32[2,20]{1,0:T(2,128)S(1)} %get-tuple-element.45), channel_id=1, source_target_pairs={{0,1},{1,0},{2,3},{3,2},{4,5},{5,4},{6,7},{7,6},{8,9},{9,8},{10,11... | collective-permute-start | bytes 488 | tf_op jit(solution)/shard_map/ppermute | solution.py:295
  12.9 5.1 %collective-permute-start.1 = (s32[2,2,20]{2,1,0:T(2,128)S(1)}, s32[2,2,20]{2,1,0:T(2,128)S(1)}, u32[]{:S(2)}, u32[]{:S(2)}) collective-permute-start(s32[2,2,20]{2,1,0:T(2,128)S(1)} %pad_add_fusion.refs_0_), channel_id=1, source_target_pairs={{0,8},{1,9},{2,10},{3,11},{4,12},{5,13},{6,14},{7,15},{8,0},{9,1},... | collective-permute-start | bytes 968 | tf_op jit(solution)/shard_map/ppermute | solution.py:295
  13.6 17.3 %collective-permute-start.10 = (bf16[10,128,128]{2,1,0:T(8,128)(2,1)S(1)}, bf16[10,128,128]{2,1,0:T(8,128)(2,1)S(1)}, u32[]{:S(2)}, u32[]{:S(2)}) collective-permute-start(bf16[10,128,128]{2,1,0:T(8,128)(2,1)S(1)} %get-tuple-element.22.refs_0_.refs_3_), channel_id=1, source_target_pairs={{0,2},{1,3},{2,0},{3,1},{4,6},{5,7},{6,4},{7,5},{8,10},{9,11},{10,... | collective-permute-start | bytes 983048 | tf_op jit(solution)/shard_map/ppermute | solution.py:295
  18.0 14.4 %collective-permute-start.6 = (bf16[10,128,128]{2,1,0:T(8,128)(2,1)S(1)}, bf16[10,128,128]{2,1,0:T(8,128)(2,1)S(1)}, u32[]{:S(2)}, u32[]{:S(2)}) collective-permute-start(bf16[10,128,128]{2,1,0:T(8,128)(2,1)S(1)} %get-tuple-element.22.refs_0_.refs_3_), channel_id=1, source_target_pairs={{0,8},{1,9},{2,10},{3,11},{4,12},{5,13},{6,14},{7,15},{8,0},{9,1},... | collective-permute-start | bytes 983048 | tf_op jit(solution)/shard_map/ppermute | solution.py:295
  19.5 12.9 %collective-permute-start.4 = (bf16[10,128,128]{2,1,0:T(8,128)(2,1)S(1)}, bf16[10,128,128]{2,1,0:T(8,128)(2,1)S(1)}, u32[]{:S(2)}, u32[]{:S(2)}) collective-permute-start(bf16[10,128,128]{2,1,0:T(8,128)(2,1)S(1)} %get-tuple-element.22.refs_0_.refs_3_), channel_id=1, source_target_pairs={{0,1},{1,0},{2,3},{3,2},{4,5},{5,4},{6,7},{7,6},{8,9},{9,8},{10,11... | collective-permute-start | bytes 983048 | tf_op jit(solution)/shard_map/ppermute | solution.py:295
  19.5 13.4 %collective-permute-start.5 = (bf16[10,128,128]{2,1,0:T(8,128)(2,1)S(1)}, bf16[10,128,128]{2,1,0:T(8,128)(2,1)S(1)}, u32[]{:S(2)}, u32[]{:S(2)}) collective-permute-start(bf16[10,128,128]{2,1,0:T(8,128)(2,1)S(1)} %get-tuple-element.23.refs_2_.refs_5_), channel_id=1, source_target_pairs={{0,1},{1,0},{2,3},{3,2},{4,5},{5,4},{6,7},{7,6},{8,9},{9,8},{10,11... | collective-permute-start | bytes 983048 | tf_op jit(solution)/shard_map/ppermute | solution.py:295
  22.4 6.8 %collective-permute-start.2 = (s32[2,2,20]{2,1,0:T(2,128)S(1)}, s32[2,2,20]{2,1,0:T(2,128)S(1)}, u32[]{:S(2)}, u32[]{:S(2)}) collective-permute-start(s32[2,2,20]{2,1,0:T(2,128)S(1)} %pad_add_fusion.refs_0_), channel_id=1, source_target_pairs={{0,2},{1,3},{2,0},{3,1},{4,6},{5,7},{6,4},{7,5},{8,10},{9,11},{10,... | collective-permute-start | bytes 968 | tf_op jit(solution)/shard_map/ppermute | solution.py:295
  29.2 7.0 %collective-permute-start.16 = (bf16[6,128,128]{2,1,0:T(8,128)(2,1)S(1)}, bf16[6,128,128]{2,1,0:T(8,128)(2,1)S(1)}, u32[]{:S(2)}, u32[]{:S(2)}) collective-permute-start(bf16[6,128,128]{2,1,0:T(8,128)(2,1)S(1)} %slice.56), channel_id=1, source_target_pairs={{0,8},{1,9},{2,10},{3,11},{4,12},{5,13},{6,14},{7,15},{8,0},{9,1},... | collective-permute-start | bytes 589832 | tf_op jit(solution)/shard_map/ppermute | solution.py:295
  30.9 5.0 %collective-permute-start.18 = (bf16[4,128,128]{2,1,0:T(8,128)(2,1)S(1)}, bf16[4,128,128]{2,1,0:T(8,128)(2,1)S(1)}, u32[]{:S(2)}, u32[]{:S(2)}) collective-permute-start(bf16[4,128,128]{2,1,0:T(8,128)(2,1)S(1)} %slice.57), channel_id=1, source_target_pairs={{0,2},{1,3},{2,0},{3,1},{4,6},{5,7},{6,4},{7,5},{8,10},{9,11},{10,... | collective-permute-start | bytes 393224 | tf_op jit(solution)/shard_map/ppermute | solution.py:295
  32.5 15.8 %collective-permute-start.13 = (bf16[10,128,128]{2,1,0:T(8,128)(2,1)S(1)}, bf16[10,128,128]{2,1,0:T(8,128)(2,1)S(1)}, u32[]{:S(2)}, u32[]{:S(2)}) collective-permute-start(bf16[10,128,128]{2,1,0:T(8,128)(2,1)S(1)} %collective-permute-done.12.refs_10_.refs_13_), channel_id=1, source_target_pairs={{0,1},{1,0},{2,3},{3,2},{4,5},{5,4},{6,7},{7,6},{8,9},{9,8},{10,11... | collective-permute-start | bytes 983048 | tf_op jit(solution)/shard_map/ppermute | solution.py:295
  32.5 13.3 %collective-permute-start.11 = (bf16[10,128,128]{2,1,0:T(8,128)(2,1)S(1)}, bf16[10,128,128]{2,1,0:T(8,128)(2,1)S(1)}, u32[]{:S(2)}, u32[]{:S(2)}) collective-permute-start(bf16[10,128,128]{2,1,0:T(8,128)(2,1)S(1)} %collective-permute-done.10.refs_8_.refs_11_), channel_id=1, source_target_pairs={{0,1},{1,0},{2,3},{3,2},{4,5},{5,4},{6,7},{7,6},{8,9},{9,8},{10,11... | collective-permute-start | bytes 983048 | tf_op jit(solution)/shard_map/ppermute | solution.py:295
  33.0 10.6 %collective-permute-start.14 = (bf16[10,128,128]{2,1,0:T(8,128)(2,1)S(1)}, bf16[10,128,128]{2,1,0:T(8,128)(2,1)S(1)}, u32[]{:S(2)}, u32[]{:S(2)}) collective-permute-start(bf16[10,128,128]{2,1,0:T(8,128)(2,1)S(1)} %collective-permute-done.10.refs_8_.refs_11_), channel_id=1, source_target_pairs={{0,8},{1,9},{2,10},{3,11},{4,12},{5,13},{6,14},{7,15},{8,0},{9,1},... | collective-permute-start | bytes 983048 | tf_op jit(solution)/shard_map/ppermute | solution.py:295
  35.8 9.9 %collective-permute-start.22 = (bf16[16,32,128]{2,1,0:T(8,128)(2,1)S(1)}, bf16[16,32,128]{2,1,0:T(8,128)(2,1)S(1)}, u32[]{:S(2)}, u32[]{:S(2)}) collective-permute-start(bf16[16,32,128]{2,1,0:T(8,128)(2,1)S(1)} %get-tuple-element.35), channel_id=1, source_target_pairs={{0,8},{1,9},{2,10},{3,11},{4,12},{5,13},{6,14},{7,15},{8,0},{9,1},... | collective-permute-start | bytes 393224 | tf_op jit(solution)/shard_map/ppermute | solution.py:295
  36.2 12.3 %collective-permute-start.9 = (bf16[10,128,128]{2,1,0:T(8,128)(2,1)S(1)}, bf16[10,128,128]{2,1,0:T(8,128)(2,1)S(1)}, u32[]{:S(2)}, u32[]{:S(2)}) collective-permute-start(bf16[10,128,128]{2,1,0:T(8,128)(2,1)S(1)} %collective-permute-done.8.refs_6_.refs_9_), channel_id=1, source_target_pairs={{0,1},{1,0},{2,3},{3,2},{4,5},{5,4},{6,7},{7,6},{8,9},{9,8},{10,11... | collective-permute-start | bytes 983048 | tf_op jit(solution)/shard_map/ppermute | solution.py:295
  43.6 5.3 %collective-permute-start.7 = (bf16[10,128,128]{2,1,0:T(8,128)(2,1)S(1)}, bf16[10,128,128]{2,1,0:T(8,128)(2,1)S(1)}, u32[]{:S(2)}, u32[]{:S(2)}) collective-permute-start(bf16[10,128,128]{2,1,0:T(8,128)(2,1)S(1)} %collective-permute-done.6.refs_4_.refs_7_), channel_id=1, source_target_pairs={{0,1},{1,0},{2,3},{3,2},{4,5},{5,4},{6,7},{7,6},{8,9},{9,8},{10,11... | collective-permute-start | bytes 983048 | tf_op jit(solution)/shard_map/ppermute | solution.py:295
  45.7 17.2 %collective-permute-start.15 = (bf16[10,128,128]{2,1,0:T(8,128)(2,1)S(1)}, bf16[10,128,128]{2,1,0:T(8,128)(2,1)S(1)}, u32[]{:S(2)}, u32[]{:S(2)}) collective-permute-start(bf16[10,128,128]{2,1,0:T(8,128)(2,1)S(1)} %collective-permute-done.14.refs_12_.refs_1_), channel_id=1, source_target_pairs={{0,1},{1,0},{2,3},{3,2},{4,5},{5,4},{6,7},{7,6},{8,9},{9,8},{10,11... | collective-permute-start | bytes 983048 | tf_op jit(solution)/shard_map/ppermute | solution.py:295
  45.7 15.3 %collective-permute-start.23 = (bf16[32,32,128]{2,1,0:T(8,128)(2,1)S(1)}, bf16[32,32,128]{2,1,0:T(8,128)(2,1)S(1)}, u32[]{:S(2)}, u32[]{:S(2)}) collective-permute-start(bf16[32,32,128]{2,1,0:T(8,128)(2,1)S(1)} %pad_maximum_fusion.refs_15_.refs_7_), channel_id=1, source_target_pairs={{0,4},{1,5},{2,6},{3,7},{4,0},{5,1},{6,2},{7,3},{8,12},{9,13},{10,... | collective-permute-start | bytes 786440 | tf_op jit(solution)/shard_map/ppermute | solution.py:301
  48.3 14.6 %collective-permute-start.17 = (bf16[6,128,128]{2,1,0:T(8,128)(2,1)S(1)}, bf16[6,128,128]{2,1,0:T(8,128)(2,1)S(1)}, u32[]{:S(2)}, u32[]{:S(2)}) collective-permute-start(bf16[6,128,128]{2,1,0:T(8,128)(2,1)S(1)} %collective-permute-done.16.refs_14_.refs_3_), channel_id=1, source_target_pairs={{0,1},{1,0},{2,3},{3,2},{4,5},{5,4},{6,7},{7,6},{8,9},{9,8},{10,11... | collective-permute-start | bytes 589832 | tf_op jit(solution)/shard_map/ppermute | solution.py:295
  48.5 14.4 %collective-permute-start.19 = (bf16[4,128,128]{2,1,0:T(8,128)(2,1)S(1)}, bf16[4,128,128]{2,1,0:T(8,128)(2,1)S(1)}, u32[]{:S(2)}, u32[]{:S(2)}) collective-permute-start(bf16[4,128,128]{2,1,0:T(8,128)(2,1)S(1)} %collective-permute-done.18.refs_16_.refs_5_), channel_id=1, source_target_pairs={{0,1},{1,0},{2,3},{3,2},{4,5},{5,4},{6,7},{7,6},{8,9},{9,8},{10,11... | collective-permute-start | bytes 393224 | tf_op jit(solution)/shard_map/ppermute | solution.py:295
  48.8 14.1 %collective-permute-start.3 = (s32[2,2,20]{2,1,0:T(2,128)S(1)}, s32[2,2,20]{2,1,0:T(2,128)S(1)}, u32[]{:S(2)}, u32[]{:S(2)}) collective-permute-start(s32[2,2,20]{2,1,0:T(2,128)S(1)} %pad_add_fusion.refs_0_), channel_id=1, source_target_pairs={{0,10},{1,11},{2,8},{3,9},{4,14},{5,15},{6,12},{7,13},{8,2},{9,3},... | collective-permute-start | bytes 968 | tf_op jit(solution)/shard_map/ppermute | solution.py:295
  64.0 6.4 %collective-permute-start.26 = (bf16[32,16,128]{2,1,0:T(8,128)(2,1)S(1)}, bf16[32,16,128]{2,1,0:T(8,128)(2,1)S(1)}, u32[]{:S(2)}, u32[]{:S(2)}) collective-permute-start(bf16[32,16,128]{2,1,0:T(8,128)(2,1)S(1)} %get-tuple-element.27.refs_5_), channel_id=1, source_target_pairs={{0,16},{8,24},{16,0},{24,8},{1,17},{9,25},{17,1},{25,9},{2,18},{10... | collective-permute-start | bytes 393224 | tf_op jit(solution)/shard_map/ppermute | solution.py:307
  65.5 7.3 %collective-permute-start.24 = (bf16[32,16,128]{2,1,0:T(8,128)(2,1)S(1)}, bf16[32,16,128]{2,1,0:T(8,128)(2,1)S(1)}, u32[]{:S(2)}, u32[]{:S(2)}) collective-permute-start(bf16[32,16,128]{2,1,0:T(8,128)(2,1)S(1)} %get-tuple-element.25.refs_5_), channel_id=1, source_target_pairs={{0,16},{8,24},{16,0},{24,8},{1,17},{9,25},{17,1},{25,9},{2,18},{10... | collective-permute-start | bytes 393224 | tf_op jit(solution)/shard_map/ppermute | solution.py:307
  72.7 9.9 %collective-permute-start.27 = (bf16[33,16,128]{2,1,0:T(8,128)(2,1)S(1)}, bf16[33,16,128]{2,1,0:T(8,128)(2,1)S(1)}, u32[]{:S(2)}, u32[]{:S(2)}) collective-permute-start(bf16[33,16,128]{2,1,0:T(8,128)(2,1)S(1)} %product.10.refs_5_), channel_id=1, source_target_pairs={{0,4},{1,5},{2,6},{3,7},{4,0},{5,1},{6,2},{7,3},{8,12},{9,13},{10,... | collective-permute-start | bytes 405512 | tf_op jit(solution)/shard_map/ppermute | solution.py:301
  75.0 11.4 %collective-permute-start.25 = (bf16[33,16,128]{2,1,0:T(8,128)(2,1)S(1)}, bf16[33,16,128]{2,1,0:T(8,128)(2,1)S(1)}, u32[]{:S(2)}, u32[]{:S(2)}) collective-permute-start(bf16[33,16,128]{2,1,0:T(8,128)(2,1)S(1)} %product.8.refs_5_), channel_id=1, source_target_pairs={{0,4},{1,5},{2,6},{3,7},{4,0},{5,1},{6,2},{7,3},{8,12},{9,13},{10,... | collective-permute-start | bytes 405512 | tf_op jit(solution)/shard_map/ppermute | solution.py:301
  84.8 5.1 %collective-permute-start.29 = (bf16[32,16,128]{2,1,0:T(8,128)(2,1)S(1)}, bf16[32,16,128]{2,1,0:T(8,128)(2,1)S(1)}, u32[]{:S(2)}, u32[]{:S(2)}) collective-permute-start(bf16[32,16,128]{2,1,0:T(8,128)(2,1)S(1)} %get-tuple-element.30.refs_4_), channel_id=1, source_target_pairs={{0,16},{8,24},{16,0},{24,8},{1,17},{9,25},{17,1},{25,9},{2,18},{10... | collective-permute-start | bytes 393224 | tf_op jit(solution)/shard_map/ppermute | solution.py:307
  88.7 5.0 %collective-permute-start.28 = (bf16[32,16,128]{2,1,0:T(8,128)(2,1)S(1)}, bf16[32,16,128]{2,1,0:T(8,128)(2,1)S(1)}, u32[]{:S(2)}, u32[]{:S(2)}) collective-permute-start(bf16[32,16,128]{2,1,0:T(8,128)(2,1)S(1)} %get-tuple-element.29.refs_2_), channel_id=1, source_target_pairs={{0,16},{8,24},{16,0},{24,8},{1,17},{9,25},{17,1},{25,9},{2,18},{10... | collective-permute-start | bytes 393224 | tf_op jit(solution)/shard_map/ppermute | solution.py:307
  94.0 4.8 %collective-permute-start.30 = (f32[32,128]{1,0:T(8,128)S(1)}, f32[32,128]{1,0:T(8,128)S(1)}, u32[]{:S(2)}, u32[]{:S(2)}) collective-permute-start(f32[32,128]{1,0:T(8,128)S(1)} %get-tuple-element.32), channel_id=1, source_target_pairs={{0,4},{1,5},{2,6},{3,7},{4,0},{5,1},{6,2},{7,3},{8,12},{9,13},{10,... | collective-permute-start | bytes 49160 | tf_op jit(solution)/shard_map/ppermute | solution.py:301
  94.1 5.0 %collective-permute-start.32 = (f32[32,128]{1,0:T(8,128)S(1)}, f32[32,128]{1,0:T(8,128)S(1)}, u32[]{:S(2)}, u32[]{:S(2)}) collective-permute-start(f32[32,128]{1,0:T(8,128)S(1)} %get-tuple-element.32), channel_id=1, source_target_pairs={{0,5},{1,4},{2,7},{3,6},{4,1},{5,0},{6,3},{7,2},{8,13},{9,12},{10,... | collective-permute-start | bytes 49160 | tf_op jit(solution)/shard_map/ppermute | solution.py:369
  94.1 4.9 %collective-permute-start.33 = (f32[32,128]{1,0:T(8,128)S(1)}, f32[32,128]{1,0:T(8,128)S(1)}, u32[]{:S(2)}, u32[]{:S(2)}) collective-permute-start(f32[32,128]{1,0:T(8,128)S(1)} %get-tuple-element.32), channel_id=1, source_target_pairs={{0,1},{1,0},{2,3},{3,2},{4,5},{5,4},{6,7},{7,6},{8,9},{9,8},{10,11... | collective-permute-start | bytes 49160 | tf_op jit(solution)/shard_map/ppermute | solution.py:295
  97.1 2.1 %collective-permute-start.31 = (bf16[2,2,4,32,128]{4,3,2,1,0:T(8,128)(2,1)S(1)}, bf16[2,2,4,32,128]{4,3,2,1,0:T(8,128)(2,1)S(1)}, u32[]{:S(2)}, u32[]{:S(2)}) collective-permute-start(bf16[2,2,4,32,128]{4,3,2,1,0:T(8,128)(2,1)S(1)} %get-tuple-element.33), channel_id=1, source_target_pairs={{0,1},{1,0},{2,3},{3,2},{4,5},{5,4},{6,7},{7,6},{8,9},{9,8},{10,11... | collective-permute-start | bytes 393224 | tf_op jit(solution)/shard_map/ppermute | solution.py:295
  99.3 5.9 %collective-permute-start.36 = (bf16[2,4,32,128]{3,2,1,0:T(8,128)(2,1)S(1)}, bf16[2,4,32,128]{3,2,1,0:T(8,128)(2,1)S(1)}, u32[]{:S(2)}, u32[]{:S(2)}) collective-permute-start(bf16[2,4,32,128]{3,2,1,0:T(8,128)(2,1)S(1)} %pad_maximum_fusion.4), channel_id=1, source_target_pairs={{0,10},{1,11},{2,8},{3,9},{4,14},{5,15},{6,12},{7,13},{8,2},{9,3},... | collective-permute-start | bytes 196616 | tf_op jit(solution)/shard_map/ppermute | solution.py:295
  102.8 4.3 %collective-permute-start.35 = (bf16[2,4,32,128]{3,2,1,0:T(8,128)(2,1)S(1)}, bf16[2,4,32,128]{3,2,1,0:T(8,128)(2,1)S(1)}, u32[]{:S(2)}, u32[]{:S(2)}) collective-permute-start(bf16[2,4,32,128]{3,2,1,0:T(8,128)(2,1)S(1)} %pad_maximum_fusion.3), channel_id=1, source_target_pairs={{0,8},{1,9},{2,10},{3,11},{4,12},{5,13},{6,14},{7,15},{8,0},{9,1},... | collective-permute-start | bytes 196616 | tf_op jit(solution)/shard_map/ppermute | solution.py:295
  103.4 4.3 %collective-permute-start.34 = (bf16[2,4,32,128]{3,2,1,0:T(8,128)(2,1)S(1)}, bf16[2,4,32,128]{3,2,1,0:T(8,128)(2,1)S(1)}, u32[]{:S(2)}, u32[]{:S(2)}) collective-permute-start(bf16[2,4,32,128]{3,2,1,0:T(8,128)(2,1)S(1)} %pad_maximum_fusion.2), channel_id=1, source_target_pairs={{0,2},{1,3},{2,0},{3,1},{4,6},{5,7},{6,4},{7,5},{8,10},{9,11},{10,... | collective-permute-start | bytes 196616 | tf_op jit(solution)/shard_map/ppermute | solution.py:295

commit v3 on v2

--- a/solution.py
+++ b/solution.py
@@ -16,16 +16,23 @@
     return pltpu.with_memory_space_constraint(value, pltpu.VMEM)
 
 
+def in_hbm(value):
+    return pltpu.with_memory_space_constraint(value, pltpu.HBM)
+
+
 def first_product(block_rows, block_cols, counts, start, tiles, row_blocks, cut):
     slots, size, _ = tiles.shape
     col_blocks, rank = start.shape[0] // size, start.shape[1]
     width = rank // 8
 
-    def body(rows_ref, cols_ref, count_ref, start_hbm, tile_hbm, keep_ref, send_ref, head_ref, tail_ref, start_ref, flipped, acc, sems):
+    def body(rows_hbm, cols_hbm, count_ref, start_hbm, tile_hbm, keep_ref, send_ref, head_ref, tail_ref, start_ref,
+             flipped, acc, rows_ref, cols_ref, sems):
         copies = [
             pltpu.make_async_copy(start_hbm, start_ref, sems.at[0]),
             pltpu.make_async_copy(tile_hbm.at[pl.ds(0, cut)], head_ref, sems.at[1]),
             pltpu.make_async_copy(tile_hbm.at[pl.ds(cut, slots - cut)], tail_ref, sems.at[2]),
+            pltpu.make_async_copy(rows_hbm, rows_ref, sems.at[3]),
+            pltpu.make_async_copy(cols_hbm, cols_ref, sems.at[4]),
         ]
         for copy in copies:
             copy.start()
@@ -33,8 +40,8 @@
         copies[0].wait()
         for c in range(col_blocks):
             flipped[c] = start_ref[c * size:(c + 1) * size, :].T
-        copies[1].wait()
-        copies[2].wait()
+        for copy in copies[1:]:
+            copy.wait()
         count = count_ref[0, 0]
         for s in range(slots):
             to = jnp.where(s < count, rows_ref[0, s], row_blocks)
@@ -51,24 +58,25 @@
                     first = pl.multiple_of((at + mine) * width, width)
                     ref[2 * dx + dz] = acc[0:row_blocks, pl.ds(first, width), :].astype(BF)
 
-    smem = pl.BlockSpec(memory_space=pltpu.SMEM)
     hbm = pl.BlockSpec(memory_space=pltpu.HBM)
     vmem = pl.BlockSpec(memory_space=pltpu.VMEM)
     return pl.pallas_call(
         body,
         out_shape=[pltpu.VMEM((4, row_blocks, width, size), BF)] * 2
         + [pltpu.VMEM((n, size, size), BF) for n in (cut, slots - cut)],
-        in_specs=[smem, smem, smem, hbm, hbm],
+        in_specs=[hbm, hbm, pl.BlockSpec(memory_space=pltpu.SMEM), hbm, hbm],
         out_specs=[vmem] * 4,
         scratch_shapes=[
             pltpu.VMEM(start.shape, BF),
             pltpu.VMEM((col_blocks, rank, size), BF),
             pltpu.VMEM((row_blocks + 1, rank, size), F32),
-            pltpu.SemaphoreType.DMA((3,)),
+            pltpu.SMEM(block_rows.shape, jnp.int32),
+            pltpu.SMEM(block_cols.shape, jnp.int32),
+            pltpu.SemaphoreType.DMA((5,)),
         ],
         compiler_params=pltpu.CompilerParams(vmem_limit_bytes=12 * 1024 * 1024),
         name="first",
-    )(block_rows, block_cols, counts, *[pltpu.with_memory_space_constraint(v, pltpu.HBM) for v in (start, tiles)])
+    )(in_hbm(block_rows), in_hbm(block_cols), counts, in_hbm(start), in_hbm(tiles))
 
 
 def flip_blocks(tiles):

time: 109 us -> 107 us (0.982)
  local copies, waits for them, and re-layouts: 1.39 us -> 0.09 us
    unnamed x4 -> x0, local copies, waits for them, and re-layouts: 1.31 us -> none
where the time goes in v3:
time: 107 us
  waiting for transfers between devices  50.2 us (47%)
  starting transfers between devices  36.2 us (34%)
  Pallas kernels  16.7 us (16%)
  other arithmetic  2.02 us (2%)
  between operations  1.57 us (1%)
    ppermute x28, waiting for transfers between devices, send(): lax.ppermute(value, ('row', 'col'), [(r * n_col + c, (r ^ dx) * n_col + (...  27.3 us
    ppermute x28, starting transfers between devices, send(): lax.ppermute(value, ('row', 'col'), [(r * n_col + c, (r ^ dx) * n_col + (...  26.1 us
    ppermute x4, waiting for transfers between devices, others_z(): lax.ppermute(value, 'col', [(c, (c + 4 * k) % n_col) for c in range(n_col)])  16 us
    pallas_call x6, Pallas kernels, block_product(): pl.pallas_call(body, out_shape=out_shape, in_specs=[pl.BlockSpec(memory_s...  11.9 us
    ppermute x4, waiting for transfers between devices, others_row(): lax.ppermute(value, 'row', [(r, (r + 2 * k) % n_row) for r in range(n_row)])  6.92 us
    ppermute x4, starting transfers between devices, others_z(): lax.ppermute(value, 'col', [(c, (c + 4 * k) % n_col) for c in range(n_col)])  5.69 us
    ppermute x4, starting transfers between devices, others_row(): lax.ppermute(value, 'row', [(r, (r + 2 * k) % n_row) for r in range(n_row)])  4.35 us
  transfers between devices with their start and end apart: 37, of which 16 were waited for; matrix products, arithmetic and copies ran while one was open for 2% of the time, Pallas kernels for 12%

profile of v3, /device:TPU:0, one launch (start us, length us, event | category | flops | bytes accessed | tf_op | source)
XLA Modules:
  0.0 106.8 jit_solution(15844559170869225746)
XLA Ops:
  1.3 1.9 %first.1 = (bf16[4,16,32,128]{3,2,1,0:T(8,128)(2,1)S(1)}, bf16[4,16,32,128]{3,2,1,0:T(8,128)(2,1)S(1)}, bf16[10,128,128]{2,1,0:T(8,128)(2,1)S(1)}, bf16[10,128,128]{2,1,0:T(8,128)(2,1)S(1)}) custom-call(s32[1,20]{1,0:T(1,128)} %rows_hbm.1, s32[1,20]{1,0:T(1,128)} %cols_hbm.1, s32[1,1]{1,0:T(1,128)} %copy.11.count_ref, bf16[1024,256]{1,0:T(8,128)(2,1)} %start_hbm.1, ...), custom_call_target="tpu_custom_call" | custom-call | tf_op jit(solution)/shard_map/first/pallas_call | solution.py:63
  3.2 0.6 collective-permute-start.20
  3.8 2.6 %collective-permute-start.12 = (bf16[10,128,128]{2,1,0:T(8,128)(2,1)S(1)}, bf16[10,128,128]{2,1,0:T(8,128)(2,1)S(1)}, u32[]{:S(2)}, u32[]{:S(2)}) collective-permute-start(bf16[10,128,128]{2,1,0:T(8,128)(2,1)S(1)} %get-tuple-element.23.refs_2_.refs_5_), channel_id=1, source_target_pairs={{0,2},{1,3},{2,0},{3,1},{4,6},{5,7},{6,4},{7,5},{8,10},{9,11},{10,... | collective-permute-start | bytes 983048 | tf_op jit(solution)/shard_map/ppermute | solution.py:303
  6.4 1.5 %collective-permute-start.8 = (bf16[10,128,128]{2,1,0:T(8,128)(2,1)S(1)}, bf16[10,128,128]{2,1,0:T(8,128)(2,1)S(1)}, u32[]{:S(2)}, u32[]{:S(2)}) collective-permute-start(bf16[10,128,128]{2,1,0:T(8,128)(2,1)S(1)} %get-tuple-element.23.refs_2_.refs_5_), channel_id=1, source_target_pairs={{0,8},{1,9},{2,10},{3,11},{4,12},{5,13},{6,14},{7,15},{8,0},{9,1},... | collective-permute-start | bytes 983048 | tf_op jit(solution)/shard_map/ppermute | solution.py:303
  7.9 0.7 compare_select_fusion
  8.7 0.5 collective-permute-start.21
  9.2 0.7 fusion.9
  9.9 1.2 %collective-permute-done = s32[2,20]{1,0:T(2,128)S(1)} collective-permute-done((s32[2,20]{1,0:T(2,128)S(1)}, s32[2,20]{1,0:T(2,128)S(1)}, u32[]{:S(2)}, u32[]{:S(2)}) %collective-permute-start) | collective-permute-done | bytes 192 | tf_op jit(solution)/shard_map/ppermute | solution.py:303
  11.1 0.7 collective-permute-start.1
  11.8 1.4 %collective-permute-start.10 = (bf16[10,128,128]{2,1,0:T(8,128)(2,1)S(1)}, bf16[10,128,128]{2,1,0:T(8,128)(2,1)S(1)}, u32[]{:S(2)}, u32[]{:S(2)}) collective-permute-start(bf16[10,128,128]{2,1,0:T(8,128)(2,1)S(1)} %get-tuple-element.22.refs_0_.refs_3_), channel_id=1, source_target_pairs={{0,2},{1,3},{2,0},{3,1},{4,6},{5,7},{6,4},{7,5},{8,10},{9,11},{10,... | collective-permute-start | bytes 983048 | tf_op jit(solution)/shard_map/ppermute | solution.py:303
  13.2 3.0 %collective-permute-done.1.refs_1_ = s32[2,2,20]{2,1,0:T(2,128)S(1)} collective-permute-done((s32[2,2,20]{2,1,0:T(2,128)S(1)}, s32[2,2,20]{2,1,0:T(2,128)S(1)}, u32[]{:S(2)}, u32[]{:S(2)}) %collective-permute-start.1) | collective-permute-done | bytes 352 | tf_op jit(solution)/shard_map/ppermute | solution.py:303
  16.2 1.5 %collective-permute-start.6 = (bf16[10,128,128]{2,1,0:T(8,128)(2,1)S(1)}, bf16[10,128,128]{2,1,0:T(8,128)(2,1)S(1)}, u32[]{:S(2)}, u32[]{:S(2)}) collective-permute-start(bf16[10,128,128]{2,1,0:T(8,128)(2,1)S(1)} %get-tuple-element.22.refs_0_.refs_3_), channel_id=1, source_target_pairs={{0,8},{1,9},{2,10},{3,11},{4,12},{5,13},{6,14},{7,15},{8,0},{9,1},... | collective-permute-start | bytes 983048 | tf_op jit(solution)/shard_map/ppermute | solution.py:303
  18.3 2.3 %collective-permute-done.21 = bf16[2,16,32,128]{3,2,1,0:T(8,128)(2,1)S(1)} collective-permute-done((bf16[2,16,32,128]{3,2,1,0:T(8,128)(2,1)S(1)}, bf16[2,16,32,128]{3,2,1,0:T(8,128)(2,1)S(1)}, u32[]{:S(2)}, u32[]{:S(2)}) %collective-permute-start.21) | collective-permute-done | bytes 262176 | tf_op jit(solution)/shard_map/ppermute | solution.py:303
  20.6 2.0 %collective-permute-start.2 = (s32[2,2,20]{2,1,0:T(2,128)S(1)}, s32[2,2,20]{2,1,0:T(2,128)S(1)}, u32[]{:S(2)}, u32[]{:S(2)}) collective-permute-start(s32[2,2,20]{2,1,0:T(2,128)S(1)} %pad_add_fusion.refs_0_), channel_id=1, source_target_pairs={{0,2},{1,3},{2,0},{3,1},{4,6},{5,7},{6,4},{7,5},{8,10},{9,11},{10,... | collective-permute-start | bytes 968 | tf_op jit(solution)/shard_map/ppermute | solution.py:303
  22.7 4.7 %collective-permute-done.2.refs_2_ = s32[2,2,20]{2,1,0:T(2,128)S(1)} collective-permute-done((s32[2,2,20]{2,1,0:T(2,128)S(1)}, s32[2,2,20]{2,1,0:T(2,128)S(1)}, u32[]{:S(2)}, u32[]{:S(2)}) %collective-permute-start.2) | collective-permute-done | bytes 352 | tf_op jit(solution)/shard_map/ppermute | solution.py:303
  27.4 1.7 %collective-permute-start.16 = (bf16[6,128,128]{2,1,0:T(8,128)(2,1)S(1)}, bf16[6,128,128]{2,1,0:T(8,128)(2,1)S(1)}, u32[]{:S(2)}, u32[]{:S(2)}) collective-permute-start(bf16[6,128,128]{2,1,0:T(8,128)(2,1)S(1)} %slice.56), channel_id=1, source_target_pairs={{0,8},{1,9},{2,10},{3,11},{4,12},{5,13},{6,14},{7,15},{8,0},{9,1},... | collective-permute-start | bytes 589832 | tf_op jit(solution)/shard_map/ppermute | solution.py:303
  29.1 1.6 %collective-permute-start.18 = (bf16[4,128,128]{2,1,0:T(8,128)(2,1)S(1)}, bf16[4,128,128]{2,1,0:T(8,128)(2,1)S(1)}, u32[]{:S(2)}, u32[]{:S(2)}) collective-permute-start(bf16[4,128,128]{2,1,0:T(8,128)(2,1)S(1)} %slice.57), channel_id=1, source_target_pairs={{0,2},{1,3},{2,0},{3,1},{4,6},{5,7},{6,4},{7,5},{8,10},{9,11},{10,... | collective-permute-start | bytes 393224 | tf_op jit(solution)/shard_map/ppermute | solution.py:303
  31.1 0.5 collective-permute-start.14
  31.7 2.3 %collective-permute-done.18.refs_16_.refs_5_ = bf16[4,128,128]{2,1,0:T(8,128)(2,1)S(1)} collective-permute-done((bf16[4,128,128]{2,1,0:T(8,128)(2,1)S(1)}, bf16[4,128,128]{2,1,0:T(8,128)(2,1)S(1)}, u32[]{:S(2)}, u32[]{:S(2)}) %collective-permute-start.18) | collective-permute-done | bytes 131104 | tf_op jit(solution)/shard_map/ppermute | solution.py:303
  34.4 7.3 %collective-permute-done.14.refs_12_.refs_1_ = bf16[10,128,128]{2,1,0:T(8,128)(2,1)S(1)} collective-permute-done((bf16[10,128,128]{2,1,0:T(8,128)(2,1)S(1)}, bf16[10,128,128]{2,1,0:T(8,128)(2,1)S(1)}, u32[]{:S(2)}, u32[]{:S(2)}) %collective-permute-start.14) | collective-permute-done | bytes 327712 | tf_op jit(solution)/shard_map/ppermute | solution.py:303
  41.7 2.1 %collective-permute-done.22 = bf16[16,32,128]{2,1,0:T(8,128)(2,1)S(1)} collective-permute-done((bf16[16,32,128]{2,1,0:T(8,128)(2,1)S(1)}, bf16[16,32,128]{2,1,0:T(8,128)(2,1)S(1)}, u32[]{:S(2)}, u32[]{:S(2)}) %collective-permute-start.22) | collective-permute-done | bytes 131104 | tf_op jit(solution)/shard_map/ppermute | solution.py:303
  43.9 2.5 %collective-permute-start.23 = (bf16[32,32,128]{2,1,0:T(8,128)(2,1)S(1)}, bf16[32,32,128]{2,1,0:T(8,128)(2,1)S(1)}, u32[]{:S(2)}, u32[]{:S(2)}) collective-permute-start(bf16[32,32,128]{2,1,0:T(8,128)(2,1)S(1)} %pad_maximum_fusion.refs_15_.refs_7_), channel_id=1, source_target_pairs={{0,4},{1,5},{2,6},{3,7},{4,0},{5,1},{6,2},{7,3},{8,12},{9,13},{10,... | collective-permute-start | bytes 786440 | tf_op jit(solution)/shard_map/ppermute | solution.py:309
  47.0 2.5 %collective-permute-start.3 = (s32[2,2,20]{2,1,0:T(2,128)S(1)}, s32[2,2,20]{2,1,0:T(2,128)S(1)}, u32[]{:S(2)}, u32[]{:S(2)}) collective-permute-start(s32[2,2,20]{2,1,0:T(2,128)S(1)} %pad_add_fusion.refs_0_), channel_id=1, source_target_pairs={{0,10},{1,11},{2,8},{3,9},{4,14},{5,15},{6,12},{7,13},{8,2},{9,3},... | collective-permute-start | bytes 968 | tf_op jit(solution)/shard_map/ppermute | solution.py:303
  49.5 9.7 %collective-permute-done.23.refs_16_.refs_8_ = bf16[32,32,128]{2,1,0:T(8,128)(2,1)S(1)} collective-permute-done((bf16[32,32,128]{2,1,0:T(8,128)(2,1)S(1)}, bf16[32,32,128]{2,1,0:T(8,128)(2,1)S(1)}, u32[]{:S(2)}, u32[]{:S(2)}) %collective-permute-start.23) | collective-permute-done | bytes 262176 | tf_op jit(solution)/shard_map/ppermute | solution.py:309
  59.2 1.8 %product.6.refs_9_ = f32[33,32,128]{2,1,0:T(8,128)S(1)} custom-call(s32[2,2,20]{2,1,0:T(2,128)S(1)} %pad_add_fusion.refs_0_, s32[2,2,20]{2,1,0:T(2,128)S(1)} %collective-permute-done.1.refs_1_, s32[2,2,20]{2,1,0:T(2,128)S(1)} %collective-permute-done.2.refs_2_, bf16[10,128,128]{2,1,0:T(8,128)(2,1)S(1)} %get-tuple-element.22.refs_0_.refs_3_, ...), custom_call_target="tpu_custom_call" | custom-call | tf_op jit(solution)/shard_map/product/pallas_call | solution.py:198
  61.1 1.1 %product.7 = (bf16[32,16,128]{2,1,0:T(8,128)(2,1)S(1)}, bf16[32,16,128]{2,1,0:T(8,128)(2,1)S(1)}) custom-call(s32[2,2,20]{2,1,0:T(2,128)S(1)} %collective-permute-done.3.refs_0_.refs_3_, bf16[10,128,128]{2,1,0:T(8,128)(2,1)S(1)} %collective-permute-done.14.refs_12_.refs_1_, bf16[10,128,128]{2,1,0:T(8,128)(2,1)S(1)} %collective-permute-done.15.refs_13_.refs_2_, ...), custom_call_target="tpu_custom_call" | custom-call | tf_op jit(solution)/shard_map/product/pallas_call | solution.py:198
  62.2 1.5 %collective-permute-start.26 = (bf16[32,16,128]{2,1,0:T(8,128)(2,1)S(1)}, bf16[32,16,128]{2,1,0:T(8,128)(2,1)S(1)}, u32[]{:S(2)}, u32[]{:S(2)}) collective-permute-start(bf16[32,16,128]{2,1,0:T(8,128)(2,1)S(1)} %get-tuple-element.27.refs_5_), channel_id=1, source_target_pairs={{0,16},{8,24},{16,0},{24,8},{1,17},{9,25},{17,1},{25,9},{2,18},{10... | collective-permute-start | bytes 393224 | tf_op jit(solution)/shard_map/ppermute | solution.py:315
  63.7 0.6 collective-permute-start.24
  64.3 1.8 %flip.1.refs_4_ = bf16[320,128,128]{2,1,0:T(8,128)(2,1)S(1)} custom-call(bf16[10,128,128]{2,1,0:T(8,128)(2,1)S(1)} %get-tuple-element.22.refs_0_.refs_3_, bf16[10,128,128]{2,1,0:T(8,128)(2,1)S(1)} %collective-permute-done.4.refs_1_.refs_4_, bf16[10,128,128]{2,1,0:T(8,128)(2,1)S(1)} %get-tuple-element.23.refs_2_.refs_5_, ...), custom_call_target="tpu_custom_call" | custom-call | tf_op jit(solution)/shard_map/flip/pallas_call | solution.py:102
  66.1 2.5 %collective-permute-done.26.refs_6_ = bf16[32,16,128]{2,1,0:T(8,128)(2,1)S(1)} collective-permute-done((bf16[32,16,128]{2,1,0:T(8,128)(2,1)S(1)}, bf16[32,16,128]{2,1,0:T(8,128)(2,1)S(1)}, u32[]{:S(2)}, u32[]{:S(2)}) %collective-permute-start.26) | collective-permute-done | bytes 131104 | tf_op jit(solution)/shard_map/ppermute | solution.py:315
  68.7 2.2 %product.10.refs_5_ = bf16[33,16,128]{2,1,0:T(8,128)(2,1)S(1)} custom-call(s32[2,2,20]{2,1,0:T(2,128)S(1)} %pad_add_fusion.refs_0_, s32[2,2,20]{2,1,0:T(2,128)S(1)} %collective-permute-done.1.refs_1_, s32[2,2,20]{2,1,0:T(2,128)S(1)} %collective-permute-done.2.refs_2_, s32[2,2,20]{2,1,0:T(2,128)S(1)} %collective-permute-done.3.refs_0_.refs_3_, ...), custom_call_target="tpu_custom_call" | custom-call | tf_op jit(solution)/shard_map/product/pallas_call | solution.py:198
  71.0 2.2 %product.8.refs_5_ = bf16[33,16,128]{2,1,0:T(8,128)(2,1)S(1)} custom-call(s32[2,2,20]{2,1,0:T(2,128)S(1)} %pad_add_fusion.refs_0_, s32[2,2,20]{2,1,0:T(2,128)S(1)} %collective-permute-done.1.refs_1_, s32[2,2,20]{2,1,0:T(2,128)S(1)} %collective-permute-done.2.refs_2_, s32[2,2,20]{2,1,0:T(2,128)S(1)} %collective-permute-done.3.refs_0_.refs_3_, ...), custom_call_target="tpu_custom_call" | custom-call | tf_op jit(solution)/shard_map/product/pallas_call | solution.py:198
  73.2 3.0 %collective-permute-start.25 = (bf16[33,16,128]{2,1,0:T(8,128)(2,1)S(1)}, bf16[33,16,128]{2,1,0:T(8,128)(2,1)S(1)}, u32[]{:S(2)}, u32[]{:S(2)}) collective-permute-start(bf16[33,16,128]{2,1,0:T(8,128)(2,1)S(1)} %product.8.refs_5_), channel_id=1, source_target_pairs={{0,4},{1,5},{2,6},{3,7},{4,0},{5,1},{6,2},{7,3},{8,12},{9,13},{10,... | collective-permute-start | bytes 405512 | tf_op jit(solution)/shard_map/ppermute | solution.py:309
  76.2 4.5 %collective-permute-done.27.refs_6_ = bf16[33,16,128]{2,1,0:T(8,128)(2,1)S(1)} collective-permute-done((bf16[33,16,128]{2,1,0:T(8,128)(2,1)S(1)}, bf16[33,16,128]{2,1,0:T(8,128)(2,1)S(1)}, u32[]{:S(2)}, u32[]{:S(2)}) %collective-permute-start.27) | collective-permute-done | bytes 135200 | tf_op jit(solution)/shard_map/ppermute | solution.py:309
  80.8 2.2 %product.11 = (bf16[32,16,128]{2,1,0:T(8,128)(2,1)S(1)}, bf16[32,16,128]{2,1,0:T(8,128)(2,1)S(1)}) custom-call(s32[2,2,20]{2,1,0:T(2,128)S(1)} %pad_add_fusion.refs_0_, s32[2,2,20]{2,1,0:T(2,128)S(1)} %collective-permute-done.1.refs_1_, s32[2,2,20]{2,1,0:T(2,128)S(1)} %collective-permute-done.2.refs_2_, ...), custom_call_target="tpu_custom_call" | custom-call | tf_op jit(solution)/shard_map/product/pallas_call | solution.py:198
  83.0 1.6 %collective-permute-start.29 = (bf16[32,16,128]{2,1,0:T(8,128)(2,1)S(1)}, bf16[32,16,128]{2,1,0:T(8,128)(2,1)S(1)}, u32[]{:S(2)}, u32[]{:S(2)}) collective-permute-start(bf16[32,16,128]{2,1,0:T(8,128)(2,1)S(1)} %get-tuple-element.30.refs_4_), channel_id=1, source_target_pairs={{0,16},{8,24},{16,0},{24,8},{1,17},{9,25},{17,1},{25,9},{2,18},{10... | collective-permute-start | bytes 393224 | tf_op jit(solution)/shard_map/ppermute | solution.py:315
  84.7 2.2 %product.9 = (bf16[32,16,128]{2,1,0:T(8,128)(2,1)S(1)}, bf16[32,16,128]{2,1,0:T(8,128)(2,1)S(1)}) custom-call(s32[2,2,20]{2,1,0:T(2,128)S(1)} %pad_add_fusion.refs_0_, s32[2,2,20]{2,1,0:T(2,128)S(1)} %collective-permute-done.1.refs_1_, s32[2,2,20]{2,1,0:T(2,128)S(1)} %collective-permute-done.2.refs_2_, ...), custom_call_target="tpu_custom_call" | custom-call | tf_op jit(solution)/shard_map/product/pallas_call | solution.py:198
  86.9 0.6 collective-permute-start.28
  87.6 0.6 collective-permute-done.29.refs_5_
  88.2 3.8 %collective-permute-done.28.refs_3_ = bf16[32,16,128]{2,1,0:T(8,128)(2,1)S(1)} collective-permute-done((bf16[32,16,128]{2,1,0:T(8,128)(2,1)S(1)}, bf16[32,16,128]{2,1,0:T(8,128)(2,1)S(1)}, u32[]{:S(2)}, u32[]{:S(2)}) %collective-permute-start.28) | collective-permute-done | bytes 131104 | tf_op jit(solution)/shard_map/ppermute | solution.py:315
  92.3 2.9 %collective-permute-start.33 = (f32[32,128]{1,0:T(8,128)S(1)}, f32[32,128]{1,0:T(8,128)S(1)}, u32[]{:S(2)}, u32[]{:S(2)}) collective-permute-start(f32[32,128]{1,0:T(8,128)S(1)} %get-tuple-element.32), channel_id=1, source_target_pairs={{0,1},{1,0},{2,3},{3,2},{4,5},{5,4},{6,7},{7,6},{8,9},{9,8},{10,11... | collective-permute-start | bytes 49160 | tf_op jit(solution)/shard_map/ppermute | solution.py:303
  95.3 1.7 %collective-permute-done.30 = f32[32,128]{1,0:T(8,128)S(1)} collective-permute-done((f32[32,128]{1,0:T(8,128)S(1)}, f32[32,128]{1,0:T(8,128)S(1)}, u32[]{:S(2)}, u32[]{:S(2)}) %collective-permute-start.30) | collective-permute-done | bytes 16416 | tf_op jit(solution)/shard_map/ppermute | solution.py:309
  97.5 3.4 %collective-permute-start.36 = (bf16[2,4,32,128]{3,2,1,0:T(8,128)(2,1)S(1)}, bf16[2,4,32,128]{3,2,1,0:T(8,128)(2,1)S(1)}, u32[]{:S(2)}, u32[]{:S(2)}) collective-permute-start(bf16[2,4,32,128]{3,2,1,0:T(8,128)(2,1)S(1)} %pad_maximum_fusion.4), channel_id=1, source_target_pairs={{0,10},{1,11},{2,8},{3,9},{4,14},{5,15},{6,12},{7,13},{8,2},{9,3},... | collective-permute-start | bytes 196616 | tf_op jit(solution)/shard_map/ppermute | solution.py:303
  101.0 0.6 collective-permute-start.35
  101.7 1.7 %collective-permute-done.36.refs_3_ = bf16[2,4,32,128]{3,2,1,0:T(8,128)(2,1)S(1)} collective-permute-done((bf16[2,4,32,128]{3,2,1,0:T(8,128)(2,1)S(1)}, bf16[2,4,32,128]{3,2,1,0:T(8,128)(2,1)S(1)}, u32[]{:S(2)}, u32[]{:S(2)}) %collective-permute-start.36) | collective-permute-done | bytes 65568 | tf_op jit(solution)/shard_map/ppermute | solution.py:303
  103.4 1.9 %collective-permute-done.35.refs_2_ = bf16[2,4,32,128]{3,2,1,0:T(8,128)(2,1)S(1)} collective-permute-done((bf16[2,4,32,128]{3,2,1,0:T(8,128)(2,1)S(1)}, bf16[2,4,32,128]{3,2,1,0:T(8,128)(2,1)S(1)}, u32[]{:S(2)}, u32[]{:S(2)}) %collective-permute-start.35) | collective-permute-done | bytes 65568 | tf_op jit(solution)/shard_map/ppermute | solution.py:303
  105.3 0.6 collective-permute-done.34.refs_1_
  105.9 0.8 assemble.1
  (60 shorter events, 3.3 us)
Async XLA Ops:
  3.2 5.3 %collective-permute-start.20 = (bf16[4,16,32,128]{3,2,1,0:T(8,128)(2,1)S(1)}, bf16[4,16,32,128]{3,2,1,0:T(8,128)(2,1)S(1)}, u32[]{:S(2)}, u32[]{:S(2)}) collective-permute-start(bf16[4,16,32,128]{3,2,1,0:T(8,128)(2,1)S(1)} %get-tuple-element.18), channel_id=1, source_target_pairs={{0,1},{1,0},{2,3},{3,2},{4,5},{5,4},{6,7},{7,6},{8,9},{9,8},{10,11... | collective-permute-start | bytes 1572872 | tf_op jit(solution)/shard_map/ppermute | solution.py:303
  3.8 13.9 %collective-permute-start.12 = (bf16[10,128,128]{2,1,0:T(8,128)(2,1)S(1)}, bf16[10,128,128]{2,1,0:T(8,128)(2,1)S(1)}, u32[]{:S(2)}, u32[]{:S(2)}) collective-permute-start(bf16[10,128,128]{2,1,0:T(8,128)(2,1)S(1)} %get-tuple-element.23.refs_2_.refs_5_), channel_id=1, source_target_pairs={{0,2},{1,3},{2,0},{3,1},{4,6},{5,7},{6,4},{7,5},{8,10},{9,11},{10,... | collective-permute-start | bytes 983048 | tf_op jit(solution)/shard_map/ppermute | solution.py:303
  6.4 11.3 %collective-permute-start.8 = (bf16[10,128,128]{2,1,0:T(8,128)(2,1)S(1)}, bf16[10,128,128]{2,1,0:T(8,128)(2,1)S(1)}, u32[]{:S(2)}, u32[]{:S(2)}) collective-permute-start(bf16[10,128,128]{2,1,0:T(8,128)(2,1)S(1)} %get-tuple-element.23.refs_2_.refs_5_), channel_id=1, source_target_pairs={{0,8},{1,9},{2,10},{3,11},{4,12},{5,13},{6,14},{7,15},{8,0},{9,1},... | collective-permute-start | bytes 983048 | tf_op jit(solution)/shard_map/ppermute | solution.py:303
  8.7 11.8 %collective-permute-start.21 = (bf16[2,16,32,128]{3,2,1,0:T(8,128)(2,1)S(1)}, bf16[2,16,32,128]{3,2,1,0:T(8,128)(2,1)S(1)}, u32[]{:S(2)}, u32[]{:S(2)}) collective-permute-start(bf16[2,16,32,128]{3,2,1,0:T(8,128)(2,1)S(1)} %slice_bitcast_fusion), channel_id=1, source_target_pairs={{0,2},{1,3},{2,0},{3,1},{4,6},{5,7},{6,4},{7,5},{8,10},{9,11},{10,... | collective-permute-start | bytes 786440 | tf_op jit(solution)/shard_map/ppermute | solution.py:303
  9.9 1.2 %collective-permute-start = (s32[2,20]{1,0:T(2,128)S(1)}, s32[2,20]{1,0:T(2,128)S(1)}, u32[]{:S(2)}, u32[]{:S(2)}) collective-permute-start(s32[2,20]{1,0:T(2,128)S(1)} %get-tuple-element.45), channel_id=1, source_target_pairs={{0,1},{1,0},{2,3},{3,2},{4,5},{5,4},{6,7},{7,6},{8,9},{9,8},{10,11... | collective-permute-start | bytes 488 | tf_op jit(solution)/shard_map/ppermute | solution.py:303
  11.1 5.1 %collective-permute-start.1 = (s32[2,2,20]{2,1,0:T(2,128)S(1)}, s32[2,2,20]{2,1,0:T(2,128)S(1)}, u32[]{:S(2)}, u32[]{:S(2)}) collective-permute-start(s32[2,2,20]{2,1,0:T(2,128)S(1)} %pad_add_fusion.refs_0_), channel_id=1, source_target_pairs={{0,8},{1,9},{2,10},{3,11},{4,12},{5,13},{6,14},{7,15},{8,0},{9,1},... | collective-permute-start | bytes 968 | tf_op jit(solution)/shard_map/ppermute | solution.py:303
  11.8 17.3 %collective-permute-start.10 = (bf16[10,128,128]{2,1,0:T(8,128)(2,1)S(1)}, bf16[10,128,128]{2,1,0:T(8,128)(2,1)S(1)}, u32[]{:S(2)}, u32[]{:S(2)}) collective-permute-start(bf16[10,128,128]{2,1,0:T(8,128)(2,1)S(1)} %get-tuple-element.22.refs_0_.refs_3_), channel_id=1, source_target_pairs={{0,2},{1,3},{2,0},{3,1},{4,6},{5,7},{6,4},{7,5},{8,10},{9,11},{10,... | collective-permute-start | bytes 983048 | tf_op jit(solution)/shard_map/ppermute | solution.py:303
  16.2 14.4 %collective-permute-start.6 = (bf16[10,128,128]{2,1,0:T(8,128)(2,1)S(1)}, bf16[10,128,128]{2,1,0:T(8,128)(2,1)S(1)}, u32[]{:S(2)}, u32[]{:S(2)}) collective-permute-start(bf16[10,128,128]{2,1,0:T(8,128)(2,1)S(1)} %get-tuple-element.22.refs_0_.refs_3_), channel_id=1, source_target_pairs={{0,8},{1,9},{2,10},{3,11},{4,12},{5,13},{6,14},{7,15},{8,0},{9,1},... | collective-permute-start | bytes 983048 | tf_op jit(solution)/shard_map/ppermute | solution.py:303
  17.7 12.9 %collective-permute-start.4 = (bf16[10,128,128]{2,1,0:T(8,128)(2,1)S(1)}, bf16[10,128,128]{2,1,0:T(8,128)(2,1)S(1)}, u32[]{:S(2)}, u32[]{:S(2)}) collective-permute-start(bf16[10,128,128]{2,1,0:T(8,128)(2,1)S(1)} %get-tuple-element.22.refs_0_.refs_3_), channel_id=1, source_target_pairs={{0,1},{1,0},{2,3},{3,2},{4,5},{5,4},{6,7},{7,6},{8,9},{9,8},{10,11... | collective-permute-start | bytes 983048 | tf_op jit(solution)/shard_map/ppermute | solution.py:303
  17.7 13.4 %collective-permute-start.5 = (bf16[10,128,128]{2,1,0:T(8,128)(2,1)S(1)}, bf16[10,128,128]{2,1,0:T(8,128)(2,1)S(1)}, u32[]{:S(2)}, u32[]{:S(2)}) collective-permute-start(bf16[10,128,128]{2,1,0:T(8,128)(2,1)S(1)} %get-tuple-element.23.refs_2_.refs_5_), channel_id=1, source_target_pairs={{0,1},{1,0},{2,3},{3,2},{4,5},{5,4},{6,7},{7,6},{8,9},{9,8},{10,11... | collective-permute-start | bytes 983048 | tf_op jit(solution)/shard_map/ppermute | solution.py:303
  20.6 6.8 %collective-permute-start.2 = (s32[2,2,20]{2,1,0:T(2,128)S(1)}, s32[2,2,20]{2,1,0:T(2,128)S(1)}, u32[]{:S(2)}, u32[]{:S(2)}) collective-permute-start(s32[2,2,20]{2,1,0:T(2,128)S(1)} %pad_add_fusion.refs_0_), channel_id=1, source_target_pairs={{0,2},{1,3},{2,0},{3,1},{4,6},{5,7},{6,4},{7,5},{8,10},{9,11},{10,... | collective-permute-start | bytes 968 | tf_op jit(solution)/shard_map/ppermute | solution.py:303
  27.4 7.0 %collective-permute-start.16 = (bf16[6,128,128]{2,1,0:T(8,128)(2,1)S(1)}, bf16[6,128,128]{2,1,0:T(8,128)(2,1)S(1)}, u32[]{:S(2)}, u32[]{:S(2)}) collective-permute-start(bf16[6,128,128]{2,1,0:T(8,128)(2,1)S(1)} %slice.56), channel_id=1, source_target_pairs={{0,8},{1,9},{2,10},{3,11},{4,12},{5,13},{6,14},{7,15},{8,0},{9,1},... | collective-permute-start | bytes 589832 | tf_op jit(solution)/shard_map/ppermute | solution.py:303
  29.1 5.0 %collective-permute-start.18 = (bf16[4,128,128]{2,1,0:T(8,128)(2,1)S(1)}, bf16[4,128,128]{2,1,0:T(8,128)(2,1)S(1)}, u32[]{:S(2)}, u32[]{:S(2)}) collective-permute-start(bf16[4,128,128]{2,1,0:T(8,128)(2,1)S(1)} %slice.57), channel_id=1, source_target_pairs={{0,2},{1,3},{2,0},{3,1},{4,6},{5,7},{6,4},{7,5},{8,10},{9,11},{10,... | collective-permute-start | bytes 393224 | tf_op jit(solution)/shard_map/ppermute | solution.py:303
  30.6 15.8 %collective-permute-start.13 = (bf16[10,128,128]{2,1,0:T(8,128)(2,1)S(1)}, bf16[10,128,128]{2,1,0:T(8,128)(2,1)S(1)}, u32[]{:S(2)}, u32[]{:S(2)}) collective-permute-start(bf16[10,128,128]{2,1,0:T(8,128)(2,1)S(1)} %collective-permute-done.12.refs_10_.refs_13_), channel_id=1, source_target_pairs={{0,1},{1,0},{2,3},{3,2},{4,5},{5,4},{6,7},{7,6},{8,9},{9,8},{10,11... | collective-permute-start | bytes 983048 | tf_op jit(solution)/shard_map/ppermute | solution.py:303
  30.6 13.3 %collective-permute-start.11 = (bf16[10,128,128]{2,1,0:T(8,128)(2,1)S(1)}, bf16[10,128,128]{2,1,0:T(8,128)(2,1)S(1)}, u32[]{:S(2)}, u32[]{:S(2)}) collective-permute-start(bf16[10,128,128]{2,1,0:T(8,128)(2,1)S(1)} %collective-permute-done.10.refs_8_.refs_11_), channel_id=1, source_target_pairs={{0,1},{1,0},{2,3},{3,2},{4,5},{5,4},{6,7},{7,6},{8,9},{9,8},{10,11... | collective-permute-start | bytes 983048 | tf_op jit(solution)/shard_map/ppermute | solution.py:303
  31.1 10.6 %collective-permute-start.14 = (bf16[10,128,128]{2,1,0:T(8,128)(2,1)S(1)}, bf16[10,128,128]{2,1,0:T(8,128)(2,1)S(1)}, u32[]{:S(2)}, u32[]{:S(2)}) collective-permute-start(bf16[10,128,128]{2,1,0:T(8,128)(2,1)S(1)} %collective-permute-done.10.refs_8_.refs_11_), channel_id=1, source_target_pairs={{0,8},{1,9},{2,10},{3,11},{4,12},{5,13},{6,14},{7,15},{8,0},{9,1},... | collective-permute-start | bytes 983048 | tf_op jit(solution)/shard_map/ppermute | solution.py:303
  34.0 9.9 %collective-permute-start.22 = (bf16[16,32,128]{2,1,0:T(8,128)(2,1)S(1)}, bf16[16,32,128]{2,1,0:T(8,128)(2,1)S(1)}, u32[]{:S(2)}, u32[]{:S(2)}) collective-permute-start(bf16[16,32,128]{2,1,0:T(8,128)(2,1)S(1)} %get-tuple-element.35), channel_id=1, source_target_pairs={{0,8},{1,9},{2,10},{3,11},{4,12},{5,13},{6,14},{7,15},{8,0},{9,1},... | collective-permute-start | bytes 393224 | tf_op jit(solution)/shard_map/ppermute | solution.py:303
  34.4 12.3 %collective-permute-start.9 = (bf16[10,128,128]{2,1,0:T(8,128)(2,1)S(1)}, bf16[10,128,128]{2,1,0:T(8,128)(2,1)S(1)}, u32[]{:S(2)}, u32[]{:S(2)}) collective-permute-start(bf16[10,128,128]{2,1,0:T(8,128)(2,1)S(1)} %collective-permute-done.8.refs_6_.refs_9_), channel_id=1, source_target_pairs={{0,1},{1,0},{2,3},{3,2},{4,5},{5,4},{6,7},{7,6},{8,9},{9,8},{10,11... | collective-permute-start | bytes 983048 | tf_op jit(solution)/shard_map/ppermute | solution.py:303
  41.7 5.3 %collective-permute-start.7 = (bf16[10,128,128]{2,1,0:T(8,128)(2,1)S(1)}, bf16[10,128,128]{2,1,0:T(8,128)(2,1)S(1)}, u32[]{:S(2)}, u32[]{:S(2)}) collective-permute-start(bf16[10,128,128]{2,1,0:T(8,128)(2,1)S(1)} %collective-permute-done.6.refs_4_.refs_7_), channel_id=1, source_target_pairs={{0,1},{1,0},{2,3},{3,2},{4,5},{5,4},{6,7},{7,6},{8,9},{9,8},{10,11... | collective-permute-start | bytes 983048 | tf_op jit(solution)/shard_map/ppermute | solution.py:303
  43.9 17.2 %collective-permute-start.15 = (bf16[10,128,128]{2,1,0:T(8,128)(2,1)S(1)}, bf16[10,128,128]{2,1,0:T(8,128)(2,1)S(1)}, u32[]{:S(2)}, u32[]{:S(2)}) collective-permute-start(bf16[10,128,128]{2,1,0:T(8,128)(2,1)S(1)} %collective-permute-done.14.refs_12_.refs_1_), channel_id=1, source_target_pairs={{0,1},{1,0},{2,3},{3,2},{4,5},{5,4},{6,7},{7,6},{8,9},{9,8},{10,11... | collective-permute-start | bytes 983048 | tf_op jit(solution)/shard_map/ppermute | solution.py:303
  43.9 15.3 %collective-permute-start.23 = (bf16[32,32,128]{2,1,0:T(8,128)(2,1)S(1)}, bf16[32,32,128]{2,1,0:T(8,128)(2,1)S(1)}, u32[]{:S(2)}, u32[]{:S(2)}) collective-permute-start(bf16[32,32,128]{2,1,0:T(8,128)(2,1)S(1)} %pad_maximum_fusion.refs_15_.refs_7_), channel_id=1, source_target_pairs={{0,4},{1,5},{2,6},{3,7},{4,0},{5,1},{6,2},{7,3},{8,12},{9,13},{10,... | collective-permute-start | bytes 786440 | tf_op jit(solution)/shard_map/ppermute | solution.py:309
  46.5 14.6 %collective-permute-start.17 = (bf16[6,128,128]{2,1,0:T(8,128)(2,1)S(1)}, bf16[6,128,128]{2,1,0:T(8,128)(2,1)S(1)}, u32[]{:S(2)}, u32[]{:S(2)}) collective-permute-start(bf16[6,128,128]{2,1,0:T(8,128)(2,1)S(1)} %collective-permute-done.16.refs_14_.refs_3_), channel_id=1, source_target_pairs={{0,1},{1,0},{2,3},{3,2},{4,5},{5,4},{6,7},{7,6},{8,9},{9,8},{10,11... | collective-permute-start | bytes 589832 | tf_op jit(solution)/shard_map/ppermute | solution.py:303
  46.7 14.4 %collective-permute-start.19 = (bf16[4,128,128]{2,1,0:T(8,128)(2,1)S(1)}, bf16[4,128,128]{2,1,0:T(8,128)(2,1)S(1)}, u32[]{:S(2)}, u32[]{:S(2)}) collective-permute-start(bf16[4,128,128]{2,1,0:T(8,128)(2,1)S(1)} %collective-permute-done.18.refs_16_.refs_5_), channel_id=1, source_target_pairs={{0,1},{1,0},{2,3},{3,2},{4,5},{5,4},{6,7},{7,6},{8,9},{9,8},{10,11... | collective-permute-start | bytes 393224 | tf_op jit(solution)/shard_map/ppermute | solution.py:303
  47.0 14.1 %collective-permute-start.3 = (s32[2,2,20]{2,1,0:T(2,128)S(1)}, s32[2,2,20]{2,1,0:T(2,128)S(1)}, u32[]{:S(2)}, u32[]{:S(2)}) collective-permute-start(s32[2,2,20]{2,1,0:T(2,128)S(1)} %pad_add_fusion.refs_0_), channel_id=1, source_target_pairs={{0,10},{1,11},{2,8},{3,9},{4,14},{5,15},{6,12},{7,13},{8,2},{9,3},... | collective-permute-start | bytes 968 | tf_op jit(solution)/shard_map/ppermute | solution.py:303
  62.2 6.4 %collective-permute-start.26 = (bf16[32,16,128]{2,1,0:T(8,128)(2,1)S(1)}, bf16[32,16,128]{2,1,0:T(8,128)(2,1)S(1)}, u32[]{:S(2)}, u32[]{:S(2)}) collective-permute-start(bf16[32,16,128]{2,1,0:T(8,128)(2,1)S(1)} %get-tuple-element.27.refs_5_), channel_id=1, source_target_pairs={{0,16},{8,24},{16,0},{24,8},{1,17},{9,25},{17,1},{25,9},{2,18},{10... | collective-permute-start | bytes 393224 | tf_op jit(solution)/shard_map/ppermute | solution.py:315
  63.7 7.3 %collective-permute-start.24 = (bf16[32,16,128]{2,1,0:T(8,128)(2,1)S(1)}, bf16[32,16,128]{2,1,0:T(8,128)(2,1)S(1)}, u32[]{:S(2)}, u32[]{:S(2)}) collective-permute-start(bf16[32,16,128]{2,1,0:T(8,128)(2,1)S(1)} %get-tuple-element.25.refs_5_), channel_id=1, source_target_pairs={{0,16},{8,24},{16,0},{24,8},{1,17},{9,25},{17,1},{25,9},{2,18},{10... | collective-permute-start | bytes 393224 | tf_op jit(solution)/shard_map/ppermute | solution.py:315
  70.9 9.9 %collective-permute-start.27 = (bf16[33,16,128]{2,1,0:T(8,128)(2,1)S(1)}, bf16[33,16,128]{2,1,0:T(8,128)(2,1)S(1)}, u32[]{:S(2)}, u32[]{:S(2)}) collective-permute-start(bf16[33,16,128]{2,1,0:T(8,128)(2,1)S(1)} %product.10.refs_5_), channel_id=1, source_target_pairs={{0,4},{1,5},{2,6},{3,7},{4,0},{5,1},{6,2},{7,3},{8,12},{9,13},{10,... | collective-permute-start | bytes 405512 | tf_op jit(solution)/shard_map/ppermute | solution.py:309
  73.2 11.4 %collective-permute-start.25 = (bf16[33,16,128]{2,1,0:T(8,128)(2,1)S(1)}, bf16[33,16,128]{2,1,0:T(8,128)(2,1)S(1)}, u32[]{:S(2)}, u32[]{:S(2)}) collective-permute-start(bf16[33,16,128]{2,1,0:T(8,128)(2,1)S(1)} %product.8.refs_5_), channel_id=1, source_target_pairs={{0,4},{1,5},{2,6},{3,7},{4,0},{5,1},{6,2},{7,3},{8,12},{9,13},{10,... | collective-permute-start | bytes 405512 | tf_op jit(solution)/shard_map/ppermute | solution.py:309
  83.0 5.2 %collective-permute-start.29 = (bf16[32,16,128]{2,1,0:T(8,128)(2,1)S(1)}, bf16[32,16,128]{2,1,0:T(8,128)(2,1)S(1)}, u32[]{:S(2)}, u32[]{:S(2)}) collective-permute-start(bf16[32,16,128]{2,1,0:T(8,128)(2,1)S(1)} %get-tuple-element.30.refs_4_), channel_id=1, source_target_pairs={{0,16},{8,24},{16,0},{24,8},{1,17},{9,25},{17,1},{25,9},{2,18},{10... | collective-permute-start | bytes 393224 | tf_op jit(solution)/shard_map/ppermute | solution.py:315
  86.9 5.0 %collective-permute-start.28 = (bf16[32,16,128]{2,1,0:T(8,128)(2,1)S(1)}, bf16[32,16,128]{2,1,0:T(8,128)(2,1)S(1)}, u32[]{:S(2)}, u32[]{:S(2)}) collective-permute-start(bf16[32,16,128]{2,1,0:T(8,128)(2,1)S(1)} %get-tuple-element.29.refs_2_), channel_id=1, source_target_pairs={{0,16},{8,24},{16,0},{24,8},{1,17},{9,25},{17,1},{25,9},{2,18},{10... | collective-permute-start | bytes 393224 | tf_op jit(solution)/shard_map/ppermute | solution.py:315
  92.2 4.8 %collective-permute-start.30 = (f32[32,128]{1,0:T(8,128)S(1)}, f32[32,128]{1,0:T(8,128)S(1)}, u32[]{:S(2)}, u32[]{:S(2)}) collective-permute-start(f32[32,128]{1,0:T(8,128)S(1)} %get-tuple-element.32), channel_id=1, source_target_pairs={{0,4},{1,5},{2,6},{3,7},{4,0},{5,1},{6,2},{7,3},{8,12},{9,13},{10,... | collective-permute-start | bytes 49160 | tf_op jit(solution)/shard_map/ppermute | solution.py:309
  92.3 5.0 %collective-permute-start.32 = (f32[32,128]{1,0:T(8,128)S(1)}, f32[32,128]{1,0:T(8,128)S(1)}, u32[]{:S(2)}, u32[]{:S(2)}) collective-permute-start(f32[32,128]{1,0:T(8,128)S(1)} %get-tuple-element.32), channel_id=1, source_target_pairs={{0,5},{1,4},{2,7},{3,6},{4,1},{5,0},{6,3},{7,2},{8,13},{9,12},{10,... | collective-permute-start | bytes 49160 | tf_op jit(solution)/shard_map/ppermute | solution.py:377
  92.3 4.9 %collective-permute-start.33 = (f32[32,128]{1,0:T(8,128)S(1)}, f32[32,128]{1,0:T(8,128)S(1)}, u32[]{:S(2)}, u32[]{:S(2)}) collective-permute-start(f32[32,128]{1,0:T(8,128)S(1)} %get-tuple-element.32), channel_id=1, source_target_pairs={{0,1},{1,0},{2,3},{3,2},{4,5},{5,4},{6,7},{7,6},{8,9},{9,8},{10,11... | collective-permute-start | bytes 49160 | tf_op jit(solution)/shard_map/ppermute | solution.py:303
  95.3 2.1 %collective-permute-start.31 = (bf16[2,2,4,32,128]{4,3,2,1,0:T(8,128)(2,1)S(1)}, bf16[2,2,4,32,128]{4,3,2,1,0:T(8,128)(2,1)S(1)}, u32[]{:S(2)}, u32[]{:S(2)}) collective-permute-start(bf16[2,2,4,32,128]{4,3,2,1,0:T(8,128)(2,1)S(1)} %get-tuple-element.33), channel_id=1, source_target_pairs={{0,1},{1,0},{2,3},{3,2},{4,5},{5,4},{6,7},{7,6},{8,9},{9,8},{10,11... | collective-permute-start | bytes 393224 | tf_op jit(solution)/shard_map/ppermute | solution.py:303
  97.5 5.8 %collective-permute-start.36 = (bf16[2,4,32,128]{3,2,1,0:T(8,128)(2,1)S(1)}, bf16[2,4,32,128]{3,2,1,0:T(8,128)(2,1)S(1)}, u32[]{:S(2)}, u32[]{:S(2)}) collective-permute-start(bf16[2,4,32,128]{3,2,1,0:T(8,128)(2,1)S(1)} %pad_maximum_fusion.4), channel_id=1, source_target_pairs={{0,10},{1,11},{2,8},{3,9},{4,14},{5,15},{6,12},{7,13},{8,2},{9,3},... | collective-permute-start | bytes 196616 | tf_op jit(solution)/shard_map/ppermute | solution.py:303
  101.0 4.3 %collective-permute-start.35 = (bf16[2,4,32,128]{3,2,1,0:T(8,128)(2,1)S(1)}, bf16[2,4,32,128]{3,2,1,0:T(8,128)(2,1)S(1)}, u32[]{:S(2)}, u32[]{:S(2)}) collective-permute-start(bf16[2,4,32,128]{3,2,1,0:T(8,128)(2,1)S(1)} %pad_maximum_fusion.3), channel_id=1, source_target_pairs={{0,8},{1,9},{2,10},{3,11},{4,12},{5,13},{6,14},{7,15},{8,0},{9,1},... | collective-permute-start | bytes 196616 | tf_op jit(solution)/shard_map/ppermute | solution.py:303
  101.6 4.3 %collective-permute-start.34 = (bf16[2,4,32,128]{3,2,1,0:T(8,128)(2,1)S(1)}, bf16[2,4,32,128]{3,2,1,0:T(8,128)(2,1)S(1)}, u32[]{:S(2)}, u32[]{:S(2)}) collective-permute-start(bf16[2,4,32,128]{3,2,1,0:T(8,128)(2,1)S(1)} %pad_maximum_fusion.2), channel_id=1, source_target_pairs={{0,2},{1,3},{2,0},{3,1},{4,6},{5,7},{6,4},{7,5},{8,10},{9,11},{10,... | collective-permute-start | bytes 196616 | tf_op jit(solution)/shard_map/ppermute | solution.py:303

commit v4 on v3

--- a/solution.py
+++ b/solution.py
@@ -317,7 +317,7 @@
         ]
 
     cut = slots // 2
-    late = slots - slots // 5
+    late = slots - slots // 4
     keep, other, tiles_0, tiles_1 = first_product(
         block_rows, block_cols, counts, start_basis, tiles, row_blocks, cut)
     image = keep.astype(F32) + send(other, 0, 0, 1).astype(F32)
@@ -390,8 +390,7 @@
 
     messages = [[jnp.stack([scaled(keep[dx, dz], squares), scaled(twin[dx, dz], twin_squares)]) for dz in range(2)] for dx in range(2)]
     messages = [
-        [messages[0][0], send(messages[0][1], 0, 1, 0)],
-        [send(messages[1][0], 1, 0, 0), send(messages[1][1], 1, 1, 0)],
+        [messages[0][0], send(messages[0][1], 0, 1, 0)], [send(messages[1][0], 1, 0, 0), send(messages[1][1], 1, 1, 0)]
     ]
     image_piece, basis_piece = assemble(messages, (image_span, basis_span))
     if image_rows < size:

time: 107 us -> 107 us (level)
  starting transfers between devices: 36.2 us -> 35.1 us
    ppermute x28, starting transfers between devices: 26.1 us -> 24.9 us  [send(): lax.ppermute(value, ('row', 'col'), [(r * n_col + c, (r ^ dx) * n_col + (...]
  transfers between devices with their start and end apart: 37 -> 37, of which waited for: 16 -> 17; matrix products, arithmetic and copies ran while one was open for 2% -> 2% of each run, Pallas kernels for 12% -> 12%
where the time goes in v4:
time: 107 us
  waiting for transfers between devices  51.1 us (48%)
  starting transfers between devices  35.1 us (33%)
  Pallas kernels  16.7 us (16%)
  other arithmetic  2.02 us (2%)
  between operations  1.59 us (1%)
    ppermute x28, waiting for transfers between devices, send(): lax.ppermute(value, ('row', 'col'), [(r * n_col + c, (r ^ dx) * n_col + (...  28 us
    ppermute x28, starting transfers between devices, send(): lax.ppermute(value, ('row', 'col'), [(r * n_col + c, (r ^ dx) * n_col + (...  24.9 us
    ppermute x4, waiting for transfers between devices, others_z(): lax.ppermute(value, 'col', [(c, (c + 4 * k) % n_col) for c in range(n_col)])  16.1 us
    pallas_call x6, Pallas kernels, block_product(): pl.pallas_call(body, out_shape=out_shape, in_specs=[pl.BlockSpec(memory_s...  11.9 us
    ppermute x4, waiting for transfers between devices, others_row(): lax.ppermute(value, 'row', [(r, (r + 2 * k) % n_row) for r in range(n_row)])  6.92 us
    ppermute x4, starting transfers between devices, others_z(): lax.ppermute(value, 'col', [(c, (c + 4 * k) % n_col) for c in range(n_col)])  5.8 us
    ppermute x4, starting transfers between devices, others_row(): lax.ppermute(value, 'row', [(r, (r + 2 * k) % n_row) for r in range(n_row)])  4.33 us
  transfers between devices with their start and end apart: 37, of which 17 were waited for; matrix products, arithmetic and copies ran while one was open for 2% of the time, Pallas kernels for 12%

profile of v4, /device:TPU:0, one launch (start us, length us, event | category | flops | bytes accessed | tf_op | source)
XLA Modules:
  0.0 106.5 jit_solution(3162620380568858301)
XLA Ops:
  1.3 1.9 %first.1 = (bf16[4,16,32,128]{3,2,1,0:T(8,128)(2,1)S(1)}, bf16[4,16,32,128]{3,2,1,0:T(8,128)(2,1)S(1)}, bf16[10,128,128]{2,1,0:T(8,128)(2,1)S(1)}, bf16[10,128,128]{2,1,0:T(8,128)(2,1)S(1)}) custom-call(s32[1,20]{1,0:T(1,128)} %rows_hbm.1, s32[1,20]{1,0:T(1,128)} %cols_hbm.1, s32[1,1]{1,0:T(1,128)} %copy.11.count_ref, bf16[1024,256]{1,0:T(8,128)(2,1)} %start_hbm.1, ...), custom_call_target="tpu_custom_call" | custom-call | tf_op jit(solution)/shard_map/first/pallas_call | solution.py:63
  3.2 0.6 collective-permute-start.20
  3.8 2.6 %collective-permute-start.12 = (bf16[10,128,128]{2,1,0:T(8,128)(2,1)S(1)}, bf16[10,128,128]{2,1,0:T(8,128)(2,1)S(1)}, u32[]{:S(2)}, u32[]{:S(2)}) collective-permute-start(bf16[10,128,128]{2,1,0:T(8,128)(2,1)S(1)} %get-tuple-element.23.refs_2_.refs_5_), channel_id=1, source_target_pairs={{0,2},{1,3},{2,0},{3,1},{4,6},{5,7},{6,4},{7,5},{8,10},{9,11},{10,... | collective-permute-start | bytes 983048 | tf_op jit(solution)/shard_map/ppermute | solution.py:303
  6.4 1.5 %collective-permute-start.8 = (bf16[10,128,128]{2,1,0:T(8,128)(2,1)S(1)}, bf16[10,128,128]{2,1,0:T(8,128)(2,1)S(1)}, u32[]{:S(2)}, u32[]{:S(2)}) collective-permute-start(bf16[10,128,128]{2,1,0:T(8,128)(2,1)S(1)} %get-tuple-element.23.refs_2_.refs_5_), channel_id=1, source_target_pairs={{0,8},{1,9},{2,10},{3,11},{4,12},{5,13},{6,14},{7,15},{8,0},{9,1},... | collective-permute-start | bytes 983048 | tf_op jit(solution)/shard_map/ppermute | solution.py:303
  8.1 0.5 collective-permute-start.21
  8.6 0.7 compare_select_fusion
  9.2 0.7 fusion.9
  9.9 1.6 %collective-permute-start.10 = (bf16[10,128,128]{2,1,0:T(8,128)(2,1)S(1)}, bf16[10,128,128]{2,1,0:T(8,128)(2,1)S(1)}, u32[]{:S(2)}, u32[]{:S(2)}) collective-permute-start(bf16[10,128,128]{2,1,0:T(8,128)(2,1)S(1)} %get-tuple-element.22.refs_0_.refs_3_), channel_id=1, source_target_pairs={{0,2},{1,3},{2,0},{3,1},{4,6},{5,7},{6,4},{7,5},{8,10},{9,11},{10,... | collective-permute-start | bytes 983048 | tf_op jit(solution)/shard_map/ppermute | solution.py:303
  11.6 0.9 collective-permute-start.6
  12.5 2.5 %collective-permute-done.12.refs_10_.refs_13_ = bf16[10,128,128]{2,1,0:T(8,128)(2,1)S(1)} collective-permute-done((bf16[10,128,128]{2,1,0:T(8,128)(2,1)S(1)}, bf16[10,128,128]{2,1,0:T(8,128)(2,1)S(1)}, u32[]{:S(2)}, u32[]{:S(2)}) %collective-permute-start.12) | collective-permute-done | bytes 327712 | tf_op jit(solution)/shard_map/ppermute | solution.py:303
  15.0 2.0 %collective-permute-done.8.refs_6_.refs_9_ = bf16[10,128,128]{2,1,0:T(8,128)(2,1)S(1)} collective-permute-done((bf16[10,128,128]{2,1,0:T(8,128)(2,1)S(1)}, bf16[10,128,128]{2,1,0:T(8,128)(2,1)S(1)}, u32[]{:S(2)}, u32[]{:S(2)}) %collective-permute-start.8) | collective-permute-done | bytes 327712 | tf_op jit(solution)/shard_map/ppermute | solution.py:303
  17.0 1.5 %collective-permute-start.1 = (s32[2,2,20]{2,1,0:T(2,128)S(1)}, s32[2,2,20]{2,1,0:T(2,128)S(1)}, u32[]{:S(2)}, u32[]{:S(2)}) collective-permute-start(s32[2,2,20]{2,1,0:T(2,128)S(1)} %pad_add_fusion.refs_0_), channel_id=1, source_target_pairs={{0,8},{1,9},{2,10},{3,11},{4,12},{5,13},{6,14},{7,15},{8,0},{9,1},... | collective-permute-start | bytes 968 | tf_op jit(solution)/shard_map/ppermute | solution.py:303
  18.5 4.7 %collective-permute-done.1.refs_1_ = s32[2,2,20]{2,1,0:T(2,128)S(1)} collective-permute-done((s32[2,2,20]{2,1,0:T(2,128)S(1)}, s32[2,2,20]{2,1,0:T(2,128)S(1)}, u32[]{:S(2)}, u32[]{:S(2)}) %collective-permute-start.1) | collective-permute-done | bytes 352 | tf_op jit(solution)/shard_map/ppermute | solution.py:303
  23.6 3.8 %collective-permute-done.2.refs_2_ = s32[2,2,20]{2,1,0:T(2,128)S(1)} collective-permute-done((s32[2,2,20]{2,1,0:T(2,128)S(1)}, s32[2,2,20]{2,1,0:T(2,128)S(1)}, u32[]{:S(2)}, u32[]{:S(2)}) %collective-permute-start.2) | collective-permute-done | bytes 352 | tf_op jit(solution)/shard_map/ppermute | solution.py:303
  27.4 1.7 %collective-permute-start.16 = (bf16[5,128,128]{2,1,0:T(8,128)(2,1)S(1)}, bf16[5,128,128]{2,1,0:T(8,128)(2,1)S(1)}, u32[]{:S(2)}, u32[]{:S(2)}) collective-permute-start(bf16[5,128,128]{2,1,0:T(8,128)(2,1)S(1)} %slice.56), channel_id=1, source_target_pairs={{0,8},{1,9},{2,10},{3,11},{4,12},{5,13},{6,14},{7,15},{8,0},{9,1},... | collective-permute-start | bytes 491528 | tf_op jit(solution)/shard_map/ppermute | solution.py:303
  29.1 1.6 %collective-permute-start.18 = (bf16[5,128,128]{2,1,0:T(8,128)(2,1)S(1)}, bf16[5,128,128]{2,1,0:T(8,128)(2,1)S(1)}, u32[]{:S(2)}, u32[]{:S(2)}) collective-permute-start(bf16[5,128,128]{2,1,0:T(8,128)(2,1)S(1)} %slice.57), channel_id=1, source_target_pairs={{0,2},{1,3},{2,0},{3,1},{4,6},{5,7},{6,4},{7,5},{8,10},{9,11},{10,... | collective-permute-start | bytes 491528 | tf_op jit(solution)/shard_map/ppermute | solution.py:303
  30.6 0.6 collective-permute-start.14
  31.3 1.6 %collective-permute-start.22 = (bf16[16,32,128]{2,1,0:T(8,128)(2,1)S(1)}, bf16[16,32,128]{2,1,0:T(8,128)(2,1)S(1)}, u32[]{:S(2)}, u32[]{:S(2)}) collective-permute-start(bf16[16,32,128]{2,1,0:T(8,128)(2,1)S(1)} %get-tuple-element.35), channel_id=1, source_target_pairs={{0,8},{1,9},{2,10},{3,11},{4,12},{5,13},{6,14},{7,15},{8,0},{9,1},... | collective-permute-start | bytes 393224 | tf_op jit(solution)/shard_map/ppermute | solution.py:303
  32.8 0.5 collective-permute-done.16.refs_14_.refs_3_
  33.3 1.1 %collective-permute-done.18.refs_16_.refs_5_ = bf16[5,128,128]{2,1,0:T(8,128)(2,1)S(1)} collective-permute-done((bf16[5,128,128]{2,1,0:T(8,128)(2,1)S(1)}, bf16[5,128,128]{2,1,0:T(8,128)(2,1)S(1)}, u32[]{:S(2)}, u32[]{:S(2)}) %collective-permute-start.18) | collective-permute-done | bytes 163872 | tf_op jit(solution)/shard_map/ppermute | solution.py:303
  34.5 6.8 %collective-permute-done.14.refs_12_.refs_1_ = bf16[10,128,128]{2,1,0:T(8,128)(2,1)S(1)} collective-permute-done((bf16[10,128,128]{2,1,0:T(8,128)(2,1)S(1)}, bf16[10,128,128]{2,1,0:T(8,128)(2,1)S(1)}, u32[]{:S(2)}, u32[]{:S(2)}) %collective-permute-start.14) | collective-permute-done | bytes 327712 | tf_op jit(solution)/shard_map/ppermute | solution.py:303
  41.3 2.3 %collective-permute-done.22 = bf16[16,32,128]{2,1,0:T(8,128)(2,1)S(1)} collective-permute-done((bf16[16,32,128]{2,1,0:T(8,128)(2,1)S(1)}, bf16[16,32,128]{2,1,0:T(8,128)(2,1)S(1)}, u32[]{:S(2)}, u32[]{:S(2)}) %collective-permute-start.22) | collective-permute-done | bytes 131104 | tf_op jit(solution)/shard_map/ppermute | solution.py:303
  43.6 2.7 %collective-permute-start.23 = (bf16[32,32,128]{2,1,0:T(8,128)(2,1)S(1)}, bf16[32,32,128]{2,1,0:T(8,128)(2,1)S(1)}, u32[]{:S(2)}, u32[]{:S(2)}) collective-permute-start(bf16[32,32,128]{2,1,0:T(8,128)(2,1)S(1)} %pad_maximum_fusion.refs_15_.refs_7_), channel_id=1, source_target_pairs={{0,4},{1,5},{2,6},{3,7},{4,0},{5,1},{6,2},{7,3},{8,12},{9,13},{10,... | collective-permute-start | bytes 786440 | tf_op jit(solution)/shard_map/ppermute | solution.py:309
  46.8 2.0 %collective-permute-start.3 = (s32[2,2,20]{2,1,0:T(2,128)S(1)}, s32[2,2,20]{2,1,0:T(2,128)S(1)}, u32[]{:S(2)}, u32[]{:S(2)}) collective-permute-start(s32[2,2,20]{2,1,0:T(2,128)S(1)} %pad_add_fusion.refs_0_), channel_id=1, source_target_pairs={{0,10},{1,11},{2,8},{3,9},{4,14},{5,15},{6,12},{7,13},{8,2},{9,3},... | collective-permute-start | bytes 968 | tf_op jit(solution)/shard_map/ppermute | solution.py:303
  48.8 10.1 %collective-permute-done.23.refs_16_.refs_8_ = bf16[32,32,128]{2,1,0:T(8,128)(2,1)S(1)} collective-permute-done((bf16[32,32,128]{2,1,0:T(8,128)(2,1)S(1)}, bf16[32,32,128]{2,1,0:T(8,128)(2,1)S(1)}, u32[]{:S(2)}, u32[]{:S(2)}) %collective-permute-start.23) | collective-permute-done | bytes 262176 | tf_op jit(solution)/shard_map/ppermute | solution.py:309
  58.9 1.8 %product.6.refs_9_ = f32[33,32,128]{2,1,0:T(8,128)S(1)} custom-call(s32[2,2,20]{2,1,0:T(2,128)S(1)} %pad_add_fusion.refs_0_, s32[2,2,20]{2,1,0:T(2,128)S(1)} %collective-permute-done.1.refs_1_, s32[2,2,20]{2,1,0:T(2,128)S(1)} %collective-permute-done.2.refs_2_, bf16[10,128,128]{2,1,0:T(8,128)(2,1)S(1)} %get-tuple-element.22.refs_0_.refs_3_, ...), custom_call_target="tpu_custom_call" | custom-call | tf_op jit(solution)/shard_map/product/pallas_call | solution.py:198
  60.8 1.1 %product.7 = (bf16[32,16,128]{2,1,0:T(8,128)(2,1)S(1)}, bf16[32,16,128]{2,1,0:T(8,128)(2,1)S(1)}) custom-call(s32[2,2,20]{2,1,0:T(2,128)S(1)} %collective-permute-done.3.refs_0_.refs_3_, bf16[10,128,128]{2,1,0:T(8,128)(2,1)S(1)} %collective-permute-done.14.refs_12_.refs_1_, bf16[10,128,128]{2,1,0:T(8,128)(2,1)S(1)} %collective-permute-done.15.refs_13_.refs_2_, ...), custom_call_target="tpu_custom_call" | custom-call | tf_op jit(solution)/shard_map/product/pallas_call | solution.py:198
  61.9 1.6 %collective-permute-start.26 = (bf16[32,16,128]{2,1,0:T(8,128)(2,1)S(1)}, bf16[32,16,128]{2,1,0:T(8,128)(2,1)S(1)}, u32[]{:S(2)}, u32[]{:S(2)}) collective-permute-start(bf16[32,16,128]{2,1,0:T(8,128)(2,1)S(1)} %get-tuple-element.27.refs_5_), channel_id=1, source_target_pairs={{0,16},{8,24},{16,0},{24,8},{1,17},{9,25},{17,1},{25,9},{2,18},{10... | collective-permute-start | bytes 393224 | tf_op jit(solution)/shard_map/ppermute | solution.py:315
  64.0 1.8 %flip.1.refs_4_ = bf16[320,128,128]{2,1,0:T(8,128)(2,1)S(1)} custom-call(bf16[10,128,128]{2,1,0:T(8,128)(2,1)S(1)} %get-tuple-element.22.refs_0_.refs_3_, bf16[10,128,128]{2,1,0:T(8,128)(2,1)S(1)} %collective-permute-done.4.refs_1_.refs_4_, bf16[10,128,128]{2,1,0:T(8,128)(2,1)S(1)} %get-tuple-element.23.refs_2_.refs_5_, ...), custom_call_target="tpu_custom_call" | custom-call | tf_op jit(solution)/shard_map/flip/pallas_call | solution.py:102
  65.8 2.5 %collective-permute-done.26.refs_6_ = bf16[32,16,128]{2,1,0:T(8,128)(2,1)S(1)} collective-permute-done((bf16[32,16,128]{2,1,0:T(8,128)(2,1)S(1)}, bf16[32,16,128]{2,1,0:T(8,128)(2,1)S(1)}, u32[]{:S(2)}, u32[]{:S(2)}) %collective-permute-start.26) | collective-permute-done | bytes 131104 | tf_op jit(solution)/shard_map/ppermute | solution.py:315
  68.3 2.2 %product.10.refs_5_ = bf16[33,16,128]{2,1,0:T(8,128)(2,1)S(1)} custom-call(s32[2,2,20]{2,1,0:T(2,128)S(1)} %pad_add_fusion.refs_0_, s32[2,2,20]{2,1,0:T(2,128)S(1)} %collective-permute-done.1.refs_1_, s32[2,2,20]{2,1,0:T(2,128)S(1)} %collective-permute-done.2.refs_2_, s32[2,2,20]{2,1,0:T(2,128)S(1)} %collective-permute-done.3.refs_0_.refs_3_, ...), custom_call_target="tpu_custom_call" | custom-call | tf_op jit(solution)/shard_map/product/pallas_call | solution.py:198
  70.7 2.2 %product.8.refs_5_ = bf16[33,16,128]{2,1,0:T(8,128)(2,1)S(1)} custom-call(s32[2,2,20]{2,1,0:T(2,128)S(1)} %pad_add_fusion.refs_0_, s32[2,2,20]{2,1,0:T(2,128)S(1)} %collective-permute-done.1.refs_1_, s32[2,2,20]{2,1,0:T(2,128)S(1)} %collective-permute-done.2.refs_2_, s32[2,2,20]{2,1,0:T(2,128)S(1)} %collective-permute-done.3.refs_0_.refs_3_, ...), custom_call_target="tpu_custom_call" | custom-call | tf_op jit(solution)/shard_map/product/pallas_call | solution.py:198
  72.9 3.0 %collective-permute-start.25 = (bf16[33,16,128]{2,1,0:T(8,128)(2,1)S(1)}, bf16[33,16,128]{2,1,0:T(8,128)(2,1)S(1)}, u32[]{:S(2)}, u32[]{:S(2)}) collective-permute-start(bf16[33,16,128]{2,1,0:T(8,128)(2,1)S(1)} %product.8.refs_5_), channel_id=1, source_target_pairs={{0,4},{1,5},{2,6},{3,7},{4,0},{5,1},{6,2},{7,3},{8,12},{9,13},{10,... | collective-permute-start | bytes 405512 | tf_op jit(solution)/shard_map/ppermute | solution.py:309
  75.9 4.4 %collective-permute-done.27.refs_6_ = bf16[33,16,128]{2,1,0:T(8,128)(2,1)S(1)} collective-permute-done((bf16[33,16,128]{2,1,0:T(8,128)(2,1)S(1)}, bf16[33,16,128]{2,1,0:T(8,128)(2,1)S(1)}, u32[]{:S(2)}, u32[]{:S(2)}) %collective-permute-start.27) | collective-permute-done | bytes 135200 | tf_op jit(solution)/shard_map/ppermute | solution.py:309
  80.3 2.2 %product.11 = (bf16[32,16,128]{2,1,0:T(8,128)(2,1)S(1)}, bf16[32,16,128]{2,1,0:T(8,128)(2,1)S(1)}) custom-call(s32[2,2,20]{2,1,0:T(2,128)S(1)} %pad_add_fusion.refs_0_, s32[2,2,20]{2,1,0:T(2,128)S(1)} %collective-permute-done.1.refs_1_, s32[2,2,20]{2,1,0:T(2,128)S(1)} %collective-permute-done.2.refs_2_, ...), custom_call_target="tpu_custom_call" | custom-call | tf_op jit(solution)/shard_map/product/pallas_call | solution.py:198
  82.6 1.6 %collective-permute-start.29 = (bf16[32,16,128]{2,1,0:T(8,128)(2,1)S(1)}, bf16[32,16,128]{2,1,0:T(8,128)(2,1)S(1)}, u32[]{:S(2)}, u32[]{:S(2)}) collective-permute-start(bf16[32,16,128]{2,1,0:T(8,128)(2,1)S(1)} %get-tuple-element.30.refs_4_), channel_id=1, source_target_pairs={{0,16},{8,24},{16,0},{24,8},{1,17},{9,25},{17,1},{25,9},{2,18},{10... | collective-permute-start | bytes 393224 | tf_op jit(solution)/shard_map/ppermute | solution.py:315
  84.2 2.2 %product.9 = (bf16[32,16,128]{2,1,0:T(8,128)(2,1)S(1)}, bf16[32,16,128]{2,1,0:T(8,128)(2,1)S(1)}) custom-call(s32[2,2,20]{2,1,0:T(2,128)S(1)} %pad_add_fusion.refs_0_, s32[2,2,20]{2,1,0:T(2,128)S(1)} %collective-permute-done.1.refs_1_, s32[2,2,20]{2,1,0:T(2,128)S(1)} %collective-permute-done.2.refs_2_, ...), custom_call_target="tpu_custom_call" | custom-call | tf_op jit(solution)/shard_map/product/pallas_call | solution.py:198
  86.4 0.6 collective-permute-start.28
  87.1 0.5 collective-permute-done.29.refs_5_
  87.6 3.9 %collective-permute-done.28.refs_3_ = bf16[32,16,128]{2,1,0:T(8,128)(2,1)S(1)} collective-permute-done((bf16[32,16,128]{2,1,0:T(8,128)(2,1)S(1)}, bf16[32,16,128]{2,1,0:T(8,128)(2,1)S(1)}, u32[]{:S(2)}, u32[]{:S(2)}) %collective-permute-start.28) | collective-permute-done | bytes 131104 | tf_op jit(solution)/shard_map/ppermute | solution.py:315
  91.8 2.9 %collective-permute-start.33 = (f32[32,128]{1,0:T(8,128)S(1)}, f32[32,128]{1,0:T(8,128)S(1)}, u32[]{:S(2)}, u32[]{:S(2)}) collective-permute-start(f32[32,128]{1,0:T(8,128)S(1)} %get-tuple-element.32), channel_id=1, source_target_pairs={{0,1},{1,0},{2,3},{3,2},{4,5},{5,4},{6,7},{7,6},{8,9},{9,8},{10,11... | collective-permute-start | bytes 49160 | tf_op jit(solution)/shard_map/ppermute | solution.py:303
  94.8 1.6 %collective-permute-done.30 = f32[32,128]{1,0:T(8,128)S(1)} collective-permute-done((f32[32,128]{1,0:T(8,128)S(1)}, f32[32,128]{1,0:T(8,128)S(1)}, u32[]{:S(2)}, u32[]{:S(2)}) %collective-permute-start.30) | collective-permute-done | bytes 16416 | tf_op jit(solution)/shard_map/ppermute | solution.py:309
  96.9 3.3 %collective-permute-start.36 = (bf16[2,4,32,128]{3,2,1,0:T(8,128)(2,1)S(1)}, bf16[2,4,32,128]{3,2,1,0:T(8,128)(2,1)S(1)}, u32[]{:S(2)}, u32[]{:S(2)}) collective-permute-start(bf16[2,4,32,128]{3,2,1,0:T(8,128)(2,1)S(1)} %pad_maximum_fusion.4), channel_id=1, source_target_pairs={{0,10},{1,11},{2,8},{3,9},{4,14},{5,15},{6,12},{7,13},{8,2},{9,3},... | collective-permute-start | bytes 196616 | tf_op jit(solution)/shard_map/ppermute | solution.py:303
  100.3 1.1 %collective-permute-start.35 = (bf16[2,4,32,128]{3,2,1,0:T(8,128)(2,1)S(1)}, bf16[2,4,32,128]{3,2,1,0:T(8,128)(2,1)S(1)}, u32[]{:S(2)}, u32[]{:S(2)}) collective-permute-start(bf16[2,4,32,128]{3,2,1,0:T(8,128)(2,1)S(1)} %pad_maximum_fusion.3), channel_id=1, source_target_pairs={{0,8},{1,9},{2,10},{3,11},{4,12},{5,13},{6,14},{7,15},{8,0},{9,1},... | collective-permute-start | bytes 196616 | tf_op jit(solution)/shard_map/ppermute | solution.py:303
  101.5 1.2 %collective-permute-done.36.refs_3_ = bf16[2,4,32,128]{3,2,1,0:T(8,128)(2,1)S(1)} collective-permute-done((bf16[2,4,32,128]{3,2,1,0:T(8,128)(2,1)S(1)}, bf16[2,4,32,128]{3,2,1,0:T(8,128)(2,1)S(1)}, u32[]{:S(2)}, u32[]{:S(2)}) %collective-permute-start.36) | collective-permute-done | bytes 65568 | tf_op jit(solution)/shard_map/ppermute | solution.py:303
  102.7 1.9 %collective-permute-done.35.refs_2_ = bf16[2,4,32,128]{3,2,1,0:T(8,128)(2,1)S(1)} collective-permute-done((bf16[2,4,32,128]{3,2,1,0:T(8,128)(2,1)S(1)}, bf16[2,4,32,128]{3,2,1,0:T(8,128)(2,1)S(1)}, u32[]{:S(2)}, u32[]{:S(2)}) %collective-permute-start.35) | collective-permute-done | bytes 65568 | tf_op jit(solution)/shard_map/ppermute | solution.py:303
  104.6 1.1 %collective-permute-done.34.refs_1_ = bf16[2,4,32,128]{3,2,1,0:T(8,128)(2,1)S(1)} collective-permute-done((bf16[2,4,32,128]{3,2,1,0:T(8,128)(2,1)S(1)}, bf16[2,4,32,128]{3,2,1,0:T(8,128)(2,1)S(1)}, u32[]{:S(2)}, u32[]{:S(2)}) %collective-permute-start.34) | collective-permute-done | bytes 65568 | tf_op jit(solution)/shard_map/ppermute | solution.py:303
  105.7 0.8 assemble.1
  (60 shorter events, 2.6 us)
Async XLA Ops:
  3.2 4.7 %collective-permute-start.20 = (bf16[4,16,32,128]{3,2,1,0:T(8,128)(2,1)S(1)}, bf16[4,16,32,128]{3,2,1,0:T(8,128)(2,1)S(1)}, u32[]{:S(2)}, u32[]{:S(2)}) collective-permute-start(bf16[4,16,32,128]{3,2,1,0:T(8,128)(2,1)S(1)} %get-tuple-element.18), channel_id=1, source_target_pairs={{0,1},{1,0},{2,3},{3,2},{4,5},{5,4},{6,7},{7,6},{8,9},{9,8},{10,11... | collective-permute-start | bytes 1572872 | tf_op jit(solution)/shard_map/ppermute | solution.py:303
  3.8 11.2 %collective-permute-start.12 = (bf16[10,128,128]{2,1,0:T(8,128)(2,1)S(1)}, bf16[10,128,128]{2,1,0:T(8,128)(2,1)S(1)}, u32[]{:S(2)}, u32[]{:S(2)}) collective-permute-start(bf16[10,128,128]{2,1,0:T(8,128)(2,1)S(1)} %get-tuple-element.23.refs_2_.refs_5_), channel_id=1, source_target_pairs={{0,2},{1,3},{2,0},{3,1},{4,6},{5,7},{6,4},{7,5},{8,10},{9,11},{10,... | collective-permute-start | bytes 983048 | tf_op jit(solution)/shard_map/ppermute | solution.py:303
  6.4 10.6 %collective-permute-start.8 = (bf16[10,128,128]{2,1,0:T(8,128)(2,1)S(1)}, bf16[10,128,128]{2,1,0:T(8,128)(2,1)S(1)}, u32[]{:S(2)}, u32[]{:S(2)}) collective-permute-start(bf16[10,128,128]{2,1,0:T(8,128)(2,1)S(1)} %get-tuple-element.23.refs_2_.refs_5_), channel_id=1, source_target_pairs={{0,8},{1,9},{2,10},{3,11},{4,12},{5,13},{6,14},{7,15},{8,0},{9,1},... | collective-permute-start | bytes 983048 | tf_op jit(solution)/shard_map/ppermute | solution.py:303
  8.1 15.2 %collective-permute-start.21 = (bf16[2,16,32,128]{3,2,1,0:T(8,128)(2,1)S(1)}, bf16[2,16,32,128]{3,2,1,0:T(8,128)(2,1)S(1)}, u32[]{:S(2)}, u32[]{:S(2)}) collective-permute-start(bf16[2,16,32,128]{3,2,1,0:T(8,128)(2,1)S(1)} %slice_bitcast_fusion), channel_id=1, source_target_pairs={{0,2},{1,3},{2,0},{3,1},{4,6},{5,7},{6,4},{7,5},{8,10},{9,11},{10,... | collective-permute-start | bytes 786440 | tf_op jit(solution)/shard_map/ppermute | solution.py:303
  9.9 1.6 %collective-permute-start = (s32[2,20]{1,0:T(2,128)S(1)}, s32[2,20]{1,0:T(2,128)S(1)}, u32[]{:S(2)}, u32[]{:S(2)}) collective-permute-start(s32[2,20]{1,0:T(2,128)S(1)} %get-tuple-element.45), channel_id=1, source_target_pairs={{0,1},{1,0},{2,3},{3,2},{4,5},{5,4},{6,7},{7,6},{8,9},{9,8},{10,11... | collective-permute-start | bytes 488 | tf_op jit(solution)/shard_map/ppermute | solution.py:303
  9.9 19.1 %collective-permute-start.10 = (bf16[10,128,128]{2,1,0:T(8,128)(2,1)S(1)}, bf16[10,128,128]{2,1,0:T(8,128)(2,1)S(1)}, u32[]{:S(2)}, u32[]{:S(2)}) collective-permute-start(bf16[10,128,128]{2,1,0:T(8,128)(2,1)S(1)} %get-tuple-element.22.refs_0_.refs_3_), channel_id=1, source_target_pairs={{0,2},{1,3},{2,0},{3,1},{4,6},{5,7},{6,4},{7,5},{8,10},{9,11},{10,... | collective-permute-start | bytes 983048 | tf_op jit(solution)/shard_map/ppermute | solution.py:303
  11.6 19.1 %collective-permute-start.6 = (bf16[10,128,128]{2,1,0:T(8,128)(2,1)S(1)}, bf16[10,128,128]{2,1,0:T(8,128)(2,1)S(1)}, u32[]{:S(2)}, u32[]{:S(2)}) collective-permute-start(bf16[10,128,128]{2,1,0:T(8,128)(2,1)S(1)} %get-tuple-element.22.refs_0_.refs_3_), channel_id=1, source_target_pairs={{0,8},{1,9},{2,10},{3,11},{4,12},{5,13},{6,14},{7,15},{8,0},{9,1},... | collective-permute-start | bytes 983048 | tf_op jit(solution)/shard_map/ppermute | solution.py:303
  15.0 15.7 %collective-permute-start.4 = (bf16[10,128,128]{2,1,0:T(8,128)(2,1)S(1)}, bf16[10,128,128]{2,1,0:T(8,128)(2,1)S(1)}, u32[]{:S(2)}, u32[]{:S(2)}) collective-permute-start(bf16[10,128,128]{2,1,0:T(8,128)(2,1)S(1)} %get-tuple-element.22.refs_0_.refs_3_), channel_id=1, source_target_pairs={{0,1},{1,0},{2,3},{3,2},{4,5},{5,4},{6,7},{7,6},{8,9},{9,8},{10,11... | collective-permute-start | bytes 983048 | tf_op jit(solution)/shard_map/ppermute | solution.py:303
  17.0 6.2 %collective-permute-start.1 = (s32[2,2,20]{2,1,0:T(2,128)S(1)}, s32[2,2,20]{2,1,0:T(2,128)S(1)}, u32[]{:S(2)}, u32[]{:S(2)}) collective-permute-start(s32[2,2,20]{2,1,0:T(2,128)S(1)} %pad_add_fusion.refs_0_), channel_id=1, source_target_pairs={{0,8},{1,9},{2,10},{3,11},{4,12},{5,13},{6,14},{7,15},{8,0},{9,1},... | collective-permute-start | bytes 968 | tf_op jit(solution)/shard_map/ppermute | solution.py:303
  23.2 8.0 %collective-permute-start.5 = (bf16[10,128,128]{2,1,0:T(8,128)(2,1)S(1)}, bf16[10,128,128]{2,1,0:T(8,128)(2,1)S(1)}, u32[]{:S(2)}, u32[]{:S(2)}) collective-permute-start(bf16[10,128,128]{2,1,0:T(8,128)(2,1)S(1)} %get-tuple-element.23.refs_2_.refs_5_), channel_id=1, source_target_pairs={{0,1},{1,0},{2,3},{3,2},{4,5},{5,4},{6,7},{7,6},{8,9},{9,8},{10,11... | collective-permute-start | bytes 983048 | tf_op jit(solution)/shard_map/ppermute | solution.py:303
  23.2 4.1 %collective-permute-start.2 = (s32[2,2,20]{2,1,0:T(2,128)S(1)}, s32[2,2,20]{2,1,0:T(2,128)S(1)}, u32[]{:S(2)}, u32[]{:S(2)}) collective-permute-start(s32[2,2,20]{2,1,0:T(2,128)S(1)} %pad_add_fusion.refs_0_), channel_id=1, source_target_pairs={{0,2},{1,3},{2,0},{3,1},{4,6},{5,7},{6,4},{7,5},{8,10},{9,11},{10,... | collective-permute-start | bytes 968 | tf_op jit(solution)/shard_map/ppermute | solution.py:303
  27.4 6.0 %collective-permute-start.16 = (bf16[5,128,128]{2,1,0:T(8,128)(2,1)S(1)}, bf16[5,128,128]{2,1,0:T(8,128)(2,1)S(1)}, u32[]{:S(2)}, u32[]{:S(2)}) collective-permute-start(bf16[5,128,128]{2,1,0:T(8,128)(2,1)S(1)} %slice.56), channel_id=1, source_target_pairs={{0,8},{1,9},{2,10},{3,11},{4,12},{5,13},{6,14},{7,15},{8,0},{9,1},... | collective-permute-start | bytes 491528 | tf_op jit(solution)/shard_map/ppermute | solution.py:303
  29.1 5.4 %collective-permute-start.18 = (bf16[5,128,128]{2,1,0:T(8,128)(2,1)S(1)}, bf16[5,128,128]{2,1,0:T(8,128)(2,1)S(1)}, u32[]{:S(2)}, u32[]{:S(2)}) collective-permute-start(bf16[5,128,128]{2,1,0:T(8,128)(2,1)S(1)} %slice.57), channel_id=1, source_target_pairs={{0,2},{1,3},{2,0},{3,1},{4,6},{5,7},{6,4},{7,5},{8,10},{9,11},{10,... | collective-permute-start | bytes 491528 | tf_op jit(solution)/shard_map/ppermute | solution.py:303
  30.6 13.0 %collective-permute-start.11 = (bf16[10,128,128]{2,1,0:T(8,128)(2,1)S(1)}, bf16[10,128,128]{2,1,0:T(8,128)(2,1)S(1)}, u32[]{:S(2)}, u32[]{:S(2)}) collective-permute-start(bf16[10,128,128]{2,1,0:T(8,128)(2,1)S(1)} %collective-permute-done.10.refs_8_.refs_11_), channel_id=1, source_target_pairs={{0,1},{1,0},{2,3},{3,2},{4,5},{5,4},{6,7},{7,6},{8,9},{9,8},{10,11... | collective-permute-start | bytes 983048 | tf_op jit(solution)/shard_map/ppermute | solution.py:303
  30.6 10.6 %collective-permute-start.14 = (bf16[10,128,128]{2,1,0:T(8,128)(2,1)S(1)}, bf16[10,128,128]{2,1,0:T(8,128)(2,1)S(1)}, u32[]{:S(2)}, u32[]{:S(2)}) collective-permute-start(bf16[10,128,128]{2,1,0:T(8,128)(2,1)S(1)} %collective-permute-done.10.refs_8_.refs_11_), channel_id=1, source_target_pairs={{0,8},{1,9},{2,10},{3,11},{4,12},{5,13},{6,14},{7,15},{8,0},{9,1},... | collective-permute-start | bytes 983048 | tf_op jit(solution)/shard_map/ppermute | solution.py:303
  31.3 12.3 %collective-permute-start.22 = (bf16[16,32,128]{2,1,0:T(8,128)(2,1)S(1)}, bf16[16,32,128]{2,1,0:T(8,128)(2,1)S(1)}, u32[]{:S(2)}, u32[]{:S(2)}) collective-permute-start(bf16[16,32,128]{2,1,0:T(8,128)(2,1)S(1)} %get-tuple-element.35), channel_id=1, source_target_pairs={{0,8},{1,9},{2,10},{3,11},{4,12},{5,13},{6,14},{7,15},{8,0},{9,1},... | collective-permute-start | bytes 393224 | tf_op jit(solution)/shard_map/ppermute | solution.py:303
  33.3 12.9 %collective-permute-start.13 = (bf16[10,128,128]{2,1,0:T(8,128)(2,1)S(1)}, bf16[10,128,128]{2,1,0:T(8,128)(2,1)S(1)}, u32[]{:S(2)}, u32[]{:S(2)}) collective-permute-start(bf16[10,128,128]{2,1,0:T(8,128)(2,1)S(1)} %collective-permute-done.12.refs_10_.refs_13_), channel_id=1, source_target_pairs={{0,1},{1,0},{2,3},{3,2},{4,5},{5,4},{6,7},{7,6},{8,9},{9,8},{10,11... | collective-permute-start | bytes 983048 | tf_op jit(solution)/shard_map/ppermute | solution.py:303
  34.4 12.1 %collective-permute-start.9 = (bf16[10,128,128]{2,1,0:T(8,128)(2,1)S(1)}, bf16[10,128,128]{2,1,0:T(8,128)(2,1)S(1)}, u32[]{:S(2)}, u32[]{:S(2)}) collective-permute-start(bf16[10,128,128]{2,1,0:T(8,128)(2,1)S(1)} %collective-permute-done.8.refs_6_.refs_9_), channel_id=1, source_target_pairs={{0,1},{1,0},{2,3},{3,2},{4,5},{5,4},{6,7},{7,6},{8,9},{9,8},{10,11... | collective-permute-start | bytes 983048 | tf_op jit(solution)/shard_map/ppermute | solution.py:303
  41.3 5.5 %collective-permute-start.7 = (bf16[10,128,128]{2,1,0:T(8,128)(2,1)S(1)}, bf16[10,128,128]{2,1,0:T(8,128)(2,1)S(1)}, u32[]{:S(2)}, u32[]{:S(2)}) collective-permute-start(bf16[10,128,128]{2,1,0:T(8,128)(2,1)S(1)} %collective-permute-done.6.refs_4_.refs_7_), channel_id=1, source_target_pairs={{0,1},{1,0},{2,3},{3,2},{4,5},{5,4},{6,7},{7,6},{8,9},{9,8},{10,11... | collective-permute-start | bytes 983048 | tf_op jit(solution)/shard_map/ppermute | solution.py:303
  43.6 17.2 %collective-permute-start.15 = (bf16[10,128,128]{2,1,0:T(8,128)(2,1)S(1)}, bf16[10,128,128]{2,1,0:T(8,128)(2,1)S(1)}, u32[]{:S(2)}, u32[]{:S(2)}) collective-permute-start(bf16[10,128,128]{2,1,0:T(8,128)(2,1)S(1)} %collective-permute-done.14.refs_12_.refs_1_), channel_id=1, source_target_pairs={{0,1},{1,0},{2,3},{3,2},{4,5},{5,4},{6,7},{7,6},{8,9},{9,8},{10,11... | collective-permute-start | bytes 983048 | tf_op jit(solution)/shard_map/ppermute | solution.py:303
  43.6 15.3 %collective-permute-start.23 = (bf16[32,32,128]{2,1,0:T(8,128)(2,1)S(1)}, bf16[32,32,128]{2,1,0:T(8,128)(2,1)S(1)}, u32[]{:S(2)}, u32[]{:S(2)}) collective-permute-start(bf16[32,32,128]{2,1,0:T(8,128)(2,1)S(1)} %pad_maximum_fusion.refs_15_.refs_7_), channel_id=1, source_target_pairs={{0,4},{1,5},{2,6},{3,7},{4,0},{5,1},{6,2},{7,3},{8,12},{9,13},{10,... | collective-permute-start | bytes 786440 | tf_op jit(solution)/shard_map/ppermute | solution.py:309
  46.3 14.5 %collective-permute-start.17 = (bf16[5,128,128]{2,1,0:T(8,128)(2,1)S(1)}, bf16[5,128,128]{2,1,0:T(8,128)(2,1)S(1)}, u32[]{:S(2)}, u32[]{:S(2)}) collective-permute-start(bf16[5,128,128]{2,1,0:T(8,128)(2,1)S(1)} %collective-permute-done.16.refs_14_.refs_3_), channel_id=1, source_target_pairs={{0,1},{1,0},{2,3},{3,2},{4,5},{5,4},{6,7},{7,6},{8,9},{9,8},{10,11... | collective-permute-start | bytes 491528 | tf_op jit(solution)/shard_map/ppermute | solution.py:303
  46.5 14.3 %collective-permute-start.19 = (bf16[5,128,128]{2,1,0:T(8,128)(2,1)S(1)}, bf16[5,128,128]{2,1,0:T(8,128)(2,1)S(1)}, u32[]{:S(2)}, u32[]{:S(2)}) collective-permute-start(bf16[5,128,128]{2,1,0:T(8,128)(2,1)S(1)} %collective-permute-done.18.refs_16_.refs_5_), channel_id=1, source_target_pairs={{0,1},{1,0},{2,3},{3,2},{4,5},{5,4},{6,7},{7,6},{8,9},{9,8},{10,11... | collective-permute-start | bytes 491528 | tf_op jit(solution)/shard_map/ppermute | solution.py:303
  46.8 14.0 %collective-permute-start.3 = (s32[2,2,20]{2,1,0:T(2,128)S(1)}, s32[2,2,20]{2,1,0:T(2,128)S(1)}, u32[]{:S(2)}, u32[]{:S(2)}) collective-permute-start(s32[2,2,20]{2,1,0:T(2,128)S(1)} %pad_add_fusion.refs_0_), channel_id=1, source_target_pairs={{0,10},{1,11},{2,8},{3,9},{4,14},{5,15},{6,12},{7,13},{8,2},{9,3},... | collective-permute-start | bytes 968 | tf_op jit(solution)/shard_map/ppermute | solution.py:303
  61.9 6.4 %collective-permute-start.26 = (bf16[32,16,128]{2,1,0:T(8,128)(2,1)S(1)}, bf16[32,16,128]{2,1,0:T(8,128)(2,1)S(1)}, u32[]{:S(2)}, u32[]{:S(2)}) collective-permute-start(bf16[32,16,128]{2,1,0:T(8,128)(2,1)S(1)} %get-tuple-element.27.refs_5_), channel_id=1, source_target_pairs={{0,16},{8,24},{16,0},{24,8},{1,17},{9,25},{17,1},{25,9},{2,18},{10... | collective-permute-start | bytes 393224 | tf_op jit(solution)/shard_map/ppermute | solution.py:315
  63.5 7.2 %collective-permute-start.24 = (bf16[32,16,128]{2,1,0:T(8,128)(2,1)S(1)}, bf16[32,16,128]{2,1,0:T(8,128)(2,1)S(1)}, u32[]{:S(2)}, u32[]{:S(2)}) collective-permute-start(bf16[32,16,128]{2,1,0:T(8,128)(2,1)S(1)} %get-tuple-element.25.refs_5_), channel_id=1, source_target_pairs={{0,16},{8,24},{16,0},{24,8},{1,17},{9,25},{17,1},{25,9},{2,18},{10... | collective-permute-start | bytes 393224 | tf_op jit(solution)/shard_map/ppermute | solution.py:315
  70.6 9.7 %collective-permute-start.27 = (bf16[33,16,128]{2,1,0:T(8,128)(2,1)S(1)}, bf16[33,16,128]{2,1,0:T(8,128)(2,1)S(1)}, u32[]{:S(2)}, u32[]{:S(2)}) collective-permute-start(bf16[33,16,128]{2,1,0:T(8,128)(2,1)S(1)} %product.10.refs_5_), channel_id=1, source_target_pairs={{0,4},{1,5},{2,6},{3,7},{4,0},{5,1},{6,2},{7,3},{8,12},{9,13},{10,... | collective-permute-start | bytes 405512 | tf_op jit(solution)/shard_map/ppermute | solution.py:309
  72.9 11.3 %collective-permute-start.25 = (bf16[33,16,128]{2,1,0:T(8,128)(2,1)S(1)}, bf16[33,16,128]{2,1,0:T(8,128)(2,1)S(1)}, u32[]{:S(2)}, u32[]{:S(2)}) collective-permute-start(bf16[33,16,128]{2,1,0:T(8,128)(2,1)S(1)} %product.8.refs_5_), channel_id=1, source_target_pairs={{0,4},{1,5},{2,6},{3,7},{4,0},{5,1},{6,2},{7,3},{8,12},{9,13},{10,... | collective-permute-start | bytes 405512 | tf_op jit(solution)/shard_map/ppermute | solution.py:309
  82.6 5.0 %collective-permute-start.29 = (bf16[32,16,128]{2,1,0:T(8,128)(2,1)S(1)}, bf16[32,16,128]{2,1,0:T(8,128)(2,1)S(1)}, u32[]{:S(2)}, u32[]{:S(2)}) collective-permute-start(bf16[32,16,128]{2,1,0:T(8,128)(2,1)S(1)} %get-tuple-element.30.refs_4_), channel_id=1, source_target_pairs={{0,16},{8,24},{16,0},{24,8},{1,17},{9,25},{17,1},{25,9},{2,18},{10... | collective-permute-start | bytes 393224 | tf_op jit(solution)/shard_map/ppermute | solution.py:315
  86.4 5.0 %collective-permute-start.28 = (bf16[32,16,128]{2,1,0:T(8,128)(2,1)S(1)}, bf16[32,16,128]{2,1,0:T(8,128)(2,1)S(1)}, u32[]{:S(2)}, u32[]{:S(2)}) collective-permute-start(bf16[32,16,128]{2,1,0:T(8,128)(2,1)S(1)} %get-tuple-element.29.refs_2_), channel_id=1, source_target_pairs={{0,16},{8,24},{16,0},{24,8},{1,17},{9,25},{17,1},{25,9},{2,18},{10... | collective-permute-start | bytes 393224 | tf_op jit(solution)/shard_map/ppermute | solution.py:315
  91.7 4.7 %collective-permute-start.30 = (f32[32,128]{1,0:T(8,128)S(1)}, f32[32,128]{1,0:T(8,128)S(1)}, u32[]{:S(2)}, u32[]{:S(2)}) collective-permute-start(f32[32,128]{1,0:T(8,128)S(1)} %get-tuple-element.32), channel_id=1, source_target_pairs={{0,4},{1,5},{2,6},{3,7},{4,0},{5,1},{6,2},{7,3},{8,12},{9,13},{10,... | collective-permute-start | bytes 49160 | tf_op jit(solution)/shard_map/ppermute | solution.py:309
  91.8 4.9 %collective-permute-start.32 = (f32[32,128]{1,0:T(8,128)S(1)}, f32[32,128]{1,0:T(8,128)S(1)}, u32[]{:S(2)}, u32[]{:S(2)}) collective-permute-start(f32[32,128]{1,0:T(8,128)S(1)} %get-tuple-element.32), channel_id=1, source_target_pairs={{0,5},{1,4},{2,7},{3,6},{4,1},{5,0},{6,3},{7,2},{8,13},{9,12},{10,... | collective-permute-start | bytes 49160 | tf_op jit(solution)/shard_map/ppermute | solution.py:377
  91.8 4.8 %collective-permute-start.33 = (f32[32,128]{1,0:T(8,128)S(1)}, f32[32,128]{1,0:T(8,128)S(1)}, u32[]{:S(2)}, u32[]{:S(2)}) collective-permute-start(f32[32,128]{1,0:T(8,128)S(1)} %get-tuple-element.32), channel_id=1, source_target_pairs={{0,1},{1,0},{2,3},{3,2},{4,5},{5,4},{6,7},{7,6},{8,9},{9,8},{10,11... | collective-permute-start | bytes 49160 | tf_op jit(solution)/shard_map/ppermute | solution.py:303
  94.8 2.0 %collective-permute-start.31 = (bf16[2,2,4,32,128]{4,3,2,1,0:T(8,128)(2,1)S(1)}, bf16[2,2,4,32,128]{4,3,2,1,0:T(8,128)(2,1)S(1)}, u32[]{:S(2)}, u32[]{:S(2)}) collective-permute-start(bf16[2,2,4,32,128]{4,3,2,1,0:T(8,128)(2,1)S(1)} %get-tuple-element.33), channel_id=1, source_target_pairs={{0,1},{1,0},{2,3},{3,2},{4,5},{5,4},{6,7},{7,6},{8,9},{9,8},{10,11... | collective-permute-start | bytes 393224 | tf_op jit(solution)/shard_map/ppermute | solution.py:303
  96.9 5.7 %collective-permute-start.36 = (bf16[2,4,32,128]{3,2,1,0:T(8,128)(2,1)S(1)}, bf16[2,4,32,128]{3,2,1,0:T(8,128)(2,1)S(1)}, u32[]{:S(2)}, u32[]{:S(2)}) collective-permute-start(bf16[2,4,32,128]{3,2,1,0:T(8,128)(2,1)S(1)} %pad_maximum_fusion.4), channel_id=1, source_target_pairs={{0,10},{1,11},{2,8},{3,9},{4,14},{5,15},{6,12},{7,13},{8,2},{9,3},... | collective-permute-start | bytes 196616 | tf_op jit(solution)/shard_map/ppermute | solution.py:303
  100.3 4.3 %collective-permute-start.35 = (bf16[2,4,32,128]{3,2,1,0:T(8,128)(2,1)S(1)}, bf16[2,4,32,128]{3,2,1,0:T(8,128)(2,1)S(1)}, u32[]{:S(2)}, u32[]{:S(2)}) collective-permute-start(bf16[2,4,32,128]{3,2,1,0:T(8,128)(2,1)S(1)} %pad_maximum_fusion.3), channel_id=1, source_target_pairs={{0,8},{1,9},{2,10},{3,11},{4,12},{5,13},{6,14},{7,15},{8,0},{9,1},... | collective-permute-start | bytes 196616 | tf_op jit(solution)/shard_map/ppermute | solution.py:303
  101.4 4.3 %collective-permute-start.34 = (bf16[2,4,32,128]{3,2,1,0:T(8,128)(2,1)S(1)}, bf16[2,4,32,128]{3,2,1,0:T(8,128)(2,1)S(1)}, u32[]{:S(2)}, u32[]{:S(2)}) collective-permute-start(bf16[2,4,32,128]{3,2,1,0:T(8,128)(2,1)S(1)} %pad_maximum_fusion.2), channel_id=1, source_target_pairs={{0,2},{1,3},{2,0},{3,1},{4,6},{5,7},{6,4},{7,5},{8,10},{9,11},{10,... | collective-permute-start | bytes 196616 | tf_op jit(solution)/shard_map/ppermute | solution.py:303
